TPU v7x, 256 devices: a whole 4x4x8 slice. The times are simulated.
256 devices in a mesh: seq: 16 (over y, x), exp: 16 (over z, core).
Axes of the slice: x: 4, y: 4, z: 8, core: 2. Of those that a mesh axis runs over, the one named last changes fastest.
Arguments:
- x_in: bfloat16 [4096, 8192], P('seq', 'exp'), may hold values from -6 to 6
- z_gate: bfloat16 [4096, 8192], P('seq', 'exp'), may hold values from -6 to 6
- b_in: bfloat16 [4096, 128], P('seq'), may hold values from -0.52734375 to 0.52734375
- c_out: bfloat16 [4096, 128], P('seq'), may hold values from -0.1875 to 0.1875
- dt_step: float32 [4096, 128], P('seq', 'exp'), may hold values from 0.12 to 2052, as said below
- rate: float32 [128], P('exp'), may hold values from 0 to 0.06, as said below
- skip: float32 [128], P('exp'), may hold values from 0.5 to 1.5
- init_state: float32 [128, 64, 128], P('exp'), may hold values from -16.970562 to 16.970562
- residual: bfloat16 [4096, 8192], P(('seq', 'exp')), may hold values from -6 to 6
- norm_gain: float32 [8192], replicated, may hold values from 0.5 to 1.5
- expert_ids: int32 [4096, 2], P(('seq', 'exp')), may hold values from 0 to 15, all different within a row; in each aligned block of 16 rows (0 to 15, 16 to 31, ...) at most 3 rows name the same one
- gate_weights: float32 [4096, 2], P(('seq', 'exp')), may hold values from 0.2 to 1
- w_gate: bfloat16 [16, 8192, 2048], P('exp', None, 'seq'), may hold values from -0.0625 to 0.0625
- w_up: bfloat16 [16, 8192, 2048], P('exp', None, 'seq'), may hold values from -0.0625 to 0.0625
- w_down: bfloat16 [16, 2048, 8192], P('exp', 'seq'), may hold values from -0.125 to 0.125
Outputs:
- layer_out: bfloat16 [4096, 8192], P(('seq', 'exp'))
Inputs may be any that keep to these rules, and one draw needn't show every extreme that they name: `dt_step`: positive step sizes. `rate`: positive rates. `expert_ids`: each row names two different experts; among the rows of one device (aligned blocks of 16 rows) no expert is named by more than 3 rows, and in every draw some expert is named by exactly 3 rows of some block.
All inputs are finite; a program needn't handle non-finite values.
Results may differ from a plain program's by a relative error of at most 0.0095.
Values may be sent and summed in bfloat16 or wider, within the bound.
A program may use at most 128 MiB of HBM per device.

v0:
```python
import jax
import jax.numpy as jnp
from jax import lax
from jax.sharding import PartitionSpec as P

GROUP = 128


PRECISE = lax.Precision.HIGHEST


def entering_2(array, axis, combine, identity):
    devices, mine = (lax.axis_size(axis), lax.axis_index(axis))
    everything = jax.tree.map(
        lambda part, kind: lax.all_gather(part.astype(kind), axis),
        array,
        (jnp.bfloat16, jnp.bfloat16),
    )
    start = jax.tree.map(
        lambda part, zero: jnp.broadcast_to(jnp.asarray(zero, part.dtype), part.shape),
        array,
        identity,
    )

    def hop(k, before):
        reached = k < mine
        new = combine(
            before, jax.tree.map(lambda part, own: part[k].astype(own.dtype), everything, array)
        )
        return jax.tree.map(lambda a, b: jnp.where(reached, a, b), new, before)

    return lax.fori_loop(0, devices, hop, start)


def chain_combine(earlier, later):
    return (earlier[0] + later[0], jnp.exp(later[0])[:, None, None] * earlier[1] + later[1])


def on_device(
    x_in,
    z_gate,
    b_in,
    c_out,
    dt_step,
    rate,
    skip,
    init_state,
    residual,
    norm_gain,
    expert_ids,
    gate_weights,
    w_gate,
    w_up,
    w_down,
):
    token_count, channels = x_in.shape
    heads_here = rate.shape[0]
    head_width = channels // heads_here
    state_width = b_in.shape[1]
    blocks = token_count // GROUP
    inputs = x_in.astype(jnp.float32).reshape(blocks, GROUP, heads_here, head_width)
    keys_in = b_in.astype(jnp.float32).reshape(blocks, GROUP, state_width)
    queries = c_out.astype(jnp.float32).reshape(blocks, GROUP, state_width)
    log_steps = (-rate[None, :] * dt_step).reshape(blocks, GROUP, heads_here)
    cumulative = jnp.cumsum(log_steps, axis=1)
    scores = jnp.einsum("ctn,csn->cts", queries, keys_in, precision=PRECISE)
    causal = jnp.arange(GROUP)[:, None] >= jnp.arange(GROUP)[None, :]
    spread = cumulative[:, :, None, :] - cumulative[:, None, :, :]
    weights = jnp.exp(jnp.where(causal[None, :, :, None], spread, -jnp.inf)) * scores[..., None]
    intra_out = jnp.einsum("ctsh,cshp->cthp", weights, inputs, precision=PRECISE)
    tail_decay = jnp.exp(cumulative[:, -1:, :] - cumulative)
    block_state = jnp.einsum("csh,cshp,csn->chpn", tail_decay, inputs, keys_in, precision=PRECISE)
    block_log = cumulative[:, -1, :]

    def advance(carried, element):
        total_log, total_state = carried
        step_log, step_state = element
        updated = (
            total_log + step_log,
            jnp.exp(step_log)[:, None, None] * total_state + step_state,
        )
        return (updated, (total_log, total_state))

    zero_state = jnp.zeros((heads_here, head_width, state_width), jnp.float32)
    zero_log = jnp.zeros((heads_here,), jnp.float32)
    (device_log, device_state), (enter_log, enter_state) = lax.scan(
        advance, (zero_log, zero_state), (block_log, block_state)
    )
    prior_log, prior_state = entering_2(
        (device_log, device_state), "seq", chain_combine, (zero_log, zero_state)
    )
    incoming = prior_state + jnp.exp(prior_log)[:, None, None] * init_state
    entering = enter_state + jnp.exp(enter_log)[:, :, None, None] * incoming[None]
    inter_out = jnp.exp(cumulative)[..., None] * jnp.einsum(
        "chpn,ctn->cthp", entering, queries, precision=PRECISE
    )
    mixed_out = (intra_out + inter_out + skip[None, None, :, None] * inputs).reshape(
        token_count, channels
    )
    mixer = (mixed_out * jax.nn.silu(z_gate.astype(jnp.float32))).astype(jnp.bfloat16)
    token_mix = lax.all_to_all(mixer, "exp", split_axis=0, concat_axis=1, tiled=True)
    stream = (residual.astype(jnp.float32) + token_mix.astype(jnp.float32)).astype(jnp.bfloat16)
    widened = stream.astype(jnp.float32)
    normed = (
        widened
        * lax.rsqrt(jnp.mean(widened * widened, axis=-1, keepdims=True) + 1e-06)
        * norm_gain[None, :]
    ).astype(jnp.bfloat16)
    rows_here = residual.shape[0]
    owners = lax.axis_size("exp")
    local_experts = w_gate.shape[0]
    experts = owners * local_experts
    capacity = max(2, 2 * rows_here // experts + 1)
    width = residual.shape[1]
    chosen = expert_ids.reshape(-1)
    onehot = (chosen[:, None] == jnp.arange(experts)[None, :]).astype(jnp.int32)
    slot_index = jnp.sum((jnp.cumsum(onehot, axis=0) - onehot) * onehot, axis=1)
    target = chosen * capacity + slot_index
    placing = (target[None, :] == jnp.arange(experts * capacity)[:, None]).astype(jnp.bfloat16)
    pair_rows = jnp.repeat(normed, 2, axis=0)
    outgoing = jnp.dot(placing, pair_rows, preferred_element_type=jnp.float32).astype(jnp.bfloat16)
    outgoing = outgoing.reshape(owners, local_experts, 1, capacity, width)
    arrived = lax.all_to_all(outgoing, "exp", split_axis=0, concat_axis=2, tiled=True)
    segment = lax.all_gather(arrived, "seq", axis=1, tiled=True)
    flattened = segment.reshape(segment.shape[0], -1, segment.shape[-1])
    gate_proj = jnp.einsum("erd,edf->erf", flattened, w_gate, preferred_element_type=jnp.float32)
    up_proj = jnp.einsum("erd,edf->erf", flattened, w_up, preferred_element_type=jnp.float32)
    active = (jax.nn.silu(gate_proj) * up_proj).astype(jnp.bfloat16)
    partial_value = jnp.einsum("erf,efd->erd", active, w_down, preferred_element_type=jnp.float32)
    partials = partial_value.reshape(segment.shape[:-1] + (partial_value.shape[-1],))
    summed = lax.psum_scatter(partials.astype(jnp.bfloat16), "seq", scatter_dimension=1, tiled=True)
    returned = lax.all_to_all(summed, "exp", split_axis=2, concat_axis=0, tiled=True)
    results = returned.reshape(experts * capacity, width)
    picked = results[target].astype(jnp.float32).reshape(rows_here, 2, width)
    mixture = jnp.sum(picked * gate_weights[:, :, None], axis=1)
    return (widened + mixture).astype(jnp.bfloat16)


def solution(mesh):
    return jax.shard_map(
        on_device,
        mesh=mesh,
        in_specs=(
            P("seq", "exp"),
            P("seq", "exp"),
            P("seq", None),
            P("seq", None),
            P("seq", "exp"),
            P("exp"),
            P("exp"),
            P("exp", None, None),
            P(("seq", "exp"), None),
            P(),
            P(("seq", "exp"), None),
            P(("seq", "exp"), None),
            P("exp", None, "seq"),
            P("exp", None, "seq"),
            P("exp", "seq", None),
        ),
        out_specs=P(("seq", "exp"), None),
        check_vma=False,
    )
```

profile of v0, /device:TPU:1, one launch (start us, length us, event | category | flops | bytes accessed | tf_op | source)
XLA Modules:
  0.0 454.0 jit_solution(192723632810441709)
XLA Ops:
  8.6 1.3 reshape.209
  10.6 4.3 while.33
  11.5 1.3 dynamic_update_slice.14
  13.6 1.3 dynamic_update_slice.14
  16.3 1.3 dynamic-slice
  18.5 34.4 %all-reduce = bf16[128]{0:T(256)(128)(2,1)S(1)} all-reduce(bf16[128]{0:T(256)(128)(2,1)S(1)} %dynamic-update-slice), channel_id=2, replica_groups=mesh['seq'=16,'exp'=16] {'seq'}, use_global_device_ids=true, to_apply=%add | all-reduce | flops 128 | bytes 512
  53.7 1.1 copy.84
  55.2 13.5 %all-gather.6.cloned.1.call-done = bf16[128,64,128]{2,1,0:T(8,128)(2,1)} async-done(((bf16[8,64,128]{2,1,0:T(8,128)(2,1)}), bf16[128,64,128]{2,1,0:T(8,128)(2,1)}) %all-gather.6.cloned.1.call-update) | async-done | bytes 2097168 | tf_op jit(solution)/shard_map/all_gather | solution.py:15
  68.7 17.0 %while.34 = (s32[]{:T(128)}, f32[8]{0:T(128)S(1)}, f32[8,64,128]{2,1,0:T(8,128)S(1)}, s32[]{:T(128)}, bf16[16,8]{1,0:T(8,128)(2,1)S(1)}, /*index=5*/bf16[16,8,64,128]{3,2,1,0:T(8,128)(2,1)}, s32[]{:T(128)}, s32[]{:T(128)}) while((s32[]{:T(128)}, f32[8]{0:T(128)S(1)}, f32[8,64,128]{2,1,0:T(8,128)S(1)}, s32[]{:T(128)}, ...), condition=%wide.region_4.5_spmd.clone, body=%wide.region_3.4_spmd.clone.sunk | while | flops 327716 | bytes 655619 | solution.py:32
  85.7 1.0 multiply_add_fusion
  86.7 1.5 fusion.13
  88.2 1.3 fusion.12
  91.0 8.5 %all-to-all-start = ((bf16[16,16,512]{2,1,0:T(8,128)(2,1)}), bf16[16,16,512]{2,1,0:T(8,128)(2,1)S(1)}, u32[]{:S(2)}, u32[]{:S(2)}) async-start(bf16[16,16,512]{2,1,0:T(8,128)(2,1)} %bitcast.12), calls=%async_computation | async-start | bytes 524288 | tf_op jit(solution)/shard_map/all_to_all | solution.py:101
  99.9 11.3 %all-to-all-done = bf16[16,16,512]{2,1,0:T(8,128)(2,1)S(1)} async-done(((bf16[16,16,512]{2,1,0:T(8,128)(2,1)}), bf16[16,16,512]{2,1,0:T(8,128)(2,1)S(1)}, u32[]{:S(2)}, u32[]{:S(2)}) %all-to-all-start) | async-done | bytes 262176 | tf_op jit(solution)/shard_map/all_to_all | solution.py:101
  112.4 1.2 convolution_convert_fusion.1
  113.6 1.5 reshape.174
  115.1 31.2 %all_to_all.34 = bf16[16,1,1,3,8192]{4,3,2,1,0:T(4,128)(2,1)S(1)} all-to-all(bf16[16,1,1,3,8192]{4,3,2,1,0:T(4,128)(2,1)S(1)} %bitcast.114), channel_id=1, replica_groups=mesh['seq'=16,'exp'=16] {'exp'}, dimensions={0} | all-to-all | bytes 1572864 | tf_op jit(solution)/shard_map/all_to_all | solution.py:123
  146.3 1.5 copy.89
  148.0 89.6 %all-gather.8.cloned.1.call-done = bf16[256,1,1,3,8192]{4,0,3,2,1:T(8,128)(2,1)} async-done(((bf16[16,1,1,3,8192]{4,0,3,2,1:T(8,128)(2,1)}), bf16[256,1,1,3,8192]{4,0,3,2,1:T(8,128)(2,1)}) %all-gather.8.cloned.1.call-update) | async-done | bytes 12582928 | tf_op jit(solution)/shard_map/all_gather | solution.py:124
  237.6 18.8 %copy.90 = bf16[256,1,1,3,8192]{4,3,0,2,1:T(4,128)(2,1)} copy(bf16[256,1,1,3,8192]{4,0,3,2,1:T(8,128)(2,1)} %all-gather.8.cloned.1.call-done) | data formatting | bytes 25165824 | tf_op jit(solution)/shard_map/all_gather | solution.py:124
  256.4 26.2 %reshape.175 = bf16[768,8192]{1,0:T(8,128)(2,1)} reshape(bf16[256,1,1,3,8192]{4,3,0,2,1:T(4,128)(2,1)} %copy.90) | data formatting | bytes 25165824 | tf_op jit(solution)/shard_map/reshape.2
  282.7 7.7 %fusion.9 = f32[768,128]{1,0:T(8,128)S(1)} fusion(bf16[768,8192]{1,0:T(8,128)(2,1)} %reshape.175, bf16[1,8192,128]{2,1,0:T(8,128)(2,1)} %param.31), kind=kOutput, calls=%fused_computation.21 | convolution fusion | flops 1610612736 | bytes 15073280 | tf_op jit(solution)/shard_map/erd,edf->erf/dot_general | solution.py:126
  292.0 3.4 fusion.17
  295.6 6.4 %fusion.5 = bf16[1,16,16,3,8192]{4,2,3,1,0:T(8,128)(2,1)} fusion(bf16[1,128,8192]{2,1,0:T(8,128)(2,1)S(1)} %copy-done, bf16[16,16,3,128]{3,2,1,0:T(4,128)(2,1)S(1)} %dot_general.46), kind=kOutput, calls=%fused_computation.16 | convolution fusion | flops 1616904192 | bytes 14876672 | tf_op jit(solution)/shard_map/erf,efd->erd/dot_general | solution.py:129
  302.0 99.5 %reduce-scatter.7.cloned.1.call-done = bf16[1,1,16,3,8192]{4,2,3,1,0:T(8,128)(2,1)} async-done(((bf16[1,16,16,3,8192]{4,2,3,1,0:T(8,128)(2,1)}), bf16[1,1,16,3,8192]{4,2,3,1,0:T(8,128)(2,1)}) %reduce-scatter.7.cloned.1.call-update) | async-done | bytes 786448
  401.5 2.8 copy.92
  404.2 7.9 %all-to-all-start.2 = ((bf16[1,1,16,3,8192]{4,3,1,0,2:T(4,128)(2,1)}), bf16[1,1,16,3,8192]{4,3,1,0,2:T(4,128)(2,1)}, u32[]{:S(2)}, u32[]{:S(2)}) async-start(bf16[1,1,16,3,8192]{4,3,1,0,2:T(4,128)(2,1)} %copy.92), calls=%async_computation.2 | async-start | bytes 2097152 | tf_op jit(solution)/shard_map/all_to_all | solution.py:132
  412.4 27.8 %all-to-all-done.2 = bf16[1,1,16,3,8192]{4,3,1,0,2:T(4,128)(2,1)} async-done(((bf16[1,1,16,3,8192]{4,3,1,0,2:T(4,128)(2,1)}), bf16[1,1,16,3,8192]{4,3,1,0,2:T(4,128)(2,1)}, u32[]{:S(2)}, u32[]{:S(2)}) %all-to-all-start.2) | async-done | bytes 786464 | tf_op jit(solution)/shard_map/all_to_all | solution.py:132
  440.2 1.7 reshape.179
  441.9 1.7 gather_fusion
  443.6 1.7 reshape.183
  445.3 1.4 multiply_reduce_fusion
  (116 shorter events, 29.6 us)
Async XLA Ops:
  6.5 289.0 %copy-start = (bf16[1,128,8192]{2,1,0:T(8,128)(2,1)S(1)}, bf16[1,128,8192]{2,1,0:T(8,128)(2,1)}, u32[]{:S(2)}) copy-start(bf16[1,128,8192]{2,1,0:T(8,128)(2,1)} %param.33) | copy-start | bytes 6291460
  6.5 3.7 copy-start.4
  6.5 62.1 %all-gather.6.cloned.1.call-start = ((), (), s32[]{:S(2)}) async-start(), calls=%async_computation.4 | async-start | bytes 2228224 | tf_op jit(solution)/shard_map/all_gather | solution.py:15
  10.6 44.2 %copy-start.7 = (s32[16,2]{0,1:T(2,128)S(1)}, s32[16,2]{0,1:T(2,128)}, u32[]{:S(2)}) copy-start(s32[16,2]{0,1:T(2,128)} %param.29) | copy-start | bytes 388
  10.6 44.4 %copy-start.2 = (bf16[256,128]{1,0:T(8,128)(2,1)S(1)}, bf16[256,128]{1,0:T(8,128)(2,1)}, u32[]{:S(2)}) copy-start(bf16[256,128]{1,0:T(8,128)(2,1)} %param.22) | copy-start | bytes 196612
  68.7 19.5 %copy-start.6 = (f32[2,128,8]{1,2,0:T(8,128)S(1)}, f32[2,128,8]{1,2,0:T(8,128)}, u32[]{:S(2)}) copy-start(f32[2,128,8]{1,2,0:T(8,128)} %copy.76) | copy-start | bytes 24580
  68.7 19.5 %copy-start.10 = (f32[8]{0:T(128)S(1)}, f32[8]{0:T(128)}, u32[]{:S(2)}) copy-start(f32[8]{0:T(128)} %param.25) | copy-start | bytes 100
  90.0 21.4 %copy-start.3 = (bf16[16,8192]{1,0:T(8,128)(2,1)S(1)}, bf16[16,8192]{1,0:T(8,128)(2,1)}, u32[]{:S(2)}) copy-start(bf16[16,8192]{1,0:T(8,128)(2,1)} %param.27) | copy-start | bytes 786436
  90.2 21.4 %copy-start.5 = (f32[8192]{0:T(1024)S(1)}, f32[8192]{0:T(1024)}, u32[]{:S(2)}) copy-start(f32[8192]{0:T(1024)} %param.28) | copy-start | bytes 98308
  91.0 20.2 %all-to-all-start = ((bf16[16,16,512]{2,1,0:T(8,128)(2,1)}), bf16[16,16,512]{2,1,0:T(8,128)(2,1)S(1)}, u32[]{:S(2)}, u32[]{:S(2)}) async-start(bf16[16,16,512]{2,1,0:T(8,128)(2,1)} %bitcast.12), calls=%async_computation | async-start | bytes 524288 | tf_op jit(solution)/shard_map/all_to_all | solution.py:101
  99.6 138.0 %all-gather.8.cloned.1.call-start = ((), (), s32[]{:S(2)}) async-start(), calls=%async_computation.5 | async-start | bytes 13369344 | tf_op jit(solution)/shard_map/all_gather | solution.py:124
  147.8 253.7 %reduce-scatter.7.cloned.1.call-start = ((), (), s32[]{:S(2)}) async-start(), calls=%async_computation.6 | async-start | bytes 13369344
  282.7 8.8 %copy-start.1 = (bf16[768,8192]{1,0:T(8,128)(2,1)S(1)}, bf16[768,8192]{1,0:T(8,128)(2,1)}, u32[]{:S(2)}) copy-start(bf16[768,8192]{1,0:T(8,128)(2,1)} %reshape.175) | copy-start | bytes 37748740
  282.7 9.4 %copy-start.9 = (bf16[1,8192,128]{2,1,0:T(8,128)(2,1)S(1)}, bf16[1,8192,128]{2,1,0:T(8,128)(2,1)}, u32[]{:S(2)}) copy-start(bf16[1,8192,128]{2,1,0:T(8,128)(2,1)} %param.32) | copy-start | bytes 6291460
  302.0 110.4 %copy-start.8 = (f32[16,2]{0,1:T(2,128)S(1)}, f32[16,2]{0,1:T(2,128)}, u32[]{:S(2)}) copy-start(f32[16,2]{0,1:T(2,128)} %param.30) | copy-start | bytes 388
  404.2 35.9 %all-to-all-start.2 = ((bf16[1,1,16,3,8192]{4,3,1,0,2:T(4,128)(2,1)}), bf16[1,1,16,3,8192]{4,3,1,0,2:T(4,128)(2,1)}, u32[]{:S(2)}, u32[]{:S(2)}) async-start(bf16[1,1,16,3,8192]{4,3,1,0,2:T(4,128)(2,1)} %copy.92), calls=%async_computation.2 | async-start | bytes 2097152 | tf_op jit(solution)/shard_map/all_to_all | solution.py:132
Sparse Core Ops, SparseCore 0:
  15.7 52.9 all-gather.5
  147.9 89.6 all-gather.7
  302.1 99.3 reduce-scatter.6
where the time goes:
time: 456 us; the launch traced here: 454 us
  waiting for transfers between devices  242 us (53%)
  local copies, waits for them, and re-layouts  68.5 us (15%)
  blocking collectives  65.6 us (14%)
  other arithmetic  24.9 us (5%)
  matrix products  22.1 us (5%)
  starting transfers between devices  16.7 us (4%)
  between operations  14.1 us (3%)
    unnamed x4, waiting for transfers between devices  99.5 us
    all_gather x1, waiting for transfers between devices, on_device(): segment = lax.all_gather(arrived, 'seq', axis=1, tiled=True)  89.6 us
    unnamed x1, blocking collectives  34.4 us
    all_to_all x1, blocking collectives, on_device(): lax.all_to_all(outgoing, 'exp', split_axis=0, concat_axis=2, tiled=True)  31.2 us
    all_to_all x1, waiting for transfers between devices, on_device(): lax.all_to_all(summed, 'exp', split_axis=2, concat_axis=0, tiled=True)  27.8 us
    another operation x1, local copies, waits for them, and re-layouts  26.2 us
    all_gather x1, local copies, waits for them, and re-layouts, on_device(): segment = lax.all_gather(arrived, 'seq', axis=1, tiled=True)  18.8 us
    select_n x16, other arithmetic, hop(): return jax.tree.map(lambda a, b: jnp.where(reached, a, b), new, before)  16.2 us
  transfers between devices with their start and end apart: 5, of which 5 were waited for; matrix products, arithmetic and copies ran while one was open for 1% of the time, Pallas kernels for 0%

commit v1 on v0

--- a/solution.py
+++ b/solution.py
@@ -9,27 +9,18 @@
 PRECISE = lax.Precision.HIGHEST
 
 
-def entering_2(array, axis, combine, identity):
-    devices, mine = (lax.axis_size(axis), lax.axis_index(axis))
-    everything = jax.tree.map(
-        lambda part, kind: lax.all_gather(part.astype(kind), axis),
-        array,
-        (jnp.bfloat16, jnp.bfloat16),
-    )
-    start = jax.tree.map(
-        lambda part, zero: jnp.broadcast_to(jnp.asarray(zero, part.dtype), part.shape),
-        array,
-        identity,
-    )
-
-    def hop(k, before):
-        reached = k < mine
-        new = combine(
-            before, jax.tree.map(lambda part, own: part[k].astype(own.dtype), everything, array)
-        )
-        return jax.tree.map(lambda a, b: jnp.where(reached, a, b), new, before)
-
-    return lax.fori_loop(0, devices, hop, start)
+def exclusive_scan(log, state, axis):
+    devices = lax.axis_size(axis)
+    inc = (log, state)
+    exc = (jnp.zeros_like(log), jnp.zeros_like(state))
+    shift = 1
+    while shift < devices:
+        pairs = [(i, i + shift) for i in range(devices - shift)]
+        got = (lax.ppermute(inc[0], axis, pairs), lax.ppermute(inc[1], axis, pairs))
+        exc = chain_combine(got, exc)
+        inc = chain_combine(got, inc)
+        shift *= 2
+    return exc
 
 
 def chain_combine(earlier, later):
@@ -86,9 +77,7 @@
     (device_log, device_state), (enter_log, enter_state) = lax.scan(
         advance, (zero_log, zero_state), (block_log, block_state)
     )
-    prior_log, prior_state = entering_2(
-        (device_log, device_state), "seq", chain_combine, (zero_log, zero_state)
-    )
+    prior_log, prior_state = exclusive_scan(device_log, device_state, "seq")
     incoming = prior_state + jnp.exp(prior_log)[:, None, None] * init_state
     entering = enter_state + jnp.exp(enter_log)[:, :, None, None] * incoming[None]
     inter_out = jnp.exp(cumulative)[..., None] * jnp.einsum(
@@ -115,21 +104,21 @@
     chosen = expert_ids.reshape(-1)
     onehot = (chosen[:, None] == jnp.arange(experts)[None, :]).astype(jnp.int32)
     slot_index = jnp.sum((jnp.cumsum(onehot, axis=0) - onehot) * onehot, axis=1)
-    target = chosen * capacity + slot_index
+    target = slot_index * experts + chosen
     placing = (target[None, :] == jnp.arange(experts * capacity)[:, None]).astype(jnp.bfloat16)
     pair_rows = jnp.repeat(normed, 2, axis=0)
     outgoing = jnp.dot(placing, pair_rows, preferred_element_type=jnp.float32).astype(jnp.bfloat16)
-    outgoing = outgoing.reshape(owners, local_experts, 1, capacity, width)
-    arrived = lax.all_to_all(outgoing, "exp", split_axis=0, concat_axis=2, tiled=True)
-    segment = lax.all_gather(arrived, "seq", axis=1, tiled=True)
-    flattened = segment.reshape(segment.shape[0], -1, segment.shape[-1])
-    gate_proj = jnp.einsum("erd,edf->erf", flattened, w_gate, preferred_element_type=jnp.float32)
-    up_proj = jnp.einsum("erd,edf->erf", flattened, w_up, preferred_element_type=jnp.float32)
+    outgoing = outgoing.reshape(capacity, experts, width)
+    arrived = lax.all_to_all(outgoing, "exp", split_axis=1, concat_axis=1, tiled=True)
+    arrived = arrived.reshape(capacity * experts, width)
+    segment = lax.all_gather(arrived, "seq", axis=0, tiled=True)
+    gate_proj = jnp.dot(segment, w_gate[0], preferred_element_type=jnp.float32)
+    up_proj = jnp.dot(segment, w_up[0], preferred_element_type=jnp.float32)
     active = (jax.nn.silu(gate_proj) * up_proj).astype(jnp.bfloat16)
-    partial_value = jnp.einsum("erf,efd->erd", active, w_down, preferred_element_type=jnp.float32)
-    partials = partial_value.reshape(segment.shape[:-1] + (partial_value.shape[-1],))
-    summed = lax.psum_scatter(partials.astype(jnp.bfloat16), "seq", scatter_dimension=1, tiled=True)
-    returned = lax.all_to_all(summed, "exp", split_axis=2, concat_axis=0, tiled=True)
+    partial_value = jnp.dot(active, w_down[0], preferred_element_type=jnp.float32)
+    summed = lax.psum_scatter(partial_value.astype(jnp.bfloat16), "seq", scatter_dimension=0, tiled=True)
+    summed = summed.reshape(capacity, experts, width)
+    returned = lax.all_to_all(summed, "exp", split_axis=1, concat_axis=1, tiled=True)
     results = returned.reshape(experts * capacity, width)
     picked = results[target].astype(jnp.float32).reshape(rows_here, 2, width)
     mixture = jnp.sum(picked * gate_weights[:, :, None], axis=1)

time: 456 us -> 401 us (0.88)
  local copies, waits for them, and re-layouts: 68.5 us -> 18 us
  starting transfers between devices: 16.7 us -> 58.2 us
  blocking collectives: 65.6 us -> 31.2 us
  other arithmetic: 24.9 us -> 11.2 us
  matrix products: 22.1 us -> 31.7 us
  waiting for transfers between devices: 242 us -> 236 us
    unnamed x4 -> x2, waiting for transfers between devices: 99.5 us -> 0.03 us
    reduce_scatter x0 -> x1, waiting for transfers between devices: none -> 99.2 us  [on_device(): lax.psum_scatter(partial_value.astype(jnp.bfloat16), 'seq', scatter_dimen...]
    ppermute x0 -> x8, starting transfers between devices: none -> 36.2 us  [exclusive_scan(): got = (lax.ppermute(inc[0], axis, pairs), lax.ppermute(inc[1], axis, pairs))]
    unnamed x1 -> x0, blocking collectives: 34.4 us -> none
    another operation x1 -> x0, local copies, waits for them, and re-layouts: 26.2 us -> none
    all_gather x2 -> x0, local copies, waits for them, and re-layouts: 18.9 us -> none  [the longest x1 18.8 us: on_device(): segment = lax.all_gather(arrived, 'seq', axis=1, tiled=True)]
    select_n x16 -> x0, other arithmetic: 16.2 us -> none  [hop(): return jax.tree.map(lambda a, b: jnp.where(reached, a, b), new, before)]
    all_gather x2 -> x1, waiting for transfers between devices: 103 us -> 89.8 us  [on_device(): segment = lax.all_gather(arrived, 'seq', axis=0, tiled=True)]
  transfers between devices with their start and end apart: 5 -> 12, of which waited for: 5 -> 9; matrix products, arithmetic and copies ran while one was open for 1% -> 2% of each run, Pallas kernels for 0% -> 0%
where the time goes in v1:
time: 401 us; the launch traced here: 400 us
  waiting for transfers between devices  236 us (59%)
  starting transfers between devices  58.2 us (15%)
  matrix products  31.7 us (8%)
  blocking collectives  31.2 us (8%)
  local copies, waits for them, and re-layouts  18 us (4%)
  between operations  13.8 us (3%)
  other arithmetic  11.2 us (3%)
    reduce_scatter x1, waiting for transfers between devices, on_device(): lax.psum_scatter(partial_value.astype(jnp.bfloat16), 'seq', scatter_dimen...  99.2 us
    all_gather x1, waiting for transfers between devices, on_device(): segment = lax.all_gather(arrived, 'seq', axis=0, tiled=True)  89.8 us
    ppermute x8, starting transfers between devices, exclusive_scan(): got = (lax.ppermute(inc[0], axis, pairs), lax.ppermute(inc[1], axis, pairs))  36.2 us
    all_to_all x1, blocking collectives, on_device(): lax.all_to_all(outgoing, 'exp', split_axis=1, concat_axis=1, tiled=True)  31.2 us
    all_to_all x1, waiting for transfers between devices, on_device(): lax.all_to_all(summed, 'exp', split_axis=1, concat_axis=1, tiled=True)  27.8 us
    dot_general x1, matrix products, on_device(): jnp.dot(active, w_down[0], preferred_element_type=jnp.float32)  19.4 us
    all_to_all x1, starting transfers between devices, on_device(): lax.all_to_all(mixer, 'exp', split_axis=0, concat_axis=1, tiled=True)  13.9 us
    all_to_all x1, waiting for transfers between devices, on_device(): lax.all_to_all(mixer, 'exp', split_axis=0, concat_axis=1, tiled=True)  11.3 us
  transfers between devices with their start and end apart: 12, of which 9 were waited for; matrix products, arithmetic and copies ran while one was open for 2% of the time, Pallas kernels for 0%

profile of v1, /device:TPU:1, one launch (start us, length us, event | category | flops | bytes accessed | tf_op | source)
XLA Modules:
  0.0 400.3 jit_solution(14622680194783239162)
XLA Ops:
  8.6 1.3 reshape.149
  10.6 1.8 while.17
  12.4 4.0 collective-permute-start.3
  16.4 3.1 collective-permute-start
  19.5 1.9 collective-permute-done
  21.5 5.6 %collective-permute-start.4 = (f32[8,64,128]{2,1,0:T(8,128)S(1)}, f32[8,64,128]{2,1,0:T(8,128)S(1)}, u32[]{:S(2)}, u32[]{:S(2)}) collective-permute-start(f32[8,64,128]{2,1,0:T(8,128)S(1)} %multiply_add_fusion.3), channel_id=1, source_target_pairs={{0,32},{16,48},{32,64},{48,80},{64,96},{80,112},{96,128},{112,144}... | collective-permute-start | bytes 786440 | tf_op jit(solution)/shard_map/ppermute | solution.py:19
  27.1 4.0 collective-permute-done.4
  31.1 7.2 %collective-permute-start.5 = (f32[8,64,128]{2,1,0:T(8,128)S(1)}, f32[8,64,128]{2,1,0:T(8,128)S(1)}, u32[]{:S(2)}, u32[]{:S(2)}) collective-permute-start(f32[8,64,128]{2,1,0:T(8,128)S(1)} %multiply_add_fusion.2), channel_id=1, source_target_pairs={{0,64},{16,80},{32,96},{48,112},{64,128},{80,144},{96,160},{112,17... | collective-permute-start | bytes 786440 | tf_op jit(solution)/shard_map/ppermute | solution.py:19
  39.1 1.6 collective-permute-start.1
  42.8 9.5 %collective-permute-start.6 = (f32[8,64,128]{2,1,0:T(8,128)}, f32[8,64,128]{2,1,0:T(8,128)}, u32[]{:S(2)}, u32[]{:S(2)}) collective-permute-start(f32[8,64,128]{2,1,0:T(8,128)} %multiply_add_fusion.1), channel_id=1, source_target_pairs={{0,128},{16,144},{32,160},{48,176},{64,192},{80,208},{96,224},{112... | collective-permute-start | bytes 786440 | tf_op jit(solution)/shard_map/ppermute | solution.py:19
  54.3 1.1 copy.95
  56.9 1.4 collective-permute-start.2
  59.6 3.7 collective-permute-start.7
  64.8 1.2 multiply_add_fusion
  66.0 1.5 fusion.11
  67.5 2.2 fusion.10
  70.3 0.8 copy.96
  71.2 13.9 %all-to-all-start = ((bf16[16,16,512]{2,1,0:T(8,128)(2,1)}), bf16[16,16,512]{2,1,0:T(8,128)(2,1)S(1)}, u32[]{:S(2)}, u32[]{:S(2)}) async-start(bf16[16,16,512]{2,1,0:T(8,128)(2,1)} %bitcast.10), calls=%async_computation | async-start | bytes 524288 | tf_op jit(solution)/shard_map/all_to_all | solution.py:90
  85.4 11.3 %all-to-all-done = bf16[16,16,512]{2,1,0:T(8,128)(2,1)S(1)} async-done(((bf16[16,16,512]{2,1,0:T(8,128)(2,1)}), bf16[16,16,512]{2,1,0:T(8,128)(2,1)S(1)}, u32[]{:S(2)}, u32[]{:S(2)}) %all-to-all-start) | async-done | bytes 262176 | tf_op jit(solution)/shard_map/all_to_all | solution.py:90
  98.9 31.2 %all_to_all.23 = bf16[3,16,8192]{2,0,1:T(4,128)(2,1)S(1)} all-to-all(bf16[3,16,8192]{2,0,1:T(4,128)(2,1)S(1)} %copy.99), channel_id=1, replica_groups=mesh['seq'=16,'exp'=16] {'exp'}, dimensions={1} | all-to-all | bytes 1572864 | tf_op jit(solution)/shard_map/all_to_all | solution.py:112
  130.1 1.5 copy.100
  131.9 89.8 %all-gather.2.cloned.1.call-done = bf16[768,8192]{1,0:T(8,128)(2,1)} async-done(((bf16[48,8192]{1,0:T(8,128)(2,1)}), bf16[768,8192]{1,0:T(8,128)(2,1)}) %all-gather.2.cloned.1.call-update) | async-done | bytes 12582928 | tf_op jit(solution)/shard_map/all_gather | solution.py:114
  221.7 7.0 %fusion.7 = f32[768,128]{1,0:T(8,128)S(1)} fusion(bf16[768,8192]{1,0:T(8,128)(2,1)} %all-gather.2.cloned.1.call-done, bf16[1,8192,128]{2,1,0:T(8,128)(2,1)} %param.29), kind=kOutput, calls=%fused_computation.14 | convolution fusion | flops 1610612736 | bytes 15073280 | tf_op jit(solution)/shard_map/dot_general | solution.py:115
  228.7 19.4 %convolution_convert_fusion = bf16[768,8192]{1,0:T(8,128)(2,1)} fusion(bf16[1,128,8192]{2,1,0:T(8,128)(2,1)S(1)} %copy-done, bf16[768,8192]{1,0:T(8,128)(2,1)} %all-gather.2.cloned.1.call-done, bf16[1,8192,128]{2,1,0:T(8,128)(2,1)} %param.30, f32[768,128]{1,0:T(8,128)S(1)} %fusion.7), kind=kOutput, calls=%fused_computation.9 | convolution fusion | flops 3228106752 | bytes 29753344 | tf_op jit(solution)/shard_map/dot_general | solution.py:118
  248.2 99.2 %reduce-scatter.2.cloned.1.call-done = bf16[48,8192]{1,0:T(8,128)(2,1)} async-done(((bf16[768,8192]{1,0:T(8,128)(2,1)}), bf16[48,8192]{1,0:T(8,128)(2,1)}) %reduce-scatter.2.cloned.1.call-update) | async-done | bytes 786448 | tf_op jit(solution)/shard_map/reduce_scatter | solution.py:119
  347.3 2.8 copy.101
  350.1 7.9 %all-to-all-start.2 = ((bf16[3,16,8192]{2,0,1:T(4,128)(2,1)}), bf16[3,16,8192]{2,0,1:T(4,128)(2,1)}, u32[]{:S(2)}, u32[]{:S(2)}) async-start(bf16[3,16,8192]{2,0,1:T(4,128)(2,1)} %copy.101), calls=%async_computation.3 | async-start | bytes 2097152 | tf_op jit(solution)/shard_map/all_to_all | solution.py:121
  358.2 27.8 %all-to-all-done.2 = bf16[3,16,8192]{2,0,1:T(4,128)(2,1)} async-done(((bf16[3,16,8192]{2,0,1:T(4,128)(2,1)}), bf16[3,16,8192]{2,0,1:T(4,128)(2,1)}, u32[]{:S(2)}, u32[]{:S(2)}) %all-to-all-start.2) | async-done | bytes 786464 | tf_op jit(solution)/shard_map/all_to_all | solution.py:121
  386.1 1.8 copy.102
  387.9 1.7 gather_fusion
  389.6 1.7 reshape.138
  391.3 1.4 multiply_reduce_fusion
  (87 shorter events, 17.9 us)
Async XLA Ops:
  6.5 222.2 %copy-start = (bf16[1,128,8192]{2,1,0:T(8,128)(2,1)S(1)}, bf16[1,128,8192]{2,1,0:T(8,128)(2,1)}, u32[]{:S(2)}) copy-start(bf16[1,128,8192]{2,1,0:T(8,128)(2,1)} %param.31) | copy-start | bytes 6291460
  6.5 3.7 copy-start.3
  10.6 27.7 %copy-start.1 = (bf16[256,128]{1,0:T(8,128)(2,1)S(1)}, bf16[256,128]{1,0:T(8,128)(2,1)}, u32[]{:S(2)}) copy-start(bf16[256,128]{1,0:T(8,128)(2,1)} %param.20) | copy-start | bytes 196612
  12.4 9.0 %collective-permute-start.3 = (f32[8,64,128]{2,1,0:T(8,128)S(1)}, f32[8,64,128]{2,1,0:T(8,128)S(1)}, u32[]{:S(2)}, u32[]{:S(2)}) collective-permute-start(f32[8,64,128]{2,1,0:T(8,128)S(1)} %get-tuple-element.48), channel_id=1, source_target_pairs={{0,16},{16,32},{32,48},{48,64},{64,80},{80,96},{96,112},{112,128},... | collective-permute-start | bytes 786440 | tf_op jit(solution)/shard_map/ppermute | solution.py:19
  16.4 5.0 %collective-permute-start = (f32[8]{0:T(128)S(1)}, f32[8]{0:T(128)S(1)}, u32[]{:S(2)}, u32[]{:S(2)}) collective-permute-start(f32[8]{0:T(128)S(1)} %get-tuple-element.47), channel_id=1, source_target_pairs={{0,16},{16,32},{32,48},{48,64},{64,80},{80,96},{96,112},{112,128},... | collective-permute-start | bytes 104 | tf_op jit(solution)/shard_map/ppermute | solution.py:19
  21.3 33.0 %copy-start.8 = (f32[8]{0:T(128)}, f32[8]{0:T(128)S(1)}, u32[]{:S(2)}) copy-start(f32[8]{0:T(128)S(1)} %collective-permute-done) | copy-start | bytes 100
  21.5 9.6 %collective-permute-start.4 = (f32[8,64,128]{2,1,0:T(8,128)S(1)}, f32[8,64,128]{2,1,0:T(8,128)S(1)}, u32[]{:S(2)}, u32[]{:S(2)}) collective-permute-start(f32[8,64,128]{2,1,0:T(8,128)S(1)} %multiply_add_fusion.3), channel_id=1, source_target_pairs={{0,32},{16,48},{32,64},{48,80},{64,96},{80,112},{96,128},{112,144}... | collective-permute-start | bytes 786440 | tf_op jit(solution)/shard_map/ppermute | solution.py:19
  31.1 10.9 %collective-permute-start.5 = (f32[8,64,128]{2,1,0:T(8,128)S(1)}, f32[8,64,128]{2,1,0:T(8,128)S(1)}, u32[]{:S(2)}, u32[]{:S(2)}) collective-permute-start(f32[8,64,128]{2,1,0:T(8,128)S(1)} %multiply_add_fusion.2), channel_id=1, source_target_pairs={{0,64},{16,80},{32,96},{48,112},{64,128},{80,144},{96,160},{112,17... | collective-permute-start | bytes 786440 | tf_op jit(solution)/shard_map/ppermute | solution.py:19
  39.1 2.4 collective-permute-start.1
  41.5 12.7 %copy-start.9 = (f32[8]{0:T(128)}, f32[8]{0:T(128)S(1)}, u32[]{:S(2)}) copy-start(f32[8]{0:T(128)S(1)} %collective-permute-done.1) | copy-start | bytes 100
  42.8 21.9 %collective-permute-start.6 = (f32[8,64,128]{2,1,0:T(8,128)}, f32[8,64,128]{2,1,0:T(8,128)}, u32[]{:S(2)}, u32[]{:S(2)}) collective-permute-start(f32[8,64,128]{2,1,0:T(8,128)} %multiply_add_fusion.1), channel_id=1, source_target_pairs={{0,128},{16,144},{32,160},{48,176},{64,192},{80,208},{96,224},{112... | collective-permute-start | bytes 786440 | tf_op jit(solution)/shard_map/ppermute | solution.py:19
  56.9 10.6 %copy-start.5 = (pred[128,128]{1,0:T(8,128)(4,1)S(1)}, pred[128,128]{1,0:T(8,128)(4,1)}, u32[]{:S(2)}) copy-start(pred[128,128]{1,0:T(8,128)(4,1)} %iota_compare_fusion) | copy-start | bytes 49156
  56.9 10.6 %copy-start.6 = (f32[2,128,8]{1,2,0:T(8,128)S(1)}, f32[2,128,8]{1,2,0:T(8,128)}, u32[]{:S(2)}) copy-start(f32[2,128,8]{1,2,0:T(8,128)} %copy.87) | copy-start | bytes 24580
  56.9 2.2 collective-permute-start.2
  59.6 4.5 %collective-permute-start.7 = (f32[8]{0:T(128)S(1)}, f32[8]{0:T(128)S(1)}, u32[]{:S(2)}, u32[]{:S(2)}) collective-permute-start(f32[8]{0:T(128)S(1)} %add.120), channel_id=1, source_target_pairs={{0,128},{16,144},{32,160},{48,176},{64,192},{80,208},{96,224},{112... | collective-permute-start | bytes 104 | tf_op jit(solution)/shard_map/ppermute | solution.py:19
  69.7 15.4 %copy-start.7 = (s32[32]{0:T(128)S(1)}, s32[32]{0:T(128)}, u32[]{:S(2)}) copy-start(s32[32]{0:T(128)} %eq.28) | copy-start | bytes 388
  70.1 26.7 %copy-start.2 = (bf16[16,8192]{1,0:T(8,128)(2,1)S(1)}, bf16[16,8192]{1,0:T(8,128)(2,1)}, u32[]{:S(2)}) copy-start(bf16[16,8192]{1,0:T(8,128)(2,1)} %param.25) | copy-start | bytes 786436
  70.3 26.8 %copy-start.4 = (f32[8192]{0:T(1024)S(1)}, f32[8192]{0:T(1024)}, u32[]{:S(2)}) copy-start(f32[8192]{0:T(1024)} %param.26) | copy-start | bytes 98308
  71.2 25.6 %all-to-all-start = ((bf16[16,16,512]{2,1,0:T(8,128)(2,1)}), bf16[16,16,512]{2,1,0:T(8,128)(2,1)S(1)}, u32[]{:S(2)}, u32[]{:S(2)}) async-start(bf16[16,16,512]{2,1,0:T(8,128)(2,1)} %bitcast.10), calls=%async_computation | async-start | bytes 524288 | tf_op jit(solution)/shard_map/all_to_all | solution.py:90
  85.1 136.6 %all-gather.2.cloned.1.call-start = ((), (), s32[]{:S(2)}) async-start(), calls=%async_computation.4 | async-start | bytes 13369344 | tf_op jit(solution)/shard_map/all_gather | solution.py:114
  131.7 215.6 %reduce-scatter.2.cloned.1.call-start = ((), (), s32[]{:S(2)}) async-start(), calls=%async_computation.5 | async-start | bytes 13369344 | tf_op jit(solution)/shard_map/reduce_scatter | solution.py:119
  248.2 110.0 %copy-start.10 = (f32[16,2]{0,1:T(2,128)S(1)}, f32[16,2]{0,1:T(2,128)}, u32[]{:S(2)}) copy-start(f32[16,2]{0,1:T(2,128)} %param.28) | copy-start | bytes 388
  350.1 36.0 %all-to-all-start.2 = ((bf16[3,16,8192]{2,0,1:T(4,128)(2,1)}), bf16[3,16,8192]{2,0,1:T(4,128)(2,1)}, u32[]{:S(2)}, u32[]{:S(2)}) async-start(bf16[3,16,8192]{2,0,1:T(4,128)(2,1)} %copy.101), calls=%async_computation.3 | async-start | bytes 2097152 | tf_op jit(solution)/shard_map/all_to_all | solution.py:121
Sparse Core Ops, SparseCore 0:
  131.8 89.8 all-gather.1
  248.3 99.0 reduce-scatter.1

commit v2 on v1

--- a/solution.py
+++ b/solution.py
@@ -110,14 +110,18 @@
     outgoing = jnp.dot(placing, pair_rows, preferred_element_type=jnp.float32).astype(jnp.bfloat16)
     outgoing = outgoing.reshape(capacity, experts, width)
     arrived = lax.all_to_all(outgoing, "exp", split_axis=1, concat_axis=1, tiled=True)
-    arrived = arrived.reshape(capacity * experts, width)
-    segment = lax.all_gather(arrived, "seq", axis=0, tiled=True)
-    gate_proj = jnp.dot(segment, w_gate[0], preferred_element_type=jnp.float32)
-    up_proj = jnp.dot(segment, w_up[0], preferred_element_type=jnp.float32)
-    active = (jax.nn.silu(gate_proj) * up_proj).astype(jnp.bfloat16)
-    partial_value = jnp.dot(active, w_down[0], preferred_element_type=jnp.float32)
-    summed = lax.psum_scatter(partial_value.astype(jnp.bfloat16), "seq", scatter_dimension=0, tiled=True)
-    summed = summed.reshape(capacity, experts, width)
+    pieces = []
+    for first, last in ((0, 1), (1, capacity)):
+        chunk = arrived[first:last].reshape((last - first) * experts, width)
+        segment = lax.all_gather(chunk, "seq", axis=0, tiled=True)
+        gate_proj = jnp.dot(segment, w_gate[0], preferred_element_type=jnp.float32)
+        up_proj = jnp.dot(segment, w_up[0], preferred_element_type=jnp.float32)
+        active = (jax.nn.silu(gate_proj) * up_proj).astype(jnp.bfloat16)
+        partial_value = jnp.dot(active, w_down[0], preferred_element_type=jnp.float32)
+        pieces.append(
+            lax.psum_scatter(partial_value.astype(jnp.bfloat16), "seq", scatter_dimension=0, tiled=True)
+        )
+    summed = jnp.concatenate(pieces, axis=0).reshape(capacity, experts, width)
     returned = lax.all_to_all(summed, "exp", split_axis=1, concat_axis=1, tiled=True)
     results = returned.reshape(experts * capacity, width)
     picked = results[target].astype(jnp.float32).reshape(rows_here, 2, width)

time: 401 us -> 495 us (1.23)
  waiting for transfers between devices: 236 us -> 327 us
    reduce_scatter x1 -> x2, waiting for transfers between devices: 99.2 us -> 164 us  [on_device(): lax.psum_scatter(partial_value.astype(jnp.bfloat16), 'seq', scatter_dimen...]
    all_gather x1 -> x2, waiting for transfers between devices: 89.8 us -> 116 us  [on_device(): segment = lax.all_gather(chunk, 'seq', axis=0, tiled=True)]
    dot_general x1 -> x2, matrix products: 19.4 us -> 12.8 us  [on_device(): jnp.dot(active, w_down[0], preferred_element_type=jnp.float32)]
    dot_general x1 -> x2, matrix products: 7.01 us -> 10.6 us  [on_device(): gate_proj = jnp.dot(segment, w_gate[0], preferred_element_type=jnp.float32)]
  transfers between devices with their start and end apart: 12 -> 14, of which waited for: 9 -> 11; matrix products, arithmetic and copies ran while one was open for 2% -> 7% of each run, Pallas kernels for 0% -> 0%
where the time goes in v2:
time: 495 us; the launch traced here: 494 us
  waiting for transfers between devices  327 us (66%)
  starting transfers between devices  59.2 us (12%)
  matrix products  31.9 us (6%)
  blocking collectives  31.2 us (6%)
  local copies, waits for them, and re-layouts  18.1 us (4%)
  between operations  13.5 us (3%)
  other arithmetic  13 us (3%)
    reduce_scatter x2, waiting for transfers between devices, on_device(): lax.psum_scatter(partial_value.astype(jnp.bfloat16), 'seq', scatter_dimen...  164 us
    all_gather x2, waiting for transfers between devices, on_device(): segment = lax.all_gather(chunk, 'seq', axis=0, tiled=True)  116 us
    ppermute x8, starting transfers between devices, exclusive_scan(): got = (lax.ppermute(inc[0], axis, pairs), lax.ppermute(inc[1], axis, pairs))  35.6 us
    all_to_all x1, blocking collectives, on_device(): lax.all_to_all(outgoing, 'exp', split_axis=1, concat_axis=1, tiled=True)  31.2 us
    all_to_all x1, waiting for transfers between devices, on_device(): lax.all_to_all(summed, 'exp', split_axis=1, concat_axis=1, tiled=True)  27.8 us
    all_to_all x1, starting transfers between devices, on_device(): lax.all_to_all(mixer, 'exp', split_axis=0, concat_axis=1, tiled=True)  14.3 us
    dot_general x2, matrix products, on_device(): jnp.dot(active, w_down[0], preferred_element_type=jnp.float32)  12.8 us
    all_to_all x1, waiting for transfers between devices, on_device(): lax.all_to_all(mixer, 'exp', split_axis=0, concat_axis=1, tiled=True)  11.3 us
  transfers between devices with their start and end apart: 14, of which 11 were waited for; matrix products, arithmetic and copies ran while one was open for 7% of the time, Pallas kernels for 0%

profile of v2, /device:TPU:1, one launch (start us, length us, event | category | flops | bytes accessed | tf_op | source)
XLA Modules:
  0.0 493.9 jit_solution(8506652656855577056)
XLA Ops:
  11.2 1.8 while.17
  13.0 4.0 collective-permute-start.3
  17.0 3.1 collective-permute-start
  20.1 1.9 collective-permute-done
  22.1 5.6 %collective-permute-start.4 = (f32[8,64,128]{2,1,0:T(8,128)S(1)}, f32[8,64,128]{2,1,0:T(8,128)S(1)}, u32[]{:S(2)}, u32[]{:S(2)}) collective-permute-start(f32[8,64,128]{2,1,0:T(8,128)S(1)} %multiply_add_fusion.3), channel_id=1, source_target_pairs={{0,32},{16,48},{32,64},{48,80},{64,96},{80,112},{96,128},{112,144}... | collective-permute-start | bytes 786440 | tf_op jit(solution)/shard_map/ppermute | solution.py:19
  27.7 3.9 collective-permute-done.4
  31.7 7.2 %collective-permute-start.5 = (f32[8,64,128]{2,1,0:T(8,128)S(1)}, f32[8,64,128]{2,1,0:T(8,128)S(1)}, u32[]{:S(2)}, u32[]{:S(2)}) collective-permute-start(f32[8,64,128]{2,1,0:T(8,128)S(1)} %multiply_add_fusion.2), channel_id=1, source_target_pairs={{0,64},{16,80},{32,96},{48,112},{64,128},{80,144},{96,160},{112,17... | collective-permute-start | bytes 786440 | tf_op jit(solution)/shard_map/ppermute | solution.py:19
  38.9 1.7 fusion.77
  40.6 1.6 collective-permute-start.1
  44.3 9.5 %collective-permute-start.6 = (f32[8,64,128]{2,1,0:T(8,128)}, f32[8,64,128]{2,1,0:T(8,128)}, u32[]{:S(2)}, u32[]{:S(2)}) collective-permute-start(f32[8,64,128]{2,1,0:T(8,128)} %multiply_add_fusion.1), channel_id=1, source_target_pairs={{0,128},{16,144},{32,160},{48,176},{64,192},{80,208},{96,224},{112... | collective-permute-start | bytes 786440 | tf_op jit(solution)/shard_map/ppermute | solution.py:19
  60.2 3.3 collective-permute-start.7
  66.1 1.5 fusion.18
  67.6 2.2 fusion.17
  71.3 14.3 %all-to-all-start = ((bf16[16,16,512]{2,1,0:T(8,128)(2,1)}), bf16[16,16,512]{2,1,0:T(8,128)(2,1)S(1)}, u32[]{:S(2)}, u32[]{:S(2)}) async-start(bf16[16,16,512]{2,1,0:T(8,128)(2,1)} %bitcast.10), calls=%async_computation | async-start | bytes 524288 | tf_op jit(solution)/shard_map/all_to_all | solution.py:90
  86.0 11.3 %all-to-all-done = bf16[16,16,512]{2,1,0:T(8,128)(2,1)S(1)} async-done(((bf16[16,16,512]{2,1,0:T(8,128)(2,1)}), bf16[16,16,512]{2,1,0:T(8,128)(2,1)S(1)}, u32[]{:S(2)}, u32[]{:S(2)}) %all-to-all-start) | async-done | bytes 262176 | tf_op jit(solution)/shard_map/all_to_all | solution.py:90
  99.4 31.2 %all_to_all.23 = bf16[3,16,8192]{2,0,1:T(4,128)(2,1)S(1)} all-to-all(bf16[3,16,8192]{2,0,1:T(4,128)(2,1)S(1)} %copy.99), channel_id=1, replica_groups=mesh['seq'=16,'exp'=16] {'exp'}, dimensions={1} | all-to-all | bytes 1572864 | tf_op jit(solution)/shard_map/all_to_all | solution.py:112
  134.1 49.5 %all-gather.6.cloned.1.call-done = bf16[1,256,8192]{2,1,0:T(8,128)(2,1)} async-done(((bf16[1,16,8192]{2,1,0:T(8,128)(2,1)}), bf16[1,256,8192]{2,1,0:T(8,128)(2,1)}) %all-gather.6.cloned.1.call-update) | async-done | bytes 4194320 | tf_op jit(solution)/shard_map/all_gather | solution.py:116
  183.6 4.1 fusion.6
  187.7 7.3 %convolution_convert_fusion.1 = bf16[256,8192]{1,0:T(8,128)(2,1)} fusion(bf16[1,128,8192]{2,1,0:T(8,128)(2,1)S(1)} %copy-done, bf16[1,8192,128]{2,1,0:T(8,128)(2,1)} %param.30, bf16[1,256,8192]{2,1,0:T(8,128)(2,1)} %all-gather.6.cloned.1.call-done, f32[256,128]{1,0:T(8,128)S(1)} %fusion.6), kind=kOutput, calls=%fused_computation.10 | convolution fusion | flops 1076035584 | bytes 12713984 | tf_op jit(solution)/shard_map/dot_general | solution.py:120
  195.1 66.5 %all-gather.4.cloned.1.call-done = bf16[512,8192]{1,0:T(8,128)(2,1)} async-done(((bf16[32,8192]{1,0:T(8,128)(2,1)}), bf16[512,8192]{1,0:T(8,128)(2,1)}) %all-gather.4.cloned.1.call-update) | async-done | bytes 8388624 | tf_op jit(solution)/shard_map/all_gather | solution.py:116
  261.6 6.4 %fusion.13 = f32[512,128]{1,0:T(8,128)S(1)} fusion(bf16[512,8192]{1,0:T(8,128)(2,1)} %all-gather.4.cloned.1.call-done, bf16[1,8192,128]{2,1,0:T(8,128)(2,1)} %param.29), kind=kOutput, calls=%fused_computation.21 | convolution fusion | flops 1073741824 | bytes 10747904 | tf_op jit(solution)/shard_map/dot_general | solution.py:117
  268.6 2.3 fusion.22
  270.9 5.6 %convolution_convert_fusion = bf16[512,8192]{1,0:T(8,128)(2,1)} fusion(bf16[512,128]{1,0:T(8,128)(2,1)S(1)} %fusion.22, bf16[1,128,8192]{2,1,0:T(8,128)(2,1)S(1)} %copy-done), kind=kOutput, calls=%fused_computation.9 | convolution fusion | flops 1077936128 | bytes 10616832 | tf_op jit(solution)/shard_map/dot_general | solution.py:120
  276.5 69.4 %reduce-scatter.3.cloned.1.call-done = bf16[16,8192]{1,0:T(8,128)(2,1)} async-done(((bf16[256,8192]{1,0:T(8,128)(2,1)}), bf16[16,8192]{1,0:T(8,128)(2,1)}) %reduce-scatter.3.cloned.1.call-update) | async-done | bytes 262160 | tf_op jit(solution)/shard_map/reduce_scatter | solution.py:122
  345.9 94.2 %reduce-scatter.5.cloned.1.call-done = bf16[32,8192]{1,0:T(8,128)(2,1)} async-done(((bf16[512,8192]{1,0:T(8,128)(2,1)}), bf16[32,8192]{1,0:T(8,128)(2,1)}) %reduce-scatter.5.cloned.1.call-update) | async-done | bytes 524304 | tf_op jit(solution)/shard_map/reduce_scatter | solution.py:122
  441.4 1.7 copy.102
  443.0 9.0 %all-to-all-start.2 = ((bf16[3,16,8192]{2,0,1:T(4,128)(2,1)}), bf16[3,16,8192]{2,0,1:T(4,128)(2,1)}, u32[]{:S(2)}, u32[]{:S(2)}) async-start(bf16[3,16,8192]{2,0,1:T(4,128)(2,1)} %copy.102), calls=%async_computation.4 | async-start | bytes 2097152 | tf_op jit(solution)/shard_map/all_to_all | solution.py:125
  452.2 27.8 %all-to-all-done.2 = bf16[3,16,8192]{2,0,1:T(4,128)(2,1)} async-done(((bf16[3,16,8192]{2,0,1:T(4,128)(2,1)}), bf16[3,16,8192]{2,0,1:T(4,128)(2,1)}, u32[]{:S(2)}, u32[]{:S(2)}) %all-to-all-start.2) | async-done | bytes 786464 | tf_op jit(solution)/shard_map/all_to_all | solution.py:125
  480.0 1.8 copy.103
  481.8 1.7 gather_fusion
  483.5 1.7 reshape.142
  485.2 1.4 multiply_reduce_fusion
  (98 shorter events, 27.5 us)
Async XLA Ops:
  6.5 181.2 %copy-start = (bf16[1,128,8192]{2,1,0:T(8,128)(2,1)S(1)}, bf16[1,128,8192]{2,1,0:T(8,128)(2,1)}, u32[]{:S(2)}) copy-start(bf16[1,128,8192]{2,1,0:T(8,128)(2,1)} %param.31) | copy-start | bytes 6291460
  6.5 4.3 copy-start.3
  13.0 9.0 %collective-permute-start.3 = (f32[8,64,128]{2,1,0:T(8,128)S(1)}, f32[8,64,128]{2,1,0:T(8,128)S(1)}, u32[]{:S(2)}, u32[]{:S(2)}) collective-permute-start(f32[8,64,128]{2,1,0:T(8,128)S(1)} %get-tuple-element.48), channel_id=1, source_target_pairs={{0,16},{16,32},{32,48},{48,64},{64,80},{80,96},{96,112},{112,128},... | collective-permute-start | bytes 786440 | tf_op jit(solution)/shard_map/ppermute | solution.py:19
  17.0 5.0 %collective-permute-start = (f32[8]{0:T(128)S(1)}, f32[8]{0:T(128)S(1)}, u32[]{:S(2)}, u32[]{:S(2)}) collective-permute-start(f32[8]{0:T(128)S(1)} %get-tuple-element.47), channel_id=1, source_target_pairs={{0,16},{16,32},{32,48},{48,64},{64,80},{80,96},{96,112},{112,128},... | collective-permute-start | bytes 104 | tf_op jit(solution)/shard_map/ppermute | solution.py:19
  22.0 9.7 %copy-start.6 = (f32[8]{0:T(128)}, f32[8]{0:T(128)S(1)}, u32[]{:S(2)}) copy-start(f32[8]{0:T(128)S(1)} %collective-permute-done) | copy-start | bytes 100
  22.1 9.6 %collective-permute-start.4 = (f32[8,64,128]{2,1,0:T(8,128)S(1)}, f32[8,64,128]{2,1,0:T(8,128)S(1)}, u32[]{:S(2)}, u32[]{:S(2)}) collective-permute-start(f32[8,64,128]{2,1,0:T(8,128)S(1)} %multiply_add_fusion.3), channel_id=1, source_target_pairs={{0,32},{16,48},{32,64},{48,80},{64,96},{80,112},{96,128},{112,144}... | collective-permute-start | bytes 786440 | tf_op jit(solution)/shard_map/ppermute | solution.py:19
  31.7 11.8 %collective-permute-start.5 = (f32[8,64,128]{2,1,0:T(8,128)S(1)}, f32[8,64,128]{2,1,0:T(8,128)S(1)}, u32[]{:S(2)}, u32[]{:S(2)}) collective-permute-start(f32[8,64,128]{2,1,0:T(8,128)S(1)} %multiply_add_fusion.2), channel_id=1, source_target_pairs={{0,64},{16,80},{32,96},{48,112},{64,128},{80,144},{96,160},{112,17... | collective-permute-start | bytes 786440 | tf_op jit(solution)/shard_map/ppermute | solution.py:19
  40.6 2.3 collective-permute-start.1
  43.0 0.6 copy-start.7
  44.3 20.5 %collective-permute-start.6 = (f32[8,64,128]{2,1,0:T(8,128)}, f32[8,64,128]{2,1,0:T(8,128)}, u32[]{:S(2)}, u32[]{:S(2)}) collective-permute-start(f32[8,64,128]{2,1,0:T(8,128)} %multiply_add_fusion.1), channel_id=1, source_target_pairs={{0,128},{16,144},{32,160},{48,176},{64,192},{80,208},{96,224},{112... | collective-permute-start | bytes 786440 | tf_op jit(solution)/shard_map/ppermute | solution.py:19
  54.6 13.0 %copy-start.5 = (pred[128,128]{1,0:T(8,128)(4,1)S(1)}, pred[128,128]{1,0:T(8,128)(4,1)}, u32[]{:S(2)}) copy-start(pred[128,128]{1,0:T(8,128)(4,1)} %iota_compare_fusion) | copy-start | bytes 49156
  57.5 2.1 collective-permute-start.2
  60.2 4.0 collective-permute-start.7
  70.2 27.2 %copy-start.2 = (bf16[16,8192]{1,0:T(8,128)(2,1)S(1)}, bf16[16,8192]{1,0:T(8,128)(2,1)}, u32[]{:S(2)}) copy-start(bf16[16,8192]{1,0:T(8,128)(2,1)} %param.25) | copy-start | bytes 786436
  70.4 27.2 %copy-start.4 = (f32[8192]{0:T(1024)S(1)}, f32[8192]{0:T(1024)}, u32[]{:S(2)}) copy-start(f32[8192]{0:T(1024)} %param.26) | copy-start | bytes 98308
  71.3 26.0 %all-to-all-start = ((bf16[16,16,512]{2,1,0:T(8,128)(2,1)}), bf16[16,16,512]{2,1,0:T(8,128)(2,1)S(1)}, u32[]{:S(2)}, u32[]{:S(2)}) async-start(bf16[16,16,512]{2,1,0:T(8,128)(2,1)} %bitcast.10), calls=%async_computation | async-start | bytes 524288 | tf_op jit(solution)/shard_map/all_to_all | solution.py:90
  85.6 98.0 %all-gather.6.cloned.1.call-start = ((), (), s32[]{:S(2)}) async-start(), calls=%async_computation.8 | async-start | bytes 4456448 | tf_op jit(solution)/shard_map/all_gather | solution.py:116
  132.1 129.5 %all-gather.4.cloned.1.call-start = ((), (), s32[]{:S(2)}) async-start(), calls=%async_computation.6 | async-start | bytes 8912896 | tf_op jit(solution)/shard_map/all_gather | solution.py:116
  133.9 212.1 %reduce-scatter.3.cloned.1.call-start = ((), (), s32[]{:S(2)}) async-start(), calls=%async_computation.5 | async-start | bytes 4456448 | tf_op jit(solution)/shard_map/reduce_scatter | solution.py:122
  195.0 245.2 %reduce-scatter.5.cloned.1.call-start = ((), (), s32[]{:S(2)}) async-start(), calls=%async_computation.7 | async-start | bytes 8912896 | tf_op jit(solution)/shard_map/reduce_scatter | solution.py:122
  261.6 6.5 %copy-start.1 = (bf16[1,8192,128]{2,1,0:T(8,128)(2,1)S(1)}, bf16[1,8192,128]{2,1,0:T(8,128)(2,1)}, u32[]{:S(2)}) copy-start(bf16[1,8192,128]{2,1,0:T(8,128)(2,1)} %param.30) | copy-start | bytes 6291460
  261.6 7.0 %copy-start.9 = (bf16[512,8192]{1,0:T(8,128)(2,1)S(1)}, bf16[512,8192]{1,0:T(8,128)(2,1)}, u32[]{:S(2)}) copy-start(bf16[512,8192]{1,0:T(8,128)(2,1)} %all-gather.4.cloned.1.call-done) | copy-start | bytes 25165828
  441.4 10.7 %copy-start.8 = (f32[16,2]{0,1:T(2,128)S(1)}, f32[16,2]{0,1:T(2,128)}, u32[]{:S(2)}) copy-start(f32[16,2]{0,1:T(2,128)} %param.28) | copy-start | bytes 388
  443.0 37.0 %all-to-all-start.2 = ((bf16[3,16,8192]{2,0,1:T(4,128)(2,1)}), bf16[3,16,8192]{2,0,1:T(4,128)(2,1)}, u32[]{:S(2)}, u32[]{:S(2)}) async-start(bf16[3,16,8192]{2,0,1:T(4,128)(2,1)} %copy.102), calls=%async_computation.4 | async-start | bytes 2097152 | tf_op jit(solution)/shard_map/all_to_all | solution.py:125
Sparse Core Ops, SparseCore 0:
  132.2 51.3 all-gather.5
  186.0 75.4 all-gather.3
  265.2 80.6 reduce-scatter.2
  350.0 90.1 reduce-scatter.4

commit v3 on v1

--- a/solution.py
+++ b/solution.py
@@ -2,11 +2,59 @@
 import jax.numpy as jnp
 from jax import lax
 from jax.sharding import PartitionSpec as P
+from jax.experimental import pallas as pl
+from jax.experimental.pallas import tpu as pltpu
 
 GROUP = 128
 
 
 PRECISE = lax.Precision.HIGHEST
+
+
+def exchange_body(x_ref, o_ref, send_sem, recv_sem, local_sem):
+    devices = x_ref.shape[0]
+    me = lax.axis_index("exp")
+    row = lax.axis_index("seq")
+    mesh_id = pl.DeviceIdType.MESH
+    barrier = pltpu.get_barrier_semaphore()
+    for step in range(1, devices):
+        peer = lax.rem(me + step, devices)
+        pl.semaphore_signal(barrier, 1, device_id=(row, peer), device_id_type=mesh_id)
+    pl.semaphore_wait(barrier, devices - 1)
+    local = pltpu.make_async_copy(x_ref.at[me], o_ref.at[me], local_sem)
+    local.start()
+    copies = []
+    for step in range(1, devices):
+        peer = lax.rem(me + step, devices)
+        copy = pltpu.make_async_remote_copy(
+            src_ref=x_ref.at[peer],
+            dst_ref=o_ref.at[me],
+            send_sem=send_sem.at[step],
+            recv_sem=recv_sem.at[step],
+            device_id=(row, peer),
+            device_id_type=mesh_id,
+        )
+        copy.start()
+        copies.append(copy)
+    local.wait()
+    for copy in copies:
+        copy.wait()
+
+
+def exchange(x, collective):
+    devices = x.shape[0]
+    return pl.pallas_call(
+        exchange_body,
+        out_shape=jax.ShapeDtypeStruct(x.shape, x.dtype),
+        in_specs=[pl.BlockSpec(memory_space=pltpu.VMEM)],
+        out_specs=pl.BlockSpec(memory_space=pltpu.VMEM),
+        scratch_shapes=[
+            pltpu.SemaphoreType.DMA((devices,)),
+            pltpu.SemaphoreType.DMA((devices,)),
+            pltpu.SemaphoreType.DMA,
+        ],
+        compiler_params=pltpu.CompilerParams(collective_id=collective, has_side_effects=True),
+    )(x)
 
 
 def exclusive_scan(log, state, axis):
@@ -87,7 +135,10 @@
         token_count, channels
     )
     mixer = (mixed_out * jax.nn.silu(z_gate.astype(jnp.float32))).astype(jnp.bfloat16)
-    token_mix = lax.all_to_all(mixer, "exp", split_axis=0, concat_axis=1, tiled=True)
+    owners = lax.axis_size("exp")
+    rows_here = residual.shape[0]
+    arrived_mix = exchange(mixer.reshape(owners, rows_here, channels), 0)
+    token_mix = arrived_mix.transpose(1, 0, 2).reshape(rows_here, owners * channels)
     stream = (residual.astype(jnp.float32) + token_mix.astype(jnp.float32)).astype(jnp.bfloat16)
     widened = stream.astype(jnp.float32)
     normed = (
@@ -95,8 +146,6 @@
         * lax.rsqrt(jnp.mean(widened * widened, axis=-1, keepdims=True) + 1e-06)
         * norm_gain[None, :]
     ).astype(jnp.bfloat16)
-    rows_here = residual.shape[0]
-    owners = lax.axis_size("exp")
     local_experts = w_gate.shape[0]
     experts = owners * local_experts
     capacity = max(2, 2 * rows_here // experts + 1)
@@ -104,12 +153,12 @@
     chosen = expert_ids.reshape(-1)
     onehot = (chosen[:, None] == jnp.arange(experts)[None, :]).astype(jnp.int32)
     slot_index = jnp.sum((jnp.cumsum(onehot, axis=0) - onehot) * onehot, axis=1)
-    target = slot_index * experts + chosen
+    target = chosen * capacity + slot_index
     placing = (target[None, :] == jnp.arange(experts * capacity)[:, None]).astype(jnp.bfloat16)
     pair_rows = jnp.repeat(normed, 2, axis=0)
     outgoing = jnp.dot(placing, pair_rows, preferred_element_type=jnp.float32).astype(jnp.bfloat16)
-    outgoing = outgoing.reshape(capacity, experts, width)
-    arrived = lax.all_to_all(outgoing, "exp", split_axis=1, concat_axis=1, tiled=True)
+    block = capacity * width // 16
+    arrived = exchange(outgoing.reshape(experts, 16, block), 1)
     arrived = arrived.reshape(capacity * experts, width)
     segment = lax.all_gather(arrived, "seq", axis=0, tiled=True)
     gate_proj = jnp.dot(segment, w_gate[0], preferred_element_type=jnp.float32)
@@ -117,8 +166,7 @@
     active = (jax.nn.silu(gate_proj) * up_proj).astype(jnp.bfloat16)
     partial_value = jnp.dot(active, w_down[0], preferred_element_type=jnp.float32)
     summed = lax.psum_scatter(partial_value.astype(jnp.bfloat16), "seq", scatter_dimension=0, tiled=True)
-    summed = summed.reshape(capacity, experts, width)
-    returned = lax.all_to_all(summed, "exp", split_axis=1, concat_axis=1, tiled=True)
+    returned = exchange(summed.reshape(experts, 16, block), 2)
     results = returned.reshape(experts * capacity, width)
     picked = results[target].astype(jnp.float32).reshape(rows_here, 2, width)
     mixture = jnp.sum(picked * gate_weights[:, :, None], axis=1)

time: 401 us -> 393 us (0.980)
  Pallas kernels: 0 us -> 74.3 us
  waiting for transfers between devices: 236 us -> 200 us
  blocking collectives: 31.2 us -> 0 us
  starting transfers between devices: 58.2 us -> 35.8 us
  local copies, waits for them, and re-layouts: 18 us -> 22.7 us
    pallas_call x0 -> x3, Pallas kernels: none -> 74.3 us  [exchange(): pl.pallas_call(exchange_body, out_shape=jax.ShapeDtypeStruct(x.shape, x.d...]
    all_to_all x2 -> x0, waiting for transfers between devices: 39.2 us -> none  [the longest x1 27.8 us: on_device(): lax.all_to_all(summed, 'exp', split_axis=1, concat_axis=1, tiled=True)]
    all_to_all x1 -> x0, blocking collectives: 31.2 us -> none  [on_device(): lax.all_to_all(outgoing, 'exp', split_axis=1, concat_axis=1, tiled=True)]
    all_to_all x2 -> x0, starting transfers between devices: 21.8 us -> none  [the longest x1 13.9 us: on_device(): lax.all_to_all(mixer, 'exp', split_axis=0, concat_axis=1, tiled=True)]
    reshape x2 -> x4, local copies, waits for them, and re-layouts: 3.47 us -> 10.2 us  [the longest x1 3.1 us: on_device(): arrived = arrived.reshape(capacity * experts, width)]
  transfers between devices with their start and end apart: 12 -> 10, of which waited for: 9 -> 8; matrix products, arithmetic and copies ran while one was open for 2% -> 2% of each run, Pallas kernels for 0% -> 0%
where the time goes in v3:
time: 393 us; the launch traced here: 392 us
  waiting for transfers between devices  200 us (51%)
  Pallas kernels  74.3 us (19%)
  starting transfers between devices  35.8 us (9%)
  matrix products  32.7 us (8%)
  local copies, waits for them, and re-layouts  22.7 us (6%)
  between operations  13.8 us (4%)
  other arithmetic  12.8 us (3%)
    reduce_scatter x1, waiting for transfers between devices, on_device(): lax.psum_scatter(partial_value.astype(jnp.bfloat16), 'seq', scatter_dimen...  98.3 us
    all_gather x1, waiting for transfers between devices, on_device(): segment = lax.all_gather(arrived, 'seq', axis=0, tiled=True)  92.7 us
    pallas_call x3, Pallas kernels, exchange(): pl.pallas_call(exchange_body, out_shape=jax.ShapeDtypeStruct(x.shape, x.d...  74.3 us
    ppermute x8, starting transfers between devices, exclusive_scan(): got = (lax.ppermute(inc[0], axis, pairs), lax.ppermute(inc[1], axis, pairs))  35.5 us
    dot_general x1, matrix products, on_device(): jnp.dot(active, w_down[0], preferred_element_type=jnp.float32)  19.4 us
    ppermute x8, waiting for transfers between devices, exclusive_scan(): got = (lax.ppermute(inc[0], axis, pairs), lax.ppermute(inc[1], axis, pairs))  9.24 us
  transfers between devices with their start and end apart: 10, of which 8 were waited for; matrix products, arithmetic and copies ran while one was open for 2% of the time, Pallas kernels for 0%

profile of v3, /device:TPU:1, one launch (start us, length us, event | category | flops | bytes accessed | tf_op | source)
XLA Modules:
  0.0 392.4 jit_solution(6510212217702151709)
XLA Ops:
  9.2 1.3 reshape.151
  11.3 1.8 while.17
  13.1 3.9 %collective-permute-start = (f32[8]{0:T(128)S(1)}, f32[8]{0:T(128)S(1)}, u32[]{:S(2)}, u32[]{:S(2)}) collective-permute-start(f32[8]{0:T(128)S(1)} %get-tuple-element.47), channel_id=1, source_target_pairs={{0,16},{16,32},{32,48},{48,64},{64,80},{80,96},{96,112},{112,128},... | collective-permute-start | bytes 104 | tf_op jit(solution)/shard_map/ppermute | solution.py:67
  17.0 3.1 collective-permute-start.3
  20.5 4.3 %collective-permute-done.3 = f32[8,64,128]{2,1,0:T(8,128)S(1)} collective-permute-done((f32[8,64,128]{2,1,0:T(8,128)S(1)}, f32[8,64,128]{2,1,0:T(8,128)S(1)}, u32[]{:S(2)}, u32[]{:S(2)}) %collective-permute-start.3) | collective-permute-done | bytes 262176 | tf_op jit(solution)/shard_map/ppermute | solution.py:67
  24.9 5.4 %collective-permute-start.4 = (f32[8,64,128]{2,1,0:T(8,128)S(1)}, f32[8,64,128]{2,1,0:T(8,128)S(1)}, u32[]{:S(2)}, u32[]{:S(2)}) collective-permute-start(f32[8,64,128]{2,1,0:T(8,128)S(1)} %multiply_add_fusion.3), channel_id=1, source_target_pairs={{0,32},{16,48},{32,64},{48,80},{64,96},{80,112},{96,128},{112,144}... | collective-permute-start | bytes 786440 | tf_op jit(solution)/shard_map/ppermute | solution.py:67
  31.3 2.7 collective-permute-done.4
  34.0 7.5 %collective-permute-start.5 = (f32[8,64,128]{2,1,0:T(8,128)S(1)}, f32[8,64,128]{2,1,0:T(8,128)S(1)}, u32[]{:S(2)}, u32[]{:S(2)}) collective-permute-start(f32[8,64,128]{2,1,0:T(8,128)S(1)} %multiply_add_fusion.2), channel_id=1, source_target_pairs={{0,64},{16,80},{32,96},{48,112},{64,128},{80,144},{96,160},{112,17... | collective-permute-start | bytes 786440 | tf_op jit(solution)/shard_map/ppermute | solution.py:67
  42.1 1.3 collective-permute-start.1
  45.6 9.7 %collective-permute-start.6 = (f32[8,64,128]{2,1,0:T(8,128)}, f32[8,64,128]{2,1,0:T(8,128)}, u32[]{:S(2)}, u32[]{:S(2)}) collective-permute-start(f32[8,64,128]{2,1,0:T(8,128)} %multiply_add_fusion.1), channel_id=1, source_target_pairs={{0,128},{16,144},{32,160},{48,176},{64,192},{80,208},{96,224},{112... | collective-permute-start | bytes 786440 | tf_op jit(solution)/shard_map/ppermute | solution.py:67
  57.7 1.1 copy.33
  58.8 1.3 collective-permute-start.2
  61.5 3.3 collective-permute-start.7
  66.1 1.2 multiply_add_fusion
  67.3 1.5 fusion.11
  68.8 2.2 fusion.10
  72.5 22.3 %shard_map.145 = bf16[16,16,512]{2,1,0:T(8,128)(2,1)} custom-call(bf16[16,16,512]{2,1,0:T(8,128)(2,1)} %bitcast.85), custom_call_target="tpu_custom_call" | custom-call | tf_op jit(solution)/shard_map/pallas_call | solution.py:46
  96.7 1.0 reshape.134
  97.7 1.4 convolution_convert_fusion.1
  99.1 1.9 reshape.135.x_ref
  101.0 25.1 %shard_map.146 = bf16[16,16,1536]{2,1,0:T(8,128)(2,1)} custom-call(bf16[16,16,1536]{2,1,0:T(8,128)(2,1)} %reshape.135.x_ref), custom_call_target="tpu_custom_call" | custom-call | tf_op jit(solution)/shard_map/pallas_call | solution.py:46
  126.1 3.1 reshape.136
  129.5 92.7 %all-gather.2.cloned.1.call-done = bf16[768,8192]{1,0:T(8,128)(2,1)} async-done(((bf16[48,8192]{1,0:T(8,128)(2,1)}), bf16[768,8192]{1,0:T(8,128)(2,1)}) %all-gather.2.cloned.1.call-update) | async-done | bytes 12582928 | tf_op jit(solution)/shard_map/all_gather | solution.py:163
  222.2 7.0 %fusion.7 = f32[768,128]{1,0:T(8,128)S(1)} fusion(bf16[768,8192]{1,0:T(8,128)(2,1)} %all-gather.2.cloned.1.call-done, bf16[1,8192,128]{2,1,0:T(8,128)(2,1)} %param.29), kind=kOutput, calls=%fused_computation.14 | convolution fusion | flops 1610612736 | bytes 15073280 | tf_op jit(solution)/shard_map/dot_general | solution.py:164
  229.2 19.4 %convolution_convert_fusion = bf16[768,8192]{1,0:T(8,128)(2,1)} fusion(bf16[1,128,8192]{2,1,0:T(8,128)(2,1)S(1)} %copy-done, bf16[768,8192]{1,0:T(8,128)(2,1)} %all-gather.2.cloned.1.call-done, bf16[1,8192,128]{2,1,0:T(8,128)(2,1)} %param.30, f32[768,128]{1,0:T(8,128)S(1)} %fusion.7), kind=kOutput, calls=%fused_computation.9 | convolution fusion | flops 3228106752 | bytes 29753344 | tf_op jit(solution)/shard_map/dot_general | solution.py:167
  249.6 98.3 %reduce-scatter.2.cloned.1.call-done = bf16[48,8192]{1,0:T(8,128)(2,1)} async-done(((bf16[768,8192]{1,0:T(8,128)(2,1)}), bf16[48,8192]{1,0:T(8,128)(2,1)}) %reduce-scatter.2.cloned.1.call-update) | async-done | bytes 786448 | tf_op jit(solution)/shard_map/reduce_scatter | solution.py:168
  347.9 3.0 reshape.137.x_ref
  350.9 26.9 %shard_map.147 = bf16[16,16,1536]{2,1,0:T(8,128)(2,1)} custom-call(bf16[16,16,1536]{2,1,0:T(8,128)(2,1)} %reshape.137.x_ref), custom_call_target="tpu_custom_call" | custom-call | tf_op jit(solution)/shard_map/pallas_call | solution.py:46
  377.8 2.2 reshape.138
  379.9 1.7 gather_fusion
  381.6 1.7 reshape.140
  383.3 1.4 multiply_reduce_fusion
  (95 shorter events, 19.7 us)
Async XLA Ops:
  6.5 222.7 %copy-start = (bf16[1,128,8192]{2,1,0:T(8,128)(2,1)S(1)}, bf16[1,128,8192]{2,1,0:T(8,128)(2,1)}, u32[]{:S(2)}) copy-start(bf16[1,128,8192]{2,1,0:T(8,128)(2,1)} %param.31) | copy-start | bytes 6291460
  6.5 4.3 %copy-start.3 = (bf16[256,128]{1,0:T(8,128)(2,1)S(1)}, bf16[256,128]{1,0:T(8,128)(2,1)}, u32[]{:S(2)}) copy-start(bf16[256,128]{1,0:T(8,128)(2,1)} %param.19) | copy-start | bytes 196612
  6.5 215.6 %all-gather.2.cloned.1.call-start = ((), (), s32[]{:S(2)}) async-start(), calls=%async_computation.1 | async-start | bytes 13369344 | tf_op jit(solution)/shard_map/all_gather | solution.py:163
  11.3 8.9 %copy-start.6 = (s32[16,2]{0,1:T(2,128)S(1)}, s32[16,2]{0,1:T(2,128)}, u32[]{:S(2)}) copy-start(s32[16,2]{0,1:T(2,128)} %param.27) | copy-start | bytes 388
  11.3 19.2 %copy-start.1 = (bf16[256,128]{1,0:T(8,128)(2,1)S(1)}, bf16[256,128]{1,0:T(8,128)(2,1)}, u32[]{:S(2)}) copy-start(bf16[256,128]{1,0:T(8,128)(2,1)} %param.20) | copy-start | bytes 196612
  13.1 7.3 %copy-start.11 = (f32[2,8]{1,0:T(2,128)}, f32[2,8]{1,0:T(2,128)S(1)}, u32[]{:S(2)}) copy-start(f32[2,8]{1,0:T(2,128)S(1)} %get-tuple-element.46) | copy-start | bytes 196
  13.1 7.4 %collective-permute-start = (f32[8]{0:T(128)S(1)}, f32[8]{0:T(128)S(1)}, u32[]{:S(2)}, u32[]{:S(2)}) collective-permute-start(f32[8]{0:T(128)S(1)} %get-tuple-element.47), channel_id=1, source_target_pairs={{0,16},{16,32},{32,48},{48,64},{64,80},{80,96},{96,112},{112,128},... | collective-permute-start | bytes 104 | tf_op jit(solution)/shard_map/ppermute | solution.py:67
  17.0 7.8 %collective-permute-start.3 = (f32[8,64,128]{2,1,0:T(8,128)S(1)}, f32[8,64,128]{2,1,0:T(8,128)S(1)}, u32[]{:S(2)}, u32[]{:S(2)}) collective-permute-start(f32[8,64,128]{2,1,0:T(8,128)S(1)} %get-tuple-element.48), channel_id=1, source_target_pairs={{0,16},{16,32},{32,48},{48,64},{64,80},{80,96},{96,112},{112,128},... | collective-permute-start | bytes 786440 | tf_op jit(solution)/shard_map/ppermute | solution.py:67
  20.5 13.5 %copy-start.8 = (f32[8]{0:T(128)}, f32[8]{0:T(128)S(1)}, u32[]{:S(2)}) copy-start(f32[8]{0:T(128)S(1)} %collective-permute-done) | copy-start | bytes 100
  24.9 9.1 %collective-permute-start.4 = (f32[8,64,128]{2,1,0:T(8,128)S(1)}, f32[8,64,128]{2,1,0:T(8,128)S(1)}, u32[]{:S(2)}, u32[]{:S(2)}) collective-permute-start(f32[8,64,128]{2,1,0:T(8,128)S(1)} %multiply_add_fusion.3), channel_id=1, source_target_pairs={{0,32},{16,48},{32,64},{48,80},{64,96},{80,112},{96,128},{112,144}... | collective-permute-start | bytes 786440 | tf_op jit(solution)/shard_map/ppermute | solution.py:67
  30.4 24.9 %copy-start.13 = (s32[32]{0:T(128)}, s32[32]{0:T(128)S(1)}, u32[]{:S(2)}) copy-start(s32[32]{0:T(128)S(1)} %select_reduce_fusion) | copy-start | bytes 388
  34.0 10.8 %collective-permute-start.5 = (f32[8,64,128]{2,1,0:T(8,128)S(1)}, f32[8,64,128]{2,1,0:T(8,128)S(1)}, u32[]{:S(2)}, u32[]{:S(2)}) collective-permute-start(f32[8,64,128]{2,1,0:T(8,128)S(1)} %multiply_add_fusion.2), channel_id=1, source_target_pairs={{0,64},{16,80},{32,96},{48,112},{64,128},{80,144},{96,160},{112,17... | collective-permute-start | bytes 786440 | tf_op jit(solution)/shard_map/ppermute | solution.py:67
  42.1 2.0 collective-permute-start.1
  44.2 1.5 copy-start.9
  45.6 20.5 %collective-permute-start.6 = (f32[8,64,128]{2,1,0:T(8,128)}, f32[8,64,128]{2,1,0:T(8,128)}, u32[]{:S(2)}, u32[]{:S(2)}) collective-permute-start(f32[8,64,128]{2,1,0:T(8,128)} %multiply_add_fusion.1), channel_id=1, source_target_pairs={{0,128},{16,144},{32,160},{48,176},{64,192},{80,208},{96,224},{112... | collective-permute-start | bytes 786440 | tf_op jit(solution)/shard_map/ppermute | solution.py:67
  56.0 12.8 %copy-start.5 = (f32[2,128,8]{1,2,0:T(8,128)S(1)}, f32[2,128,8]{1,2,0:T(8,128)}, u32[]{:S(2)}) copy-start(f32[2,128,8]{1,2,0:T(8,128)} %copy.25) | copy-start | bytes 24580
  58.8 2.1 collective-permute-start.2
  61.5 4.0 %collective-permute-start.7 = (f32[8]{0:T(128)S(1)}, f32[8]{0:T(128)S(1)}, u32[]{:S(2)}, u32[]{:S(2)}) collective-permute-start(f32[8]{0:T(128)S(1)} %add.120), channel_id=1, source_target_pairs={{0,128},{16,144},{32,160},{48,176},{64,192},{80,208},{96,224},{112... | collective-permute-start | bytes 104 | tf_op jit(solution)/shard_map/ppermute | solution.py:67
  71.5 24.4 %copy-start.2 = (bf16[16,8192]{1,0:T(8,128)(2,1)S(1)}, bf16[16,8192]{1,0:T(8,128)(2,1)}, u32[]{:S(2)}) copy-start(bf16[16,8192]{1,0:T(8,128)(2,1)} %param.25) | copy-start | bytes 786436
  71.7 24.5 %copy-start.4 = (f32[8192]{0:T(1024)S(1)}, f32[8192]{0:T(1024)}, u32[]{:S(2)}) copy-start(f32[8192]{0:T(1024)} %param.26) | copy-start | bytes 98308
  95.9 1.9 copy-start.12
  129.2 218.6 %reduce-scatter.2.cloned.1.call-start = ((), (), s32[]{:S(2)}) async-start(), calls=%async_computation.2 | async-start | bytes 13369344 | tf_op jit(solution)/shard_map/reduce_scatter | solution.py:168
  248.6 0.7 copy-start.7
  248.6 0.9 copy-start.10
  248.6 1.0 copy-start.14
Sparse Core Ops, SparseCore 0:
  129.4 92.7 all-gather.1
  248.8 99.0 reduce-scatter.1

commit v4 on v3

--- a/solution.py
+++ b/solution.py
@@ -1,3 +1,5 @@
+import functools
+
 import jax
 import jax.numpy as jnp
 from jax import lax
@@ -57,18 +59,80 @@
     )(x)
 
 
+def scan_rounds(devices):
+    rounds, base = [], 1
+    while base < devices:
+        rounds.append([j * base for j in range(1, 4) if j * base < devices])
+        base *= 4
+    return rounds
+
+
+def fold(earlier, later, state_rows):
+    row = lax.broadcasted_iota(jnp.int32, later.shape, 1)
+    decay = jnp.exp(later[:, state_rows:state_rows + 1, :])
+    return jnp.where(row < state_rows, decay, 1.0) * earlier + later
+
+
+def scan_body(devices, state_rows, x_ref, o_ref, inc_ref, recv_ref, send_sem, recv_sem):
+    me = lax.axis_index("seq")
+    col = lax.axis_index("exp")
+    mesh_id = pl.DeviceIdType.MESH
+    barrier = pltpu.get_barrier_semaphore()
+    for step in range(1, devices):
+        peer = lax.rem(me + step, devices)
+        pl.semaphore_signal(barrier, 1, device_id=(peer, col), device_id_type=mesh_id)
+    pl.semaphore_wait(barrier, devices - 1)
+    inc_ref[0] = x_ref[...]
+    o_ref[...] = jnp.zeros_like(o_ref)
+    for level, shifts in enumerate(scan_rounds(devices)):
+        def link(slot, shift, peer):
+            return pltpu.make_async_remote_copy(
+                src_ref=inc_ref.at[level],
+                dst_ref=recv_ref.at[level, slot],
+                send_sem=send_sem.at[level, slot],
+                recv_sem=recv_sem.at[level, slot],
+                device_id=(peer, col),
+                device_id_type=mesh_id,
+            )
+        for slot, shift in enumerate(shifts):
+            @pl.when(me + shift < devices)
+            def _():
+                link(slot, shift, me + shift).start()
+        inc_ref[level + 1] = inc_ref[level]
+        for slot, shift in enumerate(shifts):
+            @pl.when(me >= shift)
+            def _():
+                link(slot, shift, me - shift).wait_recv()
+                got = recv_ref[level, slot]
+                inc_ref[level + 1] = fold(got, inc_ref[level + 1], state_rows)
+                o_ref[...] = fold(got, o_ref[...], state_rows)
+        for slot, shift in enumerate(shifts):
+            @pl.when(me + shift < devices)
+            def _():
+                link(slot, shift, me + shift).wait_send()
+
+
 def exclusive_scan(log, state, axis):
     devices = lax.axis_size(axis)
-    inc = (log, state)
-    exc = (jnp.zeros_like(log), jnp.zeros_like(state))
-    shift = 1
-    while shift < devices:
-        pairs = [(i, i + shift) for i in range(devices - shift)]
-        got = (lax.ppermute(inc[0], axis, pairs), lax.ppermute(inc[1], axis, pairs))
-        exc = chain_combine(got, exc)
-        inc = chain_combine(got, inc)
-        shift *= 2
-    return exc
+    heads, state_rows, lanes = state.shape
+    packed = jnp.concatenate(
+        [state, jnp.broadcast_to(log[:, None, None], (heads, 8, lanes))], axis=1
+    )
+    levels = len(scan_rounds(devices))
+    result = pl.pallas_call(
+        functools.partial(scan_body, devices, state_rows),
+        out_shape=jax.ShapeDtypeStruct(packed.shape, packed.dtype),
+        in_specs=[pl.BlockSpec(memory_space=pltpu.VMEM)],
+        out_specs=pl.BlockSpec(memory_space=pltpu.VMEM),
+        scratch_shapes=[
+            pltpu.VMEM((levels + 1,) + packed.shape, packed.dtype),
+            pltpu.VMEM((levels, 3) + packed.shape, packed.dtype),
+            pltpu.SemaphoreType.DMA((levels, 3)),
+            pltpu.SemaphoreType.DMA((levels, 3)),
+        ],
+        compiler_params=pltpu.CompilerParams(collective_id=3, has_side_effects=True),
+    )(packed)
+    return result[:, state_rows, 0], result[:, :state_rows, :]
 
 
 def chain_combine(earlier, later):

time: 393 us -> 376 us (0.957)
  starting transfers between devices: 35.8 us -> 0.22 us
  Pallas kernels: 74.3 us -> 109 us
  waiting for transfers between devices: 200 us -> 192 us
    pallas_call x0 -> x1, Pallas kernels: none -> 40.7 us  [exclusive_scan(): pl.pallas_call(functools.partial(scan_body, devices, state_rows), out_sha...]
    ppermute x8 -> x0, starting transfers between devices: 35.5 us -> none  [exclusive_scan(): got = (lax.ppermute(inc[0], axis, pairs), lax.ppermute(inc[1], axis, pairs))]
    ppermute x8 -> x0, waiting for transfers between devices: 9.24 us -> none  [exclusive_scan(): got = (lax.ppermute(inc[0], axis, pairs), lax.ppermute(inc[1], axis, pairs))]
    pallas_call x3, Pallas kernels: 74.3 us -> 68.6 us  [exchange(): pl.pallas_call(exchange_body, out_shape=jax.ShapeDtypeStruct(x.shape, x.d...]
  transfers between devices with their start and end apart: 10 -> 2, of which waited for: 8 -> 2; matrix products, arithmetic and copies ran while one was open for 2% -> 0% of each run, Pallas kernels for 0% -> 0%
where the time goes in v4:
time: 376 us
  waiting for transfers between devices  192 us (51%)
  Pallas kernels  109 us (29%)
  matrix products  30.1 us (8%)
  local copies, waits for them, and re-layouts  20.3 us (5%)
  between operations  13.7 us (4%)
  other arithmetic  10.3 us (3%)
    reduce_scatter x1, waiting for transfers between devices, on_device(): lax.psum_scatter(partial_value.astype(jnp.bfloat16), 'seq', scatter_dimen...  98.3 us
    all_gather x1, waiting for transfers between devices, on_device(): segment = lax.all_gather(arrived, 'seq', axis=0, tiled=True)  93.3 us
    pallas_call x3, Pallas kernels, exchange(): pl.pallas_call(exchange_body, out_shape=jax.ShapeDtypeStruct(x.shape, x.d...  68.6 us
    pallas_call x1, Pallas kernels, exclusive_scan(): pl.pallas_call(functools.partial(scan_body, devices, state_rows), out_sha...  40.7 us
    dot_general x1, matrix products, on_device(): jnp.dot(active, w_down[0], preferred_element_type=jnp.float32)  19.4 us
  transfers between devices with their start and end apart: 2, of which 2 were waited for; matrix products, arithmetic and copies ran while one was open for 0% of the time, Pallas kernels for 0%

profile of v4, /device:TPU:1, one launch (start us, length us, event | category | flops | bytes accessed | tf_op | source)
XLA Modules:
  0.0 375.6 jit_solution(14665092784821815358)
XLA Ops:
  6.6 0.8 neg.12
  7.4 0.8 multiply_bitcast_fusion
  8.7 1.3 reshape.145
  10.7 1.8 while.17
  10.7 0.7 bitcast_dynamic-update-slice_fusion.2
  11.6 0.7 bitcast_dynamic-update-slice_fusion.2
  12.6 0.7 pad_maximum_fusion.x_ref
  13.3 40.7 %shard_map.145 = f32[8,72,128]{2,1,0:T(8,128)} custom-call(f32[8,72,128]{2,1,0:T(8,128)} %pad_maximum_fusion.x_ref), custom_call_target="tpu_custom_call" | custom-call | tf_op jit(solution)/shard_map/pallas_call | solution.py:122
  54.0 0.9 exponential_reduce_fusion
  55.0 1.1 multiply_add_fusion
  56.8 1.3 fusion.10
  58.9 0.8 copy.34
  59.7 16.7 %shard_map.146 = bf16[16,16,512]{2,1,0:T(8,128)(2,1)} custom-call(bf16[16,16,512]{2,1,0:T(8,128)(2,1)} %bitcast.85), custom_call_target="tpu_custom_call" | custom-call | tf_op jit(solution)/shard_map/pallas_call | solution.py:48
  76.4 1.0 convert_bitcast_fusion
  77.4 1.1 fusion.29
  79.2 1.0 reshape.128
  80.6 1.4 convolution_convert_fusion.1
  82.0 1.9 reshape.129.x_ref
  83.9 25.1 %shard_map.147 = bf16[16,16,1536]{2,1,0:T(8,128)(2,1)} custom-call(bf16[16,16,1536]{2,1,0:T(8,128)(2,1)} %reshape.129.x_ref), custom_call_target="tpu_custom_call" | custom-call | tf_op jit(solution)/shard_map/pallas_call | solution.py:48
  109.0 3.1 reshape.130
  112.4 93.3 %all-gather.2.cloned.1.call-done = bf16[768,8192]{1,0:T(8,128)(2,1)} async-done(((bf16[48,8192]{1,0:T(8,128)(2,1)}), bf16[768,8192]{1,0:T(8,128)(2,1)}) %all-gather.2.cloned.1.call-update) | async-done | bytes 12582928 | tf_op jit(solution)/shard_map/all_gather | solution.py:227
  205.7 7.0 %fusion.7 = f32[768,128]{1,0:T(8,128)S(1)} fusion(bf16[768,8192]{1,0:T(8,128)(2,1)} %all-gather.2.cloned.1.call-done, bf16[1,8192,128]{2,1,0:T(8,128)(2,1)} %param.29), kind=kOutput, calls=%fused_computation.14 | convolution fusion | flops 1610612736 | bytes 15073280 | tf_op jit(solution)/shard_map/dot_general | solution.py:228
  212.7 19.4 %convolution_convert_fusion = bf16[768,8192]{1,0:T(8,128)(2,1)} fusion(bf16[1,128,8192]{2,1,0:T(8,128)(2,1)S(1)} %copy-done, bf16[768,8192]{1,0:T(8,128)(2,1)} %all-gather.2.cloned.1.call-done, bf16[1,8192,128]{2,1,0:T(8,128)(2,1)} %param.30, f32[768,128]{1,0:T(8,128)S(1)} %fusion.7), kind=kOutput, calls=%fused_computation.9 | convolution fusion | flops 3228106752 | bytes 29753344 | tf_op jit(solution)/shard_map/dot_general | solution.py:231
  232.3 0.5 copy-done.7
  232.9 98.3 %reduce-scatter.2.cloned.1.call-done = bf16[48,8192]{1,0:T(8,128)(2,1)} async-done(((bf16[768,8192]{1,0:T(8,128)(2,1)}), bf16[48,8192]{1,0:T(8,128)(2,1)}) %reduce-scatter.2.cloned.1.call-update) | async-done | bytes 786448 | tf_op jit(solution)/shard_map/reduce_scatter | solution.py:232
  331.1 3.0 reshape.131.x_ref
  334.2 26.9 %shard_map.148 = bf16[16,16,1536]{2,1,0:T(8,128)(2,1)} custom-call(bf16[16,16,1536]{2,1,0:T(8,128)(2,1)} %reshape.131.x_ref), custom_call_target="tpu_custom_call" | custom-call | tf_op jit(solution)/shard_map/pallas_call | solution.py:48
  361.0 2.2 reshape.132
  363.2 1.7 gather_fusion
  364.9 1.7 reshape.134
  366.6 1.4 multiply_reduce_fusion
  368.0 0.8 fusion.32
  (64 shorter events, 4.6 us)
Async XLA Ops:
  6.5 206.2 %copy-start = (bf16[1,128,8192]{2,1,0:T(8,128)(2,1)S(1)}, bf16[1,128,8192]{2,1,0:T(8,128)(2,1)}, u32[]{:S(2)}) copy-start(bf16[1,128,8192]{2,1,0:T(8,128)(2,1)} %param.31) | copy-start | bytes 6291460
  6.5 3.8 %copy-start.4 = (bf16[256,128]{1,0:T(8,128)(2,1)S(1)}, bf16[256,128]{1,0:T(8,128)(2,1)}, u32[]{:S(2)}) copy-start(bf16[256,128]{1,0:T(8,128)(2,1)} %param.19) | copy-start | bytes 196612
  6.5 199.1 %all-gather.2.cloned.1.call-start = ((), (), s32[]{:S(2)}) async-start(), calls=%async_computation.1 | async-start | bytes 13369344 | tf_op jit(solution)/shard_map/all_gather | solution.py:227
  12.5 43.6 %copy-start.3 = (bf16[256,128]{1,0:T(8,128)(2,1)S(1)}, bf16[256,128]{1,0:T(8,128)(2,1)}, u32[]{:S(2)}) copy-start(bf16[256,128]{1,0:T(8,128)(2,1)} %param.20) | copy-start | bytes 196612
  12.5 43.8 %copy-start.1 = (f32[2,8,64,128]{3,2,1,0:T(8,128)S(1)}, f32[2,8,64,128]{3,2,1,0:T(8,128)}, u32[]{:S(2)}) copy-start(f32[2,8,64,128]{3,2,1,0:T(8,128)} %get-tuple-element.45) | copy-start | bytes 1572868
  12.5 44.3 %copy-start.8 = (f32[8]{0:T(128)S(1)}, f32[8]{0:T(128)}, u32[]{:S(2)}) copy-start(f32[8]{0:T(128)} %param.23) | copy-start | bytes 100
  56.3 2.2 copy-start.2
  58.8 19.8 %copy-start.5 = (f32[8192]{0:T(1024)S(1)}, f32[8192]{0:T(1024)}, u32[]{:S(2)}) copy-start(f32[8192]{0:T(1024)} %param.26) | copy-start | bytes 98308
  77.4 2.8 copy-start.6
  112.2 219.0 %reduce-scatter.2.cloned.1.call-start = ((), (), s32[]{:S(2)}) async-start(), calls=%async_computation.2 | async-start | bytes 13369344 | tf_op jit(solution)/shard_map/reduce_scatter | solution.py:232
  232.1 0.7 copy-start.7
Sparse Core Ops, SparseCore 0:
  112.3 93.3 all-gather.1
  232.2 98.8 reduce-scatter.1

commit v5 on v4

--- a/solution.py
+++ b/solution.py
@@ -57,6 +57,31 @@
         ],
         compiler_params=pltpu.CompilerParams(collective_id=collective, has_side_effects=True),
     )(x)
+
+
+def down_body(a_ref, w_ref, o_ref):
+    o_ref[...] = jnp.dot(a_ref[...], w_ref[...], preferred_element_type=jnp.float32).astype(o_ref.dtype)
+
+
+def down_project(active, weight):
+    rows, inner = active.shape
+    width = weight.shape[1]
+    columns = 1024
+    return pl.pallas_call(
+        down_body,
+        grid=(width // columns,),
+        in_specs=[
+            pl.BlockSpec((rows, inner), lambda j: (0, 0)),
+            pl.BlockSpec((inner, columns), lambda j: (0, j)),
+        ],
+        out_specs=pl.BlockSpec((rows, columns), lambda j: (0, j)),
+        out_shape=jax.ShapeDtypeStruct((rows, width), jnp.bfloat16),
+        cost_estimate=pl.CostEstimate(
+            flops=2 * rows * inner * width,
+            transcendentals=0,
+            bytes_accessed=2 * (rows * inner + inner * width + rows * width),
+        ),
+    )(active, weight)
 
 
 def scan_rounds(devices):
@@ -228,8 +253,8 @@
     gate_proj = jnp.dot(segment, w_gate[0], preferred_element_type=jnp.float32)
     up_proj = jnp.dot(segment, w_up[0], preferred_element_type=jnp.float32)
     active = (jax.nn.silu(gate_proj) * up_proj).astype(jnp.bfloat16)
-    partial_value = jnp.dot(active, w_down[0], preferred_element_type=jnp.float32)
-    summed = lax.psum_scatter(partial_value.astype(jnp.bfloat16), "seq", scatter_dimension=0, tiled=True)
+    partial_value = down_project(active, w_down[0])
+    summed = lax.psum_scatter(partial_value, "seq", scatter_dimension=0, tiled=True)
     returned = exchange(summed.reshape(experts, 16, block), 2)
     results = returned.reshape(experts * capacity, width)
     picked = results[target].astype(jnp.float32).reshape(rows_here, 2, width)

time: 376 us -> 371 us (0.987)
  matrix products: 30.1 us -> 15.5 us
  Pallas kernels: 109 us -> 118 us
    dot_general x1, matrix products: 19.4 us -> 4.08 us  [on_device(): up_proj = jnp.dot(segment, w_up[0], preferred_element_type=jnp.float32)]
    pallas_call x0 -> x1, Pallas kernels: none -> 9.06 us  [down_project(): pl.pallas_call(down_body, grid=(width // columns,), in_specs=[pl.BlockSpe...]
where the time goes in v5:
time: 371 us
  waiting for transfers between devices  192 us (52%)
  Pallas kernels  118 us (32%)
  local copies, waits for them, and re-layouts  21.3 us (6%)
  matrix products  15.5 us (4%)
  between operations  13.7 us (4%)
  other arithmetic  9.39 us (3%)
    reduce_scatter x1, waiting for transfers between devices, on_device(): lax.psum_scatter(partial_value, 'seq', scatter_dimension=0, tiled=True)  98.7 us
    all_gather x1, waiting for transfers between devices, on_device(): segment = lax.all_gather(arrived, 'seq', axis=0, tiled=True)  93.3 us
    pallas_call x3, Pallas kernels, exchange(): pl.pallas_call(exchange_body, out_shape=jax.ShapeDtypeStruct(x.shape, x.d...  68.6 us
    pallas_call x1, Pallas kernels, exclusive_scan(): pl.pallas_call(functools.partial(scan_body, devices, state_rows), out_sha...  40.7 us
    pallas_call x1, Pallas kernels, down_project(): pl.pallas_call(down_body, grid=(width // columns,), in_specs=[pl.BlockSpe...  9.06 us
    dot_general x1, matrix products, on_device(): gate_proj = jnp.dot(segment, w_gate[0], preferred_element_type=jnp.float32)  7.69 us
  transfers between devices with their start and end apart: 2, of which 2 were waited for; matrix products, arithmetic and copies ran while one was open for 0% of the time, Pallas kernels for 0%

profile of v5, /device:TPU:1, one launch (start us, length us, event | category | flops | bytes accessed | tf_op | source)
XLA Modules:
  0.0 370.6 jit_solution(12354664145908227082)
XLA Ops:
  6.6 0.8 neg.12
  7.4 0.8 multiply_bitcast_fusion
  8.7 1.3 reshape.145
  10.7 1.8 while.17
  10.7 0.7 bitcast_dynamic-update-slice_fusion.2
  11.6 0.7 bitcast_dynamic-update-slice_fusion.2
  12.6 0.7 pad_maximum_fusion.x_ref
  13.3 40.7 %shard_map.145 = f32[8,72,128]{2,1,0:T(8,128)} custom-call(f32[8,72,128]{2,1,0:T(8,128)} %pad_maximum_fusion.x_ref), custom_call_target="tpu_custom_call" | custom-call | tf_op jit(solution)/shard_map/pallas_call | solution.py:147
  54.0 0.9 exponential_reduce_fusion
  55.0 1.1 multiply_add_fusion
  56.8 1.3 fusion.9
  58.9 0.8 copy.34
  59.7 16.7 %shard_map.146 = bf16[16,16,512]{2,1,0:T(8,128)(2,1)} custom-call(bf16[16,16,512]{2,1,0:T(8,128)(2,1)} %bitcast.82), custom_call_target="tpu_custom_call" | custom-call | tf_op jit(solution)/shard_map/pallas_call | solution.py:48
  76.4 1.0 convert_bitcast_fusion
  78.2 1.0 reshape.128
  79.7 1.4 convolution_convert_fusion
  81.1 1.9 reshape.129.x_ref
  83.0 25.1 %shard_map.147 = bf16[16,16,1536]{2,1,0:T(8,128)(2,1)} custom-call(bf16[16,16,1536]{2,1,0:T(8,128)(2,1)} %reshape.129.x_ref), custom_call_target="tpu_custom_call" | custom-call | tf_op jit(solution)/shard_map/pallas_call | solution.py:48
  108.1 3.1 reshape.130
  111.4 93.3 %all-gather.2.cloned.1.call-done = bf16[768,8192]{1,0:T(8,128)(2,1)} async-done(((bf16[48,8192]{1,0:T(8,128)(2,1)}), bf16[768,8192]{1,0:T(8,128)(2,1)}) %all-gather.2.cloned.1.call-update) | async-done | bytes 12582928 | tf_op jit(solution)/shard_map/all_gather | solution.py:252
  204.8 7.7 %fusion.6 = f32[768,128]{1,0:T(8,128)S(1)} fusion(bf16[768,8192]{1,0:T(8,128)(2,1)} %all-gather.2.cloned.1.call-done, bf16[1,8192,128]{2,1,0:T(8,128)(2,1)S(1)} %copy-done), kind=kOutput, calls=%fused_computation.12 | convolution fusion | flops 1610612736 | bytes 15073280 | tf_op jit(solution)/shard_map/dot_general | solution.py:253
  212.9 0.6 copy-done.10
  213.5 4.1 %fusion.14.a_ref = bf16[768,128]{1,0:T(8,128)(2,1)} fusion(bf16[768,8192]{1,0:T(8,128)(2,1)S(1)} %copy-done.9, bf16[1,8192,128]{2,1,0:T(8,128)(2,1)S(1)} %copy-done.10, f32[768,128]{1,0:T(8,128)S(1)} %fusion.6), kind=kOutput, calls=%fused_computation.20 | convolution fusion | flops 1611202560 | bytes 15269888 | tf_op jit(solution)/shard_map/dot_general | solution.py:254
  217.6 9.1 %shard_map.148 = bf16[768,8192]{1,0:T(8,128)(2,1)} custom-call(bf16[768,128]{1,0:T(8,128)(2,1)} %fusion.14.a_ref, bf16[128,8192]{1,0:T(8,128)(2,1)} %bitcast.79), custom_call_target="tpu_custom_call" | custom-call | flops 1610612736 | bytes 14876672 | tf_op jit(solution)/shard_map/pallas_call | solution.py:70
  227.4 98.7 %reduce-scatter.2.cloned.1.call-done = bf16[48,8192]{1,0:T(8,128)(2,1)} async-done(((bf16[768,8192]{1,0:T(8,128)(2,1)}), bf16[48,8192]{1,0:T(8,128)(2,1)}) %reduce-scatter.2.cloned.1.call-update) | async-done | bytes 786448 | tf_op jit(solution)/shard_map/reduce_scatter | solution.py:257
  326.2 3.0 reshape.131.x_ref
  329.2 26.9 %shard_map.149 = bf16[16,16,1536]{2,1,0:T(8,128)(2,1)} custom-call(bf16[16,16,1536]{2,1,0:T(8,128)(2,1)} %reshape.131.x_ref), custom_call_target="tpu_custom_call" | custom-call | tf_op jit(solution)/shard_map/pallas_call | solution.py:48
  356.0 2.2 reshape.132
  358.2 1.7 gather_fusion
  359.9 1.7 reshape.134
  361.6 1.4 multiply_reduce_fusion
  363.0 0.8 fusion.29
  (71 shorter events, 5.8 us)
Async XLA Ops:
  6.5 198.2 %copy-start = (bf16[1,8192,128]{2,1,0:T(8,128)(2,1)S(1)}, bf16[1,8192,128]{2,1,0:T(8,128)(2,1)}, u32[]{:S(2)}) copy-start(bf16[1,8192,128]{2,1,0:T(8,128)(2,1)} %param.29) | copy-start | bytes 6291460
  6.5 3.8 %copy-start.5 = (bf16[256,128]{1,0:T(8,128)(2,1)S(1)}, bf16[256,128]{1,0:T(8,128)(2,1)}, u32[]{:S(2)}) copy-start(bf16[256,128]{1,0:T(8,128)(2,1)} %param.19) | copy-start | bytes 196612
  6.5 198.2 %all-gather.2.cloned.1.call-start = ((), (), s32[]{:S(2)}) async-start(), calls=%async_computation.1 | async-start | bytes 13369344 | tf_op jit(solution)/shard_map/all_gather | solution.py:252
  12.5 43.7 %copy-start.3 = (bf16[256,128]{1,0:T(8,128)(2,1)S(1)}, bf16[256,128]{1,0:T(8,128)(2,1)}, u32[]{:S(2)}) copy-start(bf16[256,128]{1,0:T(8,128)(2,1)} %param.20) | copy-start | bytes 196612
  12.5 43.8 %copy-start.1 = (f32[2,8,64,128]{3,2,1,0:T(8,128)S(1)}, f32[2,8,64,128]{3,2,1,0:T(8,128)}, u32[]{:S(2)}) copy-start(f32[2,8,64,128]{3,2,1,0:T(8,128)} %get-tuple-element.45) | copy-start | bytes 1572868
  12.5 44.3 %copy-start.11 = (f32[8]{0:T(128)S(1)}, f32[8]{0:T(128)}, u32[]{:S(2)}) copy-start(f32[8]{0:T(128)} %param.23) | copy-start | bytes 100
  56.3 2.2 copy-start.2
  58.7 18.8 %copy-start.4 = (bf16[16,8192]{1,0:T(8,128)(2,1)S(1)}, bf16[16,8192]{1,0:T(8,128)(2,1)}, u32[]{:S(2)}) copy-start(bf16[16,8192]{1,0:T(8,128)(2,1)} %param.25) | copy-start | bytes 786436
  58.9 18.8 %copy-start.6 = (f32[8192]{0:T(1024)S(1)}, f32[8192]{0:T(1024)}, u32[]{:S(2)}) copy-start(f32[8192]{0:T(1024)} %param.26) | copy-start | bytes 98308
  77.4 1.8 copy-start.7
  111.2 214.9 %reduce-scatter.2.cloned.1.call-start = ((), (), s32[]{:S(2)}) async-start(), calls=%async_computation.2 | async-start | bytes 13369344 | tf_op jit(solution)/shard_map/reduce_scatter | solution.py:257
  204.8 8.2 %copy-start.9 = (bf16[768,8192]{1,0:T(8,128)(2,1)S(1)}, bf16[768,8192]{1,0:T(8,128)(2,1)}, u32[]{:S(2)}) copy-start(bf16[768,8192]{1,0:T(8,128)(2,1)} %all-gather.2.cloned.1.call-done) | copy-start | bytes 37748740
  204.8 8.8 %copy-start.10 = (bf16[1,8192,128]{2,1,0:T(8,128)(2,1)S(1)}, bf16[1,8192,128]{2,1,0:T(8,128)(2,1)}, u32[]{:S(2)}) copy-start(bf16[1,8192,128]{2,1,0:T(8,128)(2,1)} %param.30) | copy-start | bytes 6291460
  226.7 0.7 copy-start.8
Sparse Core Ops, SparseCore 0:
  111.3 93.3 all-gather.1
  226.8 99.2 reduce-scatter.1

commit v6 on v4

--- a/solution.py
+++ b/solution.py
@@ -57,6 +57,62 @@
         ],
         compiler_params=pltpu.CompilerParams(collective_id=collective, has_side_effects=True),
     )(x)
+
+
+def expert_body(depth_steps, seg_ref, gate_ref, up_ref, down_ref, o_ref, gate_acc, up_acc, active):
+    step = pl.program_id(0)
+
+    @pl.when(step == 0)
+    def _():
+        gate_acc[...] = jnp.zeros_like(gate_acc)
+        up_acc[...] = jnp.zeros_like(up_acc)
+
+    @pl.when(step < depth_steps)
+    def _():
+        rows = seg_ref[...]
+        gate_acc[...] += jnp.dot(rows, gate_ref[...], preferred_element_type=jnp.float32)
+        up_acc[...] += jnp.dot(rows, up_ref[...], preferred_element_type=jnp.float32)
+
+    @pl.when(step == depth_steps - 1)
+    def _():
+        gate = gate_acc[...]
+        active[...] = (gate / (1.0 + jnp.exp(-gate)) * up_acc[...]).astype(active.dtype)
+
+    @pl.when(step >= depth_steps)
+    def _():
+        o_ref[...] = jnp.dot(
+            active[...], down_ref[...], preferred_element_type=jnp.float32
+        ).astype(o_ref.dtype)
+
+
+def expert_mlp(segment, gate_w, up_w, down_w):
+    rows, width = segment.shape
+    hidden = gate_w.shape[1]
+    block = 1024
+    depth_steps = width // block
+    column_steps = width // block
+    return pl.pallas_call(
+        functools.partial(expert_body, depth_steps),
+        grid=(depth_steps + column_steps,),
+        in_specs=[
+            pl.BlockSpec((rows, block), lambda i: (0, jnp.minimum(i, depth_steps - 1))),
+            pl.BlockSpec((block, hidden), lambda i: (jnp.minimum(i, depth_steps - 1), 0)),
+            pl.BlockSpec((block, hidden), lambda i: (jnp.minimum(i, depth_steps - 1), 0)),
+            pl.BlockSpec((hidden, block), lambda i: (0, jnp.maximum(i - depth_steps, 0))),
+        ],
+        out_specs=pl.BlockSpec((rows, block), lambda i: (0, jnp.maximum(i - depth_steps, 0))),
+        out_shape=jax.ShapeDtypeStruct((rows, width), jnp.bfloat16),
+        scratch_shapes=[
+            pltpu.VMEM((rows, hidden), jnp.float32),
+            pltpu.VMEM((rows, hidden), jnp.float32),
+            pltpu.VMEM((rows, hidden), jnp.bfloat16),
+        ],
+        cost_estimate=pl.CostEstimate(
+            flops=6 * rows * width * hidden,
+            transcendentals=rows * hidden,
+            bytes_accessed=2 * (2 * rows * width + 3 * width * hidden),
+        ),
+    )(segment, gate_w, up_w, down_w)
 
 
 def scan_rounds(devices):
@@ -225,11 +281,8 @@
     arrived = exchange(outgoing.reshape(experts, 16, block), 1)
     arrived = arrived.reshape(capacity * experts, width)
     segment = lax.all_gather(arrived, "seq", axis=0, tiled=True)
-    gate_proj = jnp.dot(segment, w_gate[0], preferred_element_type=jnp.float32)
-    up_proj = jnp.dot(segment, w_up[0], preferred_element_type=jnp.float32)
-    active = (jax.nn.silu(gate_proj) * up_proj).astype(jnp.bfloat16)
-    partial_value = jnp.dot(active, w_down[0], preferred_element_type=jnp.float32)
-    summed = lax.psum_scatter(partial_value.astype(jnp.bfloat16), "seq", scatter_dimension=0, tiled=True)
+    partial_value = expert_mlp(segment, w_gate[0], w_up[0], w_down[0])
+    summed = lax.psum_scatter(partial_value, "seq", scatter_dimension=0, tiled=True)
     returned = exchange(summed.reshape(experts, 16, block), 2)
     results = returned.reshape(experts * capacity, width)
     picked = results[target].astype(jnp.float32).reshape(rows_here, 2, width)

time: 376 us -> 364 us (0.968)
  matrix products: 30.1 us -> 2.67 us
  Pallas kernels: 109 us -> 129 us
    dot_general x2 -> x0, matrix products: 26.4 us -> none  [the longest x1 19.4 us: on_device(): jnp.dot(active, w_down[0], preferred_element_type=jnp.float32)]
    pallas_call x0 -> x1, Pallas kernels: none -> 20.1 us  [expert_mlp(): pl.pallas_call(functools.partial(expert_body, depth_steps), grid=(depth_s...]
where the time goes in v6:
time: 364 us; the launch traced here: 363 us
  waiting for transfers between devices  192 us (53%)
  Pallas kernels  129 us (35%)
  local copies, waits for them, and re-layouts  17.7 us (5%)
  between operations  13.7 us (4%)
  other arithmetic  7.83 us (2%)
    reduce_scatter x1, waiting for transfers between devices, on_device(): lax.psum_scatter(partial_value, 'seq', scatter_dimension=0, tiled=True)  98.4 us
    all_gather x1, waiting for transfers between devices, on_device(): segment = lax.all_gather(arrived, 'seq', axis=0, tiled=True)  93.3 us
    pallas_call x3, Pallas kernels, exchange(): pl.pallas_call(exchange_body, out_shape=jax.ShapeDtypeStruct(x.shape, x.d...  68.6 us
    pallas_call x1, Pallas kernels, exclusive_scan(): pl.pallas_call(functools.partial(scan_body, devices, state_rows), out_sha...  40.7 us
    pallas_call x1, Pallas kernels, expert_mlp(): pl.pallas_call(functools.partial(expert_body, depth_steps), grid=(depth_s...  20.1 us
  transfers between devices with their start and end apart: 2, of which 2 were waited for; matrix products, arithmetic and copies ran while one was open for 0% of the time, Pallas kernels for 0%

profile of v6, /device:TPU:1, one launch (start us, length us, event | category | flops | bytes accessed | tf_op | source)
XLA Modules:
  0.0 363.3 jit_solution(17242358040410530177)
XLA Ops:
  6.5 0.7 neg.8
  7.2 0.8 multiply_bitcast_fusion
  8.5 1.3 reshape.145
  9.8 0.3 copy.28
  10.2 0.4 fusion.11
  10.6 0.4 while.17
  11.1 0.7 pad_maximum_fusion.x_ref
  11.8 40.7 %shard_map.145 = f32[8,72,128]{2,1,0:T(8,128)} custom-call(f32[8,72,128]{2,1,0:T(8,128)} %pad_maximum_fusion.x_ref), custom_call_target="tpu_custom_call" | custom-call | tf_op jit(solution)/shard_map/pallas_call | solution.py:178
  52.5 0.9 exponential_reduce_fusion
  53.5 1.1 multiply_add_fusion
  54.7 0.5 fusion.6
  55.2 1.3 fusion.5
  56.5 0.4 copy.32
  57.3 0.8 copy.34
  58.1 16.7 %shard_map.146 = bf16[16,16,512]{2,1,0:T(8,128)(2,1)} custom-call(bf16[16,16,512]{2,1,0:T(8,128)(2,1)} %bitcast.76), custom_call_target="tpu_custom_call" | custom-call | tf_op jit(solution)/shard_map/pallas_call | solution.py:48
  74.8 1.0 convert_bitcast_fusion
  76.3 0.4 broadcast_in_dim.34
  77.4 0.3 convolution_convert_fusion
  77.7 1.9 reshape.129.x_ref
  79.6 25.1 %shard_map.147 = bf16[16,16,1536]{2,1,0:T(8,128)(2,1)} custom-call(bf16[16,16,1536]{2,1,0:T(8,128)(2,1)} %reshape.129.x_ref), custom_call_target="tpu_custom_call" | custom-call | tf_op jit(solution)/shard_map/pallas_call | solution.py:48
  104.7 3.1 reshape.130
  108.1 93.3 %all-gather.2.cloned.1.call-done.seg_ref = bf16[768,8192]{1,0:T(8,128)(2,1)} async-done(((bf16[48,8192]{1,0:T(8,128)(2,1)}), bf16[768,8192]{1,0:T(8,128)(2,1)}) %all-gather.2.cloned.1.call-update) | async-done | bytes 12582928 | tf_op jit(solution)/shard_map/all_gather | solution.py:283
  201.4 20.1 %shard_map.148 = bf16[768,8192]{1,0:T(8,128)(2,1)} custom-call(bf16[768,8192]{1,0:T(8,128)(2,1)} %all-gather.2.cloned.1.call-done.seg_ref, bf16[8192,128]{1,0:T(8,128)(2,1)} %bitcast.73, bf16[8192,128]{1,0:T(8,128)(2,1)} %bitcast.74, bf16[128,8192]{1,0:T(8,128)(2,1)} %bitcast.75), custom_call_target="tpu_custom_call" | custom-call | flops 4831838208 | bytes 31457280 | tf_op jit(solution)/shard_map/pallas_call | solution.py:94
  221.7 0.5 copy-done.7
  222.3 98.4 %reduce-scatter.2.cloned.1.call-done = bf16[48,8192]{1,0:T(8,128)(2,1)} async-done(((bf16[768,8192]{1,0:T(8,128)(2,1)}), bf16[48,8192]{1,0:T(8,128)(2,1)}) %reduce-scatter.2.cloned.1.call-update) | async-done | bytes 786448 | tf_op jit(solution)/shard_map/reduce_scatter | solution.py:285
  320.7 3.0 reshape.131.x_ref
  323.7 26.8 %shard_map.149 = bf16[16,16,1536]{2,1,0:T(8,128)(2,1)} custom-call(bf16[16,16,1536]{2,1,0:T(8,128)(2,1)} %reshape.131.x_ref), custom_call_target="tpu_custom_call" | custom-call | tf_op jit(solution)/shard_map/pallas_call | solution.py:48
  350.6 2.2 reshape.132
  352.8 0.9 gather_fusion
  353.7 0.7 reshape.134
  354.3 1.4 multiply_reduce_fusion
  355.7 0.8 fusion.19
  (63 shorter events, 3.1 us)
Async XLA Ops:
  6.5 3.6 copy-start
  6.5 194.8 %all-gather.2.cloned.1.call-start = ((), (), s32[]{:S(2)}) async-start(), calls=%async_computation.1 | async-start | bytes 13369344 | tf_op jit(solution)/shard_map/all_gather | solution.py:283
  10.6 42.9 %copy-start.3 = (f32[8,64,128]{2,1,0:T(8,128)S(1)}, f32[8,64,128]{2,1,0:T(8,128)}, u32[]{:S(2)}) copy-start(f32[8,64,128]{2,1,0:T(8,128)} %param.24) | copy-start | bytes 786436
  11.0 43.6 %copy-start.2 = (bf16[256,128]{1,0:T(8,128)(2,1)S(1)}, bf16[256,128]{1,0:T(8,128)(2,1)}, u32[]{:S(2)}) copy-start(bf16[256,128]{1,0:T(8,128)(2,1)} %param.20) | copy-start | bytes 196612
  11.0 44.2 %copy-start.8 = (f32[8]{0:T(128)S(1)}, f32[8]{0:T(128)}, u32[]{:S(2)}) copy-start(f32[8]{0:T(128)} %param.23) | copy-start | bytes 100
  54.7 2.2 copy-start.1
  57.1 18.8 %copy-start.4 = (bf16[16,8192]{1,0:T(8,128)(2,1)S(1)}, bf16[16,8192]{1,0:T(8,128)(2,1)}, u32[]{:S(2)}) copy-start(bf16[16,8192]{1,0:T(8,128)(2,1)} %param.25) | copy-start | bytes 786436
  57.3 18.8 %copy-start.5 = (f32[8192]{0:T(1024)S(1)}, f32[8192]{0:T(1024)}, u32[]{:S(2)}) copy-start(f32[8192]{0:T(1024)} %param.26) | copy-start | bytes 98308
  75.8 1.1 copy-start.6
  107.9 212.8 %reduce-scatter.2.cloned.1.call-start = ((), (), s32[]{:S(2)}) async-start(), calls=%async_computation.2 | async-start | bytes 13369344 | tf_op jit(solution)/shard_map/reduce_scatter | solution.py:285
  221.5 0.7 copy-start.7
Sparse Core Ops, SparseCore 0:
  108.0 93.3 all-gather.1
  221.7 98.9 reduce-scatter.1

commit v7 on v6

--- a/solution.py
+++ b/solution.py
@@ -123,28 +123,35 @@
     return rounds
 
 
-def fold(earlier, later, state_rows):
-    row = lax.broadcasted_iota(jnp.int32, later.shape, 1)
-    decay = jnp.exp(later[:, state_rows:state_rows + 1, :])
-    return jnp.where(row < state_rows, decay, 1.0) * earlier + later
-
-
-def scan_body(devices, state_rows, x_ref, o_ref, inc_ref, recv_ref, send_sem, recv_sem):
+def fold(earlier_state, earlier_log, later_state, later_log):
+    decay = jnp.exp(later_log[:, 0:1, :])
+    return decay * earlier_state + later_state, earlier_log + later_log
+
+
+def scan_body(devices, x_state, x_log, o_state, o_log, inc_state, inc_log, wire, recv, send_sem, recv_sem):
     me = lax.axis_index("seq")
     col = lax.axis_index("exp")
+    rows = x_state.shape[1]
     mesh_id = pl.DeviceIdType.MESH
     barrier = pltpu.get_barrier_semaphore()
     for step in range(1, devices):
         peer = lax.rem(me + step, devices)
         pl.semaphore_signal(barrier, 1, device_id=(peer, col), device_id_type=mesh_id)
     pl.semaphore_wait(barrier, devices - 1)
-    inc_ref[0] = x_ref[...]
-    o_ref[...] = jnp.zeros_like(o_ref)
+    inc_state[0] = x_state[...]
+    inc_log[0] = x_log[...]
+    o_state[...] = jnp.zeros_like(o_state)
+    o_log[...] = jnp.zeros_like(o_log)
     for level, shifts in enumerate(scan_rounds(devices)):
-        def link(slot, shift, peer):
+        log_now = inc_log[level]
+        high = log_now.astype(jnp.bfloat16).astype(jnp.float32)
+        wire[level, :, :rows, :] = inc_state[level].astype(jnp.bfloat16)
+        wire[level, :, rows:, :] = jnp.concatenate([high, log_now - high], axis=1).astype(jnp.bfloat16)
+
+        def link(slot, peer):
             return pltpu.make_async_remote_copy(
-                src_ref=inc_ref.at[level],
-                dst_ref=recv_ref.at[level, slot],
+                src_ref=wire.at[level],
+                dst_ref=recv.at[level, slot],
                 send_sem=send_sem.at[level, slot],
                 recv_sem=recv_sem.at[level, slot],
                 device_id=(peer, col),
@@ -153,42 +160,53 @@
         for slot, shift in enumerate(shifts):
             @pl.when(me + shift < devices)
             def _():
-                link(slot, shift, me + shift).start()
-        inc_ref[level + 1] = inc_ref[level]
+                link(slot, me + shift).start()
+        inc_state[level + 1] = inc_state[level]
+        inc_log[level + 1] = inc_log[level]
         for slot, shift in enumerate(shifts):
             @pl.when(me >= shift)
             def _():
-                link(slot, shift, me - shift).wait_recv()
-                got = recv_ref[level, slot]
-                inc_ref[level + 1] = fold(got, inc_ref[level + 1], state_rows)
-                o_ref[...] = fold(got, o_ref[...], state_rows)
+                link(slot, me - shift).wait_recv()
+                got_state = recv[level, slot, :, :rows, :].astype(jnp.float32)
+                parts = recv[level, slot, :, rows:, :].astype(jnp.float32)
+                got_log = parts[:, :8, :] + parts[:, 8:, :]
+                new_state, new_log = fold(got_state, got_log, inc_state[level + 1], inc_log[level + 1])
+                inc_state[level + 1] = new_state
+                inc_log[level + 1] = new_log
+                new_state, new_log = fold(got_state, got_log, o_state[...], o_log[...])
+                o_state[...] = new_state
+                o_log[...] = new_log
         for slot, shift in enumerate(shifts):
             @pl.when(me + shift < devices)
             def _():
-                link(slot, shift, me + shift).wait_send()
+                link(slot, me + shift).wait_send()
 
 
 def exclusive_scan(log, state, axis):
     devices = lax.axis_size(axis)
     heads, state_rows, lanes = state.shape
-    packed = jnp.concatenate(
-        [state, jnp.broadcast_to(log[:, None, None], (heads, 8, lanes))], axis=1
-    )
+    log_rows = jnp.broadcast_to(log[:, None, None], (heads, 8, lanes))
     levels = len(scan_rounds(devices))
-    result = pl.pallas_call(
-        functools.partial(scan_body, devices, state_rows),
-        out_shape=jax.ShapeDtypeStruct(packed.shape, packed.dtype),
-        in_specs=[pl.BlockSpec(memory_space=pltpu.VMEM)],
-        out_specs=pl.BlockSpec(memory_space=pltpu.VMEM),
+    wire_shape = (heads, state_rows + 16, lanes)
+    prior_state, prior_log = pl.pallas_call(
+        functools.partial(scan_body, devices),
+        out_shape=(
+            jax.ShapeDtypeStruct(state.shape, jnp.float32),
+            jax.ShapeDtypeStruct(log_rows.shape, jnp.float32),
+        ),
+        in_specs=[pl.BlockSpec(memory_space=pltpu.VMEM)] * 2,
+        out_specs=(pl.BlockSpec(memory_space=pltpu.VMEM),) * 2,
         scratch_shapes=[
-            pltpu.VMEM((levels + 1,) + packed.shape, packed.dtype),
-            pltpu.VMEM((levels, 3) + packed.shape, packed.dtype),
+            pltpu.VMEM((levels + 1,) + state.shape, jnp.float32),
+            pltpu.VMEM((levels + 1,) + log_rows.shape, jnp.float32),
+            pltpu.VMEM((levels,) + wire_shape, jnp.bfloat16),
+            pltpu.VMEM((levels, 3) + wire_shape, jnp.bfloat16),
             pltpu.SemaphoreType.DMA((levels, 3)),
             pltpu.SemaphoreType.DMA((levels, 3)),
         ],
         compiler_params=pltpu.CompilerParams(collective_id=3, has_side_effects=True),
-    )(packed)
-    return result[:, state_rows, 0], result[:, :state_rows, :]
+    )(state, log_rows)
+    return prior_log[:, 0, 0], prior_state
 
 
 def chain_combine(earlier, later):

time: 364 us -> 350 us (0.962)
  Pallas kernels: 129 us -> 115 us
    pallas_call x1, Pallas kernels: 40.7 us -> 26.4 us  [exclusive_scan(): pl.pallas_call(functools.partial(scan_body, devices), out_shape=(jax.Shap...]
where the time goes in v7:
time: 350 us; the launch traced here: 349 us
  waiting for transfers between devices  192 us (55%)
  Pallas kernels  115 us (33%)
  local copies, waits for them, and re-layouts  18.3 us (5%)
  between operations  13.7 us (4%)
  other arithmetic  7.08 us (2%)
    reduce_scatter x1, waiting for transfers between devices, on_device(): lax.psum_scatter(partial_value, 'seq', scatter_dimension=0, tiled=True)  98.4 us
    all_gather x1, waiting for transfers between devices, on_device(): segment = lax.all_gather(arrived, 'seq', axis=0, tiled=True)  93.6 us
    pallas_call x3, Pallas kernels, exchange(): pl.pallas_call(exchange_body, out_shape=jax.ShapeDtypeStruct(x.shape, x.d...  68.5 us
    pallas_call x1, Pallas kernels, exclusive_scan(): pl.pallas_call(functools.partial(scan_body, devices), out_shape=(jax.Shap...  26.4 us
    pallas_call x1, Pallas kernels, expert_mlp(): pl.pallas_call(functools.partial(expert_body, depth_steps), grid=(depth_s...  20.1 us
  transfers between devices with their start and end apart: 2, of which 2 were waited for; matrix products, arithmetic and copies ran while one was open for 0% of the time, Pallas kernels for 0%

profile of v7, /device:TPU:1, one launch (start us, length us, event | category | flops | bytes accessed | tf_op | source)
XLA Modules:
  0.0 349.3 jit_solution(4735996659076473303)
XLA Ops:
  6.5 0.7 neg.8
  7.2 0.8 multiply_bitcast_fusion
  8.5 1.3 reshape.145
  9.8 0.3 copy.28
  10.2 0.4 fusion.11
  10.6 0.4 while.17
  11.0 0.7 broadcast_in_dim.33.x_log
  11.7 26.4 %shard_map.145 = (f32[8,64,128]{2,1,0:T(8,128)}, f32[8,8,128]{2,1,0:T(8,128)}) custom-call(f32[8,64,128]{2,1,0:T(8,128)S(1)} %get-tuple-element.49.x_state, f32[8,8,128]{2,1,0:T(8,128)} %broadcast_in_dim.33.x_log), custom_call_target="tpu_custom_call" | custom-call | tf_op jit(solution)/shard_map/pallas_call | solution.py:191
  38.2 0.9 exponential_reduce_fusion
  39.3 1.0 multiply_add_fusion
  40.4 0.5 fusion.6
  40.8 1.3 fusion.5
  42.2 0.4 copy.32
  42.9 0.8 copy.34
  43.8 16.7 %shard_map.146 = bf16[16,16,512]{2,1,0:T(8,128)(2,1)} custom-call(bf16[16,16,512]{2,1,0:T(8,128)(2,1)} %bitcast.76), custom_call_target="tpu_custom_call" | custom-call | tf_op jit(solution)/shard_map/pallas_call | solution.py:48
  60.5 1.0 convert_bitcast_fusion
  61.9 0.4 broadcast_in_dim.34
  63.0 0.3 convolution_convert_fusion
  63.4 1.9 reshape.129.x_ref
  65.3 25.1 %shard_map.147 = bf16[16,16,1536]{2,1,0:T(8,128)(2,1)} custom-call(bf16[16,16,1536]{2,1,0:T(8,128)(2,1)} %reshape.129.x_ref), custom_call_target="tpu_custom_call" | custom-call | tf_op jit(solution)/shard_map/pallas_call | solution.py:48
  90.4 3.1 reshape.130
  93.7 93.6 %all-gather.2.cloned.1.call-done.seg_ref = bf16[768,8192]{1,0:T(8,128)(2,1)} async-done(((bf16[48,8192]{1,0:T(8,128)(2,1)}), bf16[768,8192]{1,0:T(8,128)(2,1)}) %all-gather.2.cloned.1.call-update) | async-done | bytes 12582928 | tf_op jit(solution)/shard_map/all_gather | solution.py:301
  187.3 20.1 %shard_map.148 = bf16[768,8192]{1,0:T(8,128)(2,1)} custom-call(bf16[768,8192]{1,0:T(8,128)(2,1)} %all-gather.2.cloned.1.call-done.seg_ref, bf16[8192,128]{1,0:T(8,128)(2,1)} %bitcast.73, bf16[8192,128]{1,0:T(8,128)(2,1)} %bitcast.74, bf16[128,8192]{1,0:T(8,128)(2,1)} %bitcast.75), custom_call_target="tpu_custom_call" | custom-call | flops 4831838208 | bytes 31457280 | tf_op jit(solution)/shard_map/pallas_call | solution.py:94
  207.7 0.5 copy-done.7
  208.2 98.4 %reduce-scatter.2.cloned.1.call-done = bf16[48,8192]{1,0:T(8,128)(2,1)} async-done(((bf16[768,8192]{1,0:T(8,128)(2,1)}), bf16[48,8192]{1,0:T(8,128)(2,1)}) %reduce-scatter.2.cloned.1.call-update) | async-done | bytes 786448 | tf_op jit(solution)/shard_map/reduce_scatter | solution.py:303
  306.6 3.0 reshape.131.x_ref
  309.7 26.8 %shard_map.149 = bf16[16,16,1536]{2,1,0:T(8,128)(2,1)} custom-call(bf16[16,16,1536]{2,1,0:T(8,128)(2,1)} %reshape.131.x_ref), custom_call_target="tpu_custom_call" | custom-call | tf_op jit(solution)/shard_map/pallas_call | solution.py:48
  336.5 2.2 reshape.132
  338.7 0.9 gather_fusion
  339.6 0.7 reshape.134
  340.2 1.4 multiply_reduce_fusion
  341.6 0.8 fusion.19
  (62 shorter events, 3.1 us)
Async XLA Ops:
  6.5 3.6 %copy-start = (bf16[256,128]{1,0:T(8,128)(2,1)S(1)}, bf16[256,128]{1,0:T(8,128)(2,1)}, u32[]{:S(2)}) copy-start(bf16[256,128]{1,0:T(8,128)(2,1)} %param.19) | copy-start | bytes 196612
  6.5 180.8 %all-gather.2.cloned.1.call-start = ((), (), s32[]{:S(2)}) async-start(), calls=%async_computation.1 | async-start | bytes 13369344 | tf_op jit(solution)/shard_map/all_gather | solution.py:301
  10.6 28.6 %copy-start.2 = (bf16[256,128]{1,0:T(8,128)(2,1)S(1)}, bf16[256,128]{1,0:T(8,128)(2,1)}, u32[]{:S(2)}) copy-start(bf16[256,128]{1,0:T(8,128)(2,1)} %param.20) | copy-start | bytes 196612
  10.6 28.7 %copy-start.3 = (f32[8,64,128]{2,1,0:T(8,128)S(1)}, f32[8,64,128]{2,1,0:T(8,128)}, u32[]{:S(2)}) copy-start(f32[8,64,128]{2,1,0:T(8,128)} %param.24) | copy-start | bytes 786436
  11.0 29.8 %copy-start.8 = (f32[8]{0:T(128)S(1)}, f32[8]{0:T(128)}, u32[]{:S(2)}) copy-start(f32[8]{0:T(128)} %param.23) | copy-start | bytes 100
  40.4 2.2 copy-start.1
  42.7 18.8 %copy-start.4 = (bf16[16,8192]{1,0:T(8,128)(2,1)S(1)}, bf16[16,8192]{1,0:T(8,128)(2,1)}, u32[]{:S(2)}) copy-start(bf16[16,8192]{1,0:T(8,128)(2,1)} %param.25) | copy-start | bytes 786436
  42.9 18.8 %copy-start.5 = (f32[8192]{0:T(1024)S(1)}, f32[8192]{0:T(1024)}, u32[]{:S(2)}) copy-start(f32[8192]{0:T(1024)} %param.26) | copy-start | bytes 98308
  61.5 1.1 copy-start.6
  93.5 213.1 %reduce-scatter.2.cloned.1.call-start = ((), (), s32[]{:S(2)}) async-start(), calls=%async_computation.2 | async-start | bytes 13369344 | tf_op jit(solution)/shard_map/reduce_scatter | solution.py:303
  207.4 0.7 copy-start.7
Sparse Core Ops, SparseCore 0:
  93.6 93.6 all-gather.1
  207.6 99.0 reduce-scatter.1

commit v8 on v7

--- a/solution.py
+++ b/solution.py
@@ -69,9 +69,11 @@
 
     @pl.when(step < depth_steps)
     def _():
-        rows = seg_ref[...]
-        gate_acc[...] += jnp.dot(rows, gate_ref[...], preferred_element_type=jnp.float32)
-        up_acc[...] += jnp.dot(rows, up_ref[...], preferred_element_type=jnp.float32)
+        joined = jnp.concatenate([gate_ref[...], up_ref[...]], axis=1)
+        both = jnp.dot(seg_ref[...], joined, preferred_element_type=jnp.float32)
+        hidden = gate_acc.shape[1]
+        gate_acc[...] += both[:, :hidden]
+        up_acc[...] += both[:, hidden:]
 
     @pl.when(step == depth_steps - 1)
     def _():
@@ -88,7 +90,7 @@
 def expert_mlp(segment, gate_w, up_w, down_w):
     rows, width = segment.shape
     hidden = gate_w.shape[1]
-    block = 1024
+    block = 2048
     depth_steps = width // block
     column_steps = width // block
     return pl.pallas_call(

time: 350 us -> 345 us (0.986)
  Pallas kernels: 115 us -> 110 us
    pallas_call x1, Pallas kernels: 20.1 us -> 14.8 us  [expert_mlp(): pl.pallas_call(functools.partial(expert_body, depth_steps), grid=(depth_s...]
where the time goes in v8:
time: 345 us; the launch traced here: 344 us
  waiting for transfers between devices  192 us (56%)
  Pallas kernels  110 us (32%)
  local copies, waits for them, and re-layouts  18.3 us (5%)
  between operations  13.7 us (4%)
  other arithmetic  7.08 us (2%)
    reduce_scatter x1, waiting for transfers between devices, on_device(): lax.psum_scatter(partial_value, 'seq', scatter_dimension=0, tiled=True)  98.5 us
    all_gather x1, waiting for transfers between devices, on_device(): segment = lax.all_gather(arrived, 'seq', axis=0, tiled=True)  93.6 us
    pallas_call x3, Pallas kernels, exchange(): pl.pallas_call(exchange_body, out_shape=jax.ShapeDtypeStruct(x.shape, x.d...  68.6 us
    pallas_call x1, Pallas kernels, exclusive_scan(): pl.pallas_call(functools.partial(scan_body, devices), out_shape=(jax.Shap...  26.4 us
    pallas_call x1, Pallas kernels, expert_mlp(): pl.pallas_call(functools.partial(expert_body, depth_steps), grid=(depth_s...  14.8 us
  transfers between devices with their start and end apart: 2, of which 2 were waited for; matrix products, arithmetic and copies ran while one was open for 0% of the time, Pallas kernels for 0%

profile of v8, /device:TPU:1, one launch (start us, length us, event | category | flops | bytes accessed | tf_op | source)
XLA Modules:
  0.0 344.1 jit_solution(16818426510238225481)
XLA Ops:
  6.5 0.7 neg.8
  7.2 0.8 multiply_bitcast_fusion
  8.5 1.3 reshape.145
  9.8 0.3 copy.28
  10.2 0.4 fusion.11
  10.6 0.4 while.17
  11.0 0.7 broadcast_in_dim.33.x_log
  11.7 26.4 %shard_map.145 = (f32[8,64,128]{2,1,0:T(8,128)}, f32[8,8,128]{2,1,0:T(8,128)}) custom-call(f32[8,64,128]{2,1,0:T(8,128)S(1)} %get-tuple-element.49.x_state, f32[8,8,128]{2,1,0:T(8,128)} %broadcast_in_dim.33.x_log), custom_call_target="tpu_custom_call" | custom-call | tf_op jit(solution)/shard_map/pallas_call | solution.py:193
  38.2 0.9 exponential_reduce_fusion
  39.3 1.0 multiply_add_fusion
  40.4 0.5 fusion.6
  40.8 1.3 fusion.5
  42.2 0.4 copy.32
  42.9 0.8 copy.34
  43.8 16.7 %shard_map.146 = bf16[16,16,512]{2,1,0:T(8,128)(2,1)} custom-call(bf16[16,16,512]{2,1,0:T(8,128)(2,1)} %bitcast.76), custom_call_target="tpu_custom_call" | custom-call | tf_op jit(solution)/shard_map/pallas_call | solution.py:48
  60.5 1.0 convert_bitcast_fusion
  61.9 0.4 broadcast_in_dim.34
  63.0 0.3 convolution_convert_fusion
  63.4 1.9 reshape.129.x_ref
  65.3 25.1 %shard_map.147 = bf16[16,16,1536]{2,1,0:T(8,128)(2,1)} custom-call(bf16[16,16,1536]{2,1,0:T(8,128)(2,1)} %reshape.129.x_ref), custom_call_target="tpu_custom_call" | custom-call | tf_op jit(solution)/shard_map/pallas_call | solution.py:48
  90.4 3.1 reshape.130
  93.7 93.6 %all-gather.2.cloned.1.call-done.seg_ref = bf16[768,8192]{1,0:T(8,128)(2,1)} async-done(((bf16[48,8192]{1,0:T(8,128)(2,1)}), bf16[768,8192]{1,0:T(8,128)(2,1)}) %all-gather.2.cloned.1.call-update) | async-done | bytes 12582928 | tf_op jit(solution)/shard_map/all_gather | solution.py:303
  187.3 14.8 %shard_map.148 = bf16[768,8192]{1,0:T(8,128)(2,1)} custom-call(bf16[768,8192]{1,0:T(8,128)(2,1)} %all-gather.2.cloned.1.call-done.seg_ref, bf16[8192,128]{1,0:T(8,128)(2,1)} %bitcast.73, bf16[8192,128]{1,0:T(8,128)(2,1)} %bitcast.74, bf16[128,8192]{1,0:T(8,128)(2,1)} %bitcast.75), custom_call_target="tpu_custom_call" | custom-call | flops 4831838208 | bytes 31457280 | tf_op jit(solution)/shard_map/pallas_call | solution.py:96
  202.3 0.5 copy-done.7
  202.9 98.5 %reduce-scatter.2.cloned.1.call-done = bf16[48,8192]{1,0:T(8,128)(2,1)} async-done(((bf16[768,8192]{1,0:T(8,128)(2,1)}), bf16[48,8192]{1,0:T(8,128)(2,1)}) %reduce-scatter.2.cloned.1.call-update) | async-done | bytes 786448 | tf_op jit(solution)/shard_map/reduce_scatter | solution.py:305
  301.4 3.0 reshape.131.x_ref
  304.5 26.8 %shard_map.149 = bf16[16,16,1536]{2,1,0:T(8,128)(2,1)} custom-call(bf16[16,16,1536]{2,1,0:T(8,128)(2,1)} %reshape.131.x_ref), custom_call_target="tpu_custom_call" | custom-call | tf_op jit(solution)/shard_map/pallas_call | solution.py:48
  331.3 2.2 reshape.132
  333.5 0.9 gather_fusion
  334.4 0.7 reshape.134
  335.0 1.4 multiply_reduce_fusion
  336.5 0.8 fusion.19
  (62 shorter events, 3.1 us)
Async XLA Ops:
  6.5 3.6 %copy-start = (bf16[256,128]{1,0:T(8,128)(2,1)S(1)}, bf16[256,128]{1,0:T(8,128)(2,1)}, u32[]{:S(2)}) copy-start(bf16[256,128]{1,0:T(8,128)(2,1)} %param.19) | copy-start | bytes 196612
  6.5 180.8 %all-gather.2.cloned.1.call-start = ((), (), s32[]{:S(2)}) async-start(), calls=%async_computation.1 | async-start | bytes 13369344 | tf_op jit(solution)/shard_map/all_gather | solution.py:303
  10.6 28.6 %copy-start.2 = (bf16[256,128]{1,0:T(8,128)(2,1)S(1)}, bf16[256,128]{1,0:T(8,128)(2,1)}, u32[]{:S(2)}) copy-start(bf16[256,128]{1,0:T(8,128)(2,1)} %param.20) | copy-start | bytes 196612
  10.6 28.7 %copy-start.3 = (f32[8,64,128]{2,1,0:T(8,128)S(1)}, f32[8,64,128]{2,1,0:T(8,128)}, u32[]{:S(2)}) copy-start(f32[8,64,128]{2,1,0:T(8,128)} %param.24) | copy-start | bytes 786436
  11.0 29.8 %copy-start.8 = (f32[8]{0:T(128)S(1)}, f32[8]{0:T(128)}, u32[]{:S(2)}) copy-start(f32[8]{0:T(128)} %param.23) | copy-start | bytes 100
  40.4 2.2 copy-start.1
  42.7 18.8 %copy-start.4 = (bf16[16,8192]{1,0:T(8,128)(2,1)S(1)}, bf16[16,8192]{1,0:T(8,128)(2,1)}, u32[]{:S(2)}) copy-start(bf16[16,8192]{1,0:T(8,128)(2,1)} %param.25) | copy-start | bytes 786436
  42.9 18.8 %copy-start.5 = (f32[8192]{0:T(1024)S(1)}, f32[8192]{0:T(1024)}, u32[]{:S(2)}) copy-start(f32[8192]{0:T(1024)} %param.26) | copy-start | bytes 98308
  61.5 1.1 copy-start.6
  93.5 207.9 %reduce-scatter.2.cloned.1.call-start = ((), (), s32[]{:S(2)}) async-start(), calls=%async_computation.2 | async-start | bytes 13369344 | tf_op jit(solution)/shard_map/reduce_scatter | solution.py:305
  202.1 0.7 copy-start.7
Sparse Core Ops, SparseCore 0:
  93.6 93.6 all-gather.1
  202.3 99.1 reduce-scatter.1

commit v9 on v8

--- a/solution.py
+++ b/solution.py
@@ -90,9 +90,10 @@
 def expert_mlp(segment, gate_w, up_w, down_w):
     rows, width = segment.shape
     hidden = gate_w.shape[1]
-    block = 2048
+    block = 4096
+    columns = 2048
     depth_steps = width // block
-    column_steps = width // block
+    column_steps = width // columns
     return pl.pallas_call(
         functools.partial(expert_body, depth_steps),
         grid=(depth_steps + column_steps,),
@@ -100,9 +101,9 @@
             pl.BlockSpec((rows, block), lambda i: (0, jnp.minimum(i, depth_steps - 1))),
             pl.BlockSpec((block, hidden), lambda i: (jnp.minimum(i, depth_steps - 1), 0)),
             pl.BlockSpec((block, hidden), lambda i: (jnp.minimum(i, depth_steps - 1), 0)),
-            pl.BlockSpec((hidden, block), lambda i: (0, jnp.maximum(i - depth_steps, 0))),
+            pl.BlockSpec((hidden, columns), lambda i: (0, jnp.maximum(i - depth_steps, 0))),
         ],
-        out_specs=pl.BlockSpec((rows, block), lambda i: (0, jnp.maximum(i - depth_steps, 0))),
+        out_specs=pl.BlockSpec((rows, columns), lambda i: (0, jnp.maximum(i - depth_steps, 0))),
         out_shape=jax.ShapeDtypeStruct((rows, width), jnp.bfloat16),
         scratch_shapes=[
             pltpu.VMEM((rows, hidden), jnp.float32),

time: 345 us -> 344 us (level)
  no operation moved by 1% of the time
where the time goes in v9:
time: 344 us; the launch traced here: 343 us
  waiting for transfers between devices  192 us (56%)
  Pallas kernels  109 us (32%)
  local copies, waits for them, and re-layouts  18.3 us (5%)
  between operations  13.7 us (4%)
  other arithmetic  7.08 us (2%)
    reduce_scatter x1, waiting for transfers between devices, on_device(): lax.psum_scatter(partial_value, 'seq', scatter_dimension=0, tiled=True)  98.4 us
    all_gather x1, waiting for transfers between devices, on_device(): segment = lax.all_gather(arrived, 'seq', axis=0, tiled=True)  93.6 us
    pallas_call x3, Pallas kernels, exchange(): pl.pallas_call(exchange_body, out_shape=jax.ShapeDtypeStruct(x.shape, x.d...  68.6 us
    pallas_call x1, Pallas kernels, exclusive_scan(): pl.pallas_call(functools.partial(scan_body, devices), out_shape=(jax.Shap...  26.4 us
    pallas_call x1, Pallas kernels, expert_mlp(): pl.pallas_call(functools.partial(expert_body, depth_steps), grid=(depth_s...  14.4 us
  transfers between devices with their start and end apart: 2, of which 2 were waited for; matrix products, arithmetic and copies ran while one was open for 0% of the time, Pallas kernels for 0%

profile of v9, /device:TPU:1, one launch (start us, length us, event | category | flops | bytes accessed | tf_op | source)
XLA Modules:
  0.0 343.5 jit_solution(8776409080478171781)
XLA Ops:
  6.5 0.7 neg.8
  7.2 0.8 multiply_bitcast_fusion
  8.5 1.3 reshape.145
  9.8 0.3 copy.28
  10.2 0.4 fusion.11
  10.6 0.4 while.17
  11.0 0.7 broadcast_in_dim.33.x_log
  11.7 26.4 %shard_map.145 = (f32[8,64,128]{2,1,0:T(8,128)}, f32[8,8,128]{2,1,0:T(8,128)}) custom-call(f32[8,64,128]{2,1,0:T(8,128)S(1)} %get-tuple-element.49.x_state, f32[8,8,128]{2,1,0:T(8,128)} %broadcast_in_dim.33.x_log), custom_call_target="tpu_custom_call" | custom-call | tf_op jit(solution)/shard_map/pallas_call | solution.py:194
  38.2 0.9 exponential_reduce_fusion
  39.3 1.0 multiply_add_fusion
  40.4 0.5 fusion.6
  40.8 1.3 fusion.5
  42.2 0.4 copy.32
  42.9 0.8 copy.34
  43.8 16.7 %shard_map.146 = bf16[16,16,512]{2,1,0:T(8,128)(2,1)} custom-call(bf16[16,16,512]{2,1,0:T(8,128)(2,1)} %bitcast.76), custom_call_target="tpu_custom_call" | custom-call | tf_op jit(solution)/shard_map/pallas_call | solution.py:48
  60.5 1.0 convert_bitcast_fusion
  61.9 0.4 broadcast_in_dim.34
  63.0 0.3 convolution_convert_fusion
  63.4 1.9 reshape.129.x_ref
  65.3 25.1 %shard_map.147 = bf16[16,16,1536]{2,1,0:T(8,128)(2,1)} custom-call(bf16[16,16,1536]{2,1,0:T(8,128)(2,1)} %reshape.129.x_ref), custom_call_target="tpu_custom_call" | custom-call | tf_op jit(solution)/shard_map/pallas_call | solution.py:48
  90.4 3.1 reshape.130
  93.7 93.6 %all-gather.2.cloned.1.call-done.seg_ref = bf16[768,8192]{1,0:T(8,128)(2,1)} async-done(((bf16[48,8192]{1,0:T(8,128)(2,1)}), bf16[768,8192]{1,0:T(8,128)(2,1)}) %all-gather.2.cloned.1.call-update) | async-done | bytes 12582928 | tf_op jit(solution)/shard_map/all_gather | solution.py:304
  187.3 14.4 %shard_map.148 = bf16[768,8192]{1,0:T(8,128)(2,1)} custom-call(bf16[768,8192]{1,0:T(8,128)(2,1)} %all-gather.2.cloned.1.call-done.seg_ref, bf16[8192,128]{1,0:T(8,128)(2,1)} %bitcast.73, bf16[8192,128]{1,0:T(8,128)(2,1)} %bitcast.74, bf16[128,8192]{1,0:T(8,128)(2,1)} %bitcast.75), custom_call_target="tpu_custom_call" | custom-call | flops 4831838208 | bytes 31457280 | tf_op jit(solution)/shard_map/pallas_call | solution.py:97
  201.9 0.5 copy-done.7
  202.5 98.4 %reduce-scatter.2.cloned.1.call-done = bf16[48,8192]{1,0:T(8,128)(2,1)} async-done(((bf16[768,8192]{1,0:T(8,128)(2,1)}), bf16[48,8192]{1,0:T(8,128)(2,1)}) %reduce-scatter.2.cloned.1.call-update) | async-done | bytes 786448 | tf_op jit(solution)/shard_map/reduce_scatter | solution.py:306
  300.9 3.0 reshape.131.x_ref
  303.9 26.8 %shard_map.149 = bf16[16,16,1536]{2,1,0:T(8,128)(2,1)} custom-call(bf16[16,16,1536]{2,1,0:T(8,128)(2,1)} %reshape.131.x_ref), custom_call_target="tpu_custom_call" | custom-call | tf_op jit(solution)/shard_map/pallas_call | solution.py:48
  330.7 2.2 reshape.132
  332.9 0.9 gather_fusion
  333.8 0.7 reshape.134
  334.4 1.4 multiply_reduce_fusion
  335.9 0.8 fusion.19
  (62 shorter events, 3.1 us)
Async XLA Ops:
  6.5 3.6 %copy-start = (bf16[256,128]{1,0:T(8,128)(2,1)S(1)}, bf16[256,128]{1,0:T(8,128)(2,1)}, u32[]{:S(2)}) copy-start(bf16[256,128]{1,0:T(8,128)(2,1)} %param.19) | copy-start | bytes 196612
  6.5 180.8 %all-gather.2.cloned.1.call-start = ((), (), s32[]{:S(2)}) async-start(), calls=%async_computation.1 | async-start | bytes 13369344 | tf_op jit(solution)/shard_map/all_gather | solution.py:304
  10.6 28.6 %copy-start.2 = (bf16[256,128]{1,0:T(8,128)(2,1)S(1)}, bf16[256,128]{1,0:T(8,128)(2,1)}, u32[]{:S(2)}) copy-start(bf16[256,128]{1,0:T(8,128)(2,1)} %param.20) | copy-start | bytes 196612
  10.6 28.7 %copy-start.3 = (f32[8,64,128]{2,1,0:T(8,128)S(1)}, f32[8,64,128]{2,1,0:T(8,128)}, u32[]{:S(2)}) copy-start(f32[8,64,128]{2,1,0:T(8,128)} %param.24) | copy-start | bytes 786436
  11.0 29.8 %copy-start.8 = (f32[8]{0:T(128)S(1)}, f32[8]{0:T(128)}, u32[]{:S(2)}) copy-start(f32[8]{0:T(128)} %param.23) | copy-start | bytes 100
  40.4 2.2 copy-start.1
  42.7 18.8 %copy-start.4 = (bf16[16,8192]{1,0:T(8,128)(2,1)S(1)}, bf16[16,8192]{1,0:T(8,128)(2,1)}, u32[]{:S(2)}) copy-start(bf16[16,8192]{1,0:T(8,128)(2,1)} %param.25) | copy-start | bytes 786436
  42.9 18.8 %copy-start.5 = (f32[8192]{0:T(1024)S(1)}, f32[8192]{0:T(1024)}, u32[]{:S(2)}) copy-start(f32[8192]{0:T(1024)} %param.26) | copy-start | bytes 98308
  61.5 1.1 copy-start.6
  93.5 207.4 %reduce-scatter.2.cloned.1.call-start = ((), (), s32[]{:S(2)}) async-start(), calls=%async_computation.2 | async-start | bytes 13369344 | tf_op jit(solution)/shard_map/reduce_scatter | solution.py:306
  201.7 0.7 copy-start.7
Sparse Core Ops, SparseCore 0:
  93.6 93.6 all-gather.1
  201.9 98.9 reduce-scatter.1

commit v10 on v9

--- a/solution.py
+++ b/solution.py
@@ -22,11 +22,12 @@
     for step in range(1, devices):
         peer = lax.rem(me + step, devices)
         pl.semaphore_signal(barrier, 1, device_id=(row, peer), device_id_type=mesh_id)
-    pl.semaphore_wait(barrier, devices - 1)
     local = pltpu.make_async_copy(x_ref.at[me], o_ref.at[me], local_sem)
     local.start()
+    pl.semaphore_wait(barrier, devices - 1)
     copies = []
-    for step in range(1, devices):
+    order = sorted(range(1, devices), key=lambda step: -min(step, devices - step))
+    for step in order:
         peer = lax.rem(me + step, devices)
         copy = pltpu.make_async_remote_copy(
             src_ref=x_ref.at[peer],

time: 344 us -> 343 us (level)
  no operation moved by 1% of the time
where the time goes in v10:
time: 343 us
  waiting for transfers between devices  191 us (56%)
  Pallas kernels  109 us (32%)
  local copies, waits for them, and re-layouts  18.3 us (5%)
  between operations  13.7 us (4%)
  other arithmetic  7.08 us (2%)
    reduce_scatter x1, waiting for transfers between devices, on_device(): lax.psum_scatter(partial_value, 'seq', scatter_dimension=0, tiled=True)  98.4 us
    all_gather x1, waiting for transfers between devices, on_device(): segment = lax.all_gather(arrived, 'seq', axis=0, tiled=True)  92.8 us
    pallas_call x3, Pallas kernels, exchange(): pl.pallas_call(exchange_body, out_shape=jax.ShapeDtypeStruct(x.shape, x.d...  68.5 us
    pallas_call x1, Pallas kernels, exclusive_scan(): pl.pallas_call(functools.partial(scan_body, devices), out_shape=(jax.Shap...  26.4 us
    pallas_call x1, Pallas kernels, expert_mlp(): pl.pallas_call(functools.partial(expert_body, depth_steps), grid=(depth_s...  14.4 us
  transfers between devices with their start and end apart: 2, of which 2 were waited for; matrix products, arithmetic and copies ran while one was open for 0% of the time, Pallas kernels for 0%

profile of v10, /device:TPU:1, one launch (start us, length us, event | category | flops | bytes accessed | tf_op | source)
XLA Modules:
  0.0 342.6 jit_solution(3340220187219049537)
XLA Ops:
  6.5 0.7 neg.8
  7.2 0.8 multiply_bitcast_fusion
  8.5 1.3 reshape.145
  9.8 0.3 copy.28
  10.2 0.4 fusion.11
  10.6 0.4 while.17
  11.0 0.7 broadcast_in_dim.33.x_log
  11.7 26.4 %shard_map.145 = (f32[8,64,128]{2,1,0:T(8,128)}, f32[8,8,128]{2,1,0:T(8,128)}) custom-call(f32[8,64,128]{2,1,0:T(8,128)S(1)} %get-tuple-element.49.x_state, f32[8,8,128]{2,1,0:T(8,128)} %broadcast_in_dim.33.x_log), custom_call_target="tpu_custom_call" | custom-call | tf_op jit(solution)/shard_map/pallas_call | solution.py:195
  38.2 0.9 exponential_reduce_fusion
  39.3 1.0 multiply_add_fusion
  40.4 0.5 fusion.6
  40.8 1.3 fusion.5
  42.2 0.4 copy.32
  42.9 0.8 copy.34
  43.8 16.7 %shard_map.146 = bf16[16,16,512]{2,1,0:T(8,128)(2,1)} custom-call(bf16[16,16,512]{2,1,0:T(8,128)(2,1)} %bitcast.76), custom_call_target="tpu_custom_call" | custom-call | tf_op jit(solution)/shard_map/pallas_call | solution.py:49
  60.5 1.0 convert_bitcast_fusion
  61.9 0.4 broadcast_in_dim.34
  63.0 0.3 convolution_convert_fusion
  63.4 1.9 reshape.129.x_ref
  65.3 24.8 %shard_map.147 = bf16[16,16,1536]{2,1,0:T(8,128)(2,1)} custom-call(bf16[16,16,1536]{2,1,0:T(8,128)(2,1)} %reshape.129.x_ref), custom_call_target="tpu_custom_call" | custom-call | tf_op jit(solution)/shard_map/pallas_call | solution.py:49
  90.1 3.1 reshape.130
  93.5 92.8 %all-gather.2.cloned.1.call-done.seg_ref = bf16[768,8192]{1,0:T(8,128)(2,1)} async-done(((bf16[48,8192]{1,0:T(8,128)(2,1)}), bf16[768,8192]{1,0:T(8,128)(2,1)}) %all-gather.2.cloned.1.call-update) | async-done | bytes 12582928 | tf_op jit(solution)/shard_map/all_gather | solution.py:305
  186.3 14.4 %shard_map.148 = bf16[768,8192]{1,0:T(8,128)(2,1)} custom-call(bf16[768,8192]{1,0:T(8,128)(2,1)} %all-gather.2.cloned.1.call-done.seg_ref, bf16[8192,128]{1,0:T(8,128)(2,1)} %bitcast.73, bf16[8192,128]{1,0:T(8,128)(2,1)} %bitcast.74, bf16[128,8192]{1,0:T(8,128)(2,1)} %bitcast.75), custom_call_target="tpu_custom_call" | custom-call | flops 4831838208 | bytes 31457280 | tf_op jit(solution)/shard_map/pallas_call | solution.py:98
  200.9 0.5 copy-done.7
  201.4 98.4 %reduce-scatter.2.cloned.1.call-done = bf16[48,8192]{1,0:T(8,128)(2,1)} async-done(((bf16[768,8192]{1,0:T(8,128)(2,1)}), bf16[48,8192]{1,0:T(8,128)(2,1)}) %reduce-scatter.2.cloned.1.call-update) | async-done | bytes 786448 | tf_op jit(solution)/shard_map/reduce_scatter | solution.py:307
  299.8 3.0 reshape.131.x_ref
  302.9 27.0 %shard_map.149 = bf16[16,16,1536]{2,1,0:T(8,128)(2,1)} custom-call(bf16[16,16,1536]{2,1,0:T(8,128)(2,1)} %reshape.131.x_ref), custom_call_target="tpu_custom_call" | custom-call | tf_op jit(solution)/shard_map/pallas_call | solution.py:49
  329.9 2.2 reshape.132
  332.1 0.9 gather_fusion
  332.9 0.7 reshape.134
  333.6 1.4 multiply_reduce_fusion
  335.0 0.8 fusion.19
  (62 shorter events, 3.1 us)
Async XLA Ops:
  6.5 3.6 %copy-start = (bf16[256,128]{1,0:T(8,128)(2,1)S(1)}, bf16[256,128]{1,0:T(8,128)(2,1)}, u32[]{:S(2)}) copy-start(bf16[256,128]{1,0:T(8,128)(2,1)} %param.19) | copy-start | bytes 196612
  6.5 179.7 %all-gather.2.cloned.1.call-start = ((), (), s32[]{:S(2)}) async-start(), calls=%async_computation.1 | async-start | bytes 13369344 | tf_op jit(solution)/shard_map/all_gather | solution.py:305
  10.6 28.6 %copy-start.2 = (bf16[256,128]{1,0:T(8,128)(2,1)S(1)}, bf16[256,128]{1,0:T(8,128)(2,1)}, u32[]{:S(2)}) copy-start(bf16[256,128]{1,0:T(8,128)(2,1)} %param.20) | copy-start | bytes 196612
  10.6 28.7 %copy-start.3 = (f32[8,64,128]{2,1,0:T(8,128)S(1)}, f32[8,64,128]{2,1,0:T(8,128)}, u32[]{:S(2)}) copy-start(f32[8,64,128]{2,1,0:T(8,128)} %param.24) | copy-start | bytes 786436
  11.0 29.8 %copy-start.8 = (f32[8]{0:T(128)S(1)}, f32[8]{0:T(128)}, u32[]{:S(2)}) copy-start(f32[8]{0:T(128)} %param.23) | copy-start | bytes 100
  40.4 2.2 copy-start.1
  42.7 18.8 %copy-start.4 = (bf16[16,8192]{1,0:T(8,128)(2,1)S(1)}, bf16[16,8192]{1,0:T(8,128)(2,1)}, u32[]{:S(2)}) copy-start(bf16[16,8192]{1,0:T(8,128)(2,1)} %param.25) | copy-start | bytes 786436
  42.9 18.8 %copy-start.5 = (f32[8192]{0:T(1024)S(1)}, f32[8192]{0:T(1024)}, u32[]{:S(2)}) copy-start(f32[8192]{0:T(1024)} %param.26) | copy-start | bytes 98308
  61.5 1.1 copy-start.6
  93.2 206.6 %reduce-scatter.2.cloned.1.call-start = ((), (), s32[]{:S(2)}) async-start(), calls=%async_computation.2 | async-start | bytes 13369344 | tf_op jit(solution)/shard_map/reduce_scatter | solution.py:307
  200.7 0.7 copy-start.7
Sparse Core Ops, SparseCore 0:
  93.3 92.8 all-gather.1
  200.8 98.9 reduce-scatter.1

commit v11 on v10

--- a/solution.py
+++ b/solution.py
@@ -120,11 +120,7 @@
 
 
 def scan_rounds(devices):
-    rounds, base = [], 1
-    while base < devices:
-        rounds.append([j * base for j in range(1, 4) if j * base < devices])
-        base *= 4
-    return rounds
+    return [list(range(1, devices))]
 
 
 def fold(earlier_state, earlier_log, later_state, later_log):
@@ -204,9 +200,9 @@
             pltpu.VMEM((levels + 1,) + state.shape, jnp.float32),
             pltpu.VMEM((levels + 1,) + log_rows.shape, jnp.float32),
             pltpu.VMEM((levels,) + wire_shape, jnp.bfloat16),
-            pltpu.VMEM((levels, 3) + wire_shape, jnp.bfloat16),
-            pltpu.SemaphoreType.DMA((levels, 3)),
-            pltpu.SemaphoreType.DMA((levels, 3)),
+            pltpu.VMEM((levels, devices - 1) + wire_shape, jnp.bfloat16),
+            pltpu.SemaphoreType.DMA((levels, devices - 1)),
+            pltpu.SemaphoreType.DMA((levels, devices - 1)),
         ],
         compiler_params=pltpu.CompilerParams(collective_id=3, has_side_effects=True),
     )(state, log_rows)

time: 343 us -> 362 us (1.055)
  Pallas kernels: 109 us -> 126 us
    pallas_call x1, Pallas kernels: 26.4 us -> 43.5 us  [exclusive_scan(): pl.pallas_call(functools.partial(scan_body, devices), out_shape=(jax.Shap...]
where the time goes in v11:
time: 362 us; the launch traced here: 361 us
  waiting for transfers between devices  192 us (53%)
  Pallas kernels  126 us (35%)
  local copies, waits for them, and re-layouts  18.3 us (5%)
  between operations  13.7 us (4%)
  other arithmetic  7.08 us (2%)
    reduce_scatter x1, waiting for transfers between devices, on_device(): lax.psum_scatter(partial_value, 'seq', scatter_dimension=0, tiled=True)  98.3 us
    all_gather x1, waiting for transfers between devices, on_device(): segment = lax.all_gather(arrived, 'seq', axis=0, tiled=True)  94.2 us
    pallas_call x3, Pallas kernels, exchange(): pl.pallas_call(exchange_body, out_shape=jax.ShapeDtypeStruct(x.shape, x.d...  68.5 us
    pallas_call x1, Pallas kernels, exclusive_scan(): pl.pallas_call(functools.partial(scan_body, devices), out_shape=(jax.Shap...  43.5 us
    pallas_call x1, Pallas kernels, expert_mlp(): pl.pallas_call(functools.partial(expert_body, depth_steps), grid=(depth_s...  14.4 us
  transfers between devices with their start and end apart: 2, of which 2 were waited for; matrix products, arithmetic and copies ran while one was open for 0% of the time, Pallas kernels for 0%

profile of v11, /device:TPU:1, one launch (start us, length us, event | category | flops | bytes accessed | tf_op | source)
XLA Modules:
  0.0 360.9 jit_solution(12037337769760210129)
XLA Ops:
  6.5 0.7 neg.8
  7.2 0.8 multiply_bitcast_fusion
  8.5 1.3 reshape.145
  9.8 0.3 copy.28
  10.2 0.4 fusion.11
  10.6 0.4 while.17
  11.0 0.7 broadcast_in_dim.33.x_log
  11.7 43.5 %shard_map.145 = (f32[8,64,128]{2,1,0:T(8,128)}, f32[8,8,128]{2,1,0:T(8,128)}) custom-call(f32[8,64,128]{2,1,0:T(8,128)S(1)} %get-tuple-element.49.x_state, f32[8,8,128]{2,1,0:T(8,128)} %broadcast_in_dim.33.x_log), custom_call_target="tpu_custom_call" | custom-call | tf_op jit(solution)/shard_map/pallas_call | solution.py:191
  55.2 0.9 exponential_reduce_fusion
  56.3 1.0 multiply_add_fusion
  57.4 0.5 fusion.6
  57.9 1.3 fusion.5
  59.2 0.4 copy.32
  60.0 0.8 copy.34
  60.8 16.7 %shard_map.146 = bf16[16,16,512]{2,1,0:T(8,128)(2,1)} custom-call(bf16[16,16,512]{2,1,0:T(8,128)(2,1)} %bitcast.76), custom_call_target="tpu_custom_call" | custom-call | tf_op jit(solution)/shard_map/pallas_call | solution.py:49
  77.5 1.0 convert_bitcast_fusion
  78.9 0.4 broadcast_in_dim.34
  80.1 0.3 convolution_convert_fusion
  80.4 1.9 reshape.129.x_ref
  82.3 24.8 %shard_map.147 = bf16[16,16,1536]{2,1,0:T(8,128)(2,1)} custom-call(bf16[16,16,1536]{2,1,0:T(8,128)(2,1)} %reshape.129.x_ref), custom_call_target="tpu_custom_call" | custom-call | tf_op jit(solution)/shard_map/pallas_call | solution.py:49
  107.1 3.1 reshape.130
  110.5 94.2 %all-gather.2.cloned.1.call-done.seg_ref = bf16[768,8192]{1,0:T(8,128)(2,1)} async-done(((bf16[48,8192]{1,0:T(8,128)(2,1)}), bf16[768,8192]{1,0:T(8,128)(2,1)}) %all-gather.2.cloned.1.call-update) | async-done | bytes 12582928 | tf_op jit(solution)/shard_map/all_gather | solution.py:301
  204.7 14.4 %shard_map.148 = bf16[768,8192]{1,0:T(8,128)(2,1)} custom-call(bf16[768,8192]{1,0:T(8,128)(2,1)} %all-gather.2.cloned.1.call-done.seg_ref, bf16[8192,128]{1,0:T(8,128)(2,1)} %bitcast.73, bf16[8192,128]{1,0:T(8,128)(2,1)} %bitcast.74, bf16[128,8192]{1,0:T(8,128)(2,1)} %bitcast.75), custom_call_target="tpu_custom_call" | custom-call | flops 4831838208 | bytes 31457280 | tf_op jit(solution)/shard_map/pallas_call | solution.py:98
  219.3 0.5 copy-done.7
  219.8 98.3 %reduce-scatter.2.cloned.1.call-done = bf16[48,8192]{1,0:T(8,128)(2,1)} async-done(((bf16[768,8192]{1,0:T(8,128)(2,1)}), bf16[48,8192]{1,0:T(8,128)(2,1)}) %reduce-scatter.2.cloned.1.call-update) | async-done | bytes 786448 | tf_op jit(solution)/shard_map/reduce_scatter | solution.py:303
  318.1 3.0 reshape.131.x_ref
  321.1 27.0 %shard_map.149 = bf16[16,16,1536]{2,1,0:T(8,128)(2,1)} custom-call(bf16[16,16,1536]{2,1,0:T(8,128)(2,1)} %reshape.131.x_ref), custom_call_target="tpu_custom_call" | custom-call | tf_op jit(solution)/shard_map/pallas_call | solution.py:49
  348.1 2.2 reshape.132
  350.3 0.9 gather_fusion
  351.2 0.7 reshape.134
  351.9 1.4 multiply_reduce_fusion
  353.3 0.8 fusion.19
  (62 shorter events, 3.1 us)
Async XLA Ops:
  6.5 3.6 %copy-start = (bf16[256,128]{1,0:T(8,128)(2,1)S(1)}, bf16[256,128]{1,0:T(8,128)(2,1)}, u32[]{:S(2)}) copy-start(bf16[256,128]{1,0:T(8,128)(2,1)} %param.19) | copy-start | bytes 196612
  6.5 198.1 %all-gather.2.cloned.1.call-start = ((), (), s32[]{:S(2)}) async-start(), calls=%async_computation.1 | async-start | bytes 13369344 | tf_op jit(solution)/shard_map/all_gather | solution.py:301
  10.6 45.6 %copy-start.2 = (bf16[256,128]{1,0:T(8,128)(2,1)S(1)}, bf16[256,128]{1,0:T(8,128)(2,1)}, u32[]{:S(2)}) copy-start(bf16[256,128]{1,0:T(8,128)(2,1)} %param.20) | copy-start | bytes 196612
  10.6 45.7 %copy-start.3 = (f32[8,64,128]{2,1,0:T(8,128)S(1)}, f32[8,64,128]{2,1,0:T(8,128)}, u32[]{:S(2)}) copy-start(f32[8,64,128]{2,1,0:T(8,128)} %param.24) | copy-start | bytes 786436
  11.0 46.9 %copy-start.8 = (f32[8]{0:T(128)S(1)}, f32[8]{0:T(128)}, u32[]{:S(2)}) copy-start(f32[8]{0:T(128)} %param.23) | copy-start | bytes 100
  57.4 2.2 copy-start.1
  59.8 18.8 %copy-start.4 = (bf16[16,8192]{1,0:T(8,128)(2,1)S(1)}, bf16[16,8192]{1,0:T(8,128)(2,1)}, u32[]{:S(2)}) copy-start(bf16[16,8192]{1,0:T(8,128)(2,1)} %param.25) | copy-start | bytes 786436
  59.9 18.9 %copy-start.5 = (f32[8192]{0:T(1024)S(1)}, f32[8192]{0:T(1024)}, u32[]{:S(2)}) copy-start(f32[8192]{0:T(1024)} %param.26) | copy-start | bytes 98308
  78.5 1.1 copy-start.6
  110.3 207.8 %reduce-scatter.2.cloned.1.call-start = ((), (), s32[]{:S(2)}) async-start(), calls=%async_computation.2 | async-start | bytes 13369344 | tf_op jit(solution)/shard_map/reduce_scatter | solution.py:303
  219.1 0.7 copy-start.7
Sparse Core Ops, SparseCore 0:
  110.4 94.2 all-gather.1
  219.2 98.8 reduce-scatter.1

commit v12 on v10

--- a/solution.py
+++ b/solution.py
@@ -142,14 +142,15 @@
         peer = lax.rem(me + step, devices)
         pl.semaphore_signal(barrier, 1, device_id=(peer, col), device_id_type=mesh_id)
     pl.semaphore_wait(barrier, devices - 1)
-    inc_state[0] = x_state[...]
-    inc_log[0] = x_log[...]
     o_state[...] = jnp.zeros_like(o_state)
     o_log[...] = jnp.zeros_like(o_log)
-    for level, shifts in enumerate(scan_rounds(devices)):
-        log_now = inc_log[level]
+    levels = scan_rounds(devices)
+    for level, shifts in enumerate(levels):
+        last = level == len(levels) - 1
+        state_now = x_state if level == 0 else inc_state.at[level]
+        log_now = x_log[...] if level == 0 else inc_log[level]
         high = log_now.astype(jnp.bfloat16).astype(jnp.float32)
-        wire[level, :, :rows, :] = inc_state[level].astype(jnp.bfloat16)
+        wire[level, :, :rows, :] = state_now[...].astype(jnp.bfloat16)
         wire[level, :, rows:, :] = jnp.concatenate([high, log_now - high], axis=1).astype(jnp.bfloat16)
 
         def link(slot, peer):
@@ -165,8 +166,9 @@
             @pl.when(me + shift < devices)
             def _():
                 link(slot, me + shift).start()
-        inc_state[level + 1] = inc_state[level]
-        inc_log[level + 1] = inc_log[level]
+        if not last:
+            inc_state[level + 1] = state_now[...]
+            inc_log[level + 1] = log_now
         for slot, shift in enumerate(shifts):
             @pl.when(me >= shift)
             def _():
@@ -174,9 +176,10 @@
                 got_state = recv[level, slot, :, :rows, :].astype(jnp.float32)
                 parts = recv[level, slot, :, rows:, :].astype(jnp.float32)
                 got_log = parts[:, :8, :] + parts[:, 8:, :]
-                new_state, new_log = fold(got_state, got_log, inc_state[level + 1], inc_log[level + 1])
-                inc_state[level + 1] = new_state
-                inc_log[level + 1] = new_log
+                if not last:
+                    new_state, new_log = fold(got_state, got_log, inc_state[level + 1], inc_log[level + 1])
+                    inc_state[level + 1] = new_state
+                    inc_log[level + 1] = new_log
                 new_state, new_log = fold(got_state, got_log, o_state[...], o_log[...])
                 o_state[...] = new_state
                 o_log[...] = new_log

time: 343 us -> 343 us (level)
  no operation moved by 1% of the time
where the time goes in v12:
time: 343 us
  waiting for transfers between devices  191 us (56%)
  Pallas kernels  109 us (32%)
  local copies, waits for them, and re-layouts  18.3 us (5%)
  between operations  13.7 us (4%)
  other arithmetic  7.08 us (2%)
    reduce_scatter x1, waiting for transfers between devices, on_device(): lax.psum_scatter(partial_value, 'seq', scatter_dimension=0, tiled=True)  98.7 us
    all_gather x1, waiting for transfers between devices, on_device(): segment = lax.all_gather(arrived, 'seq', axis=0, tiled=True)  92.7 us
    pallas_call x3, Pallas kernels, exchange(): pl.pallas_call(exchange_body, out_shape=jax.ShapeDtypeStruct(x.shape, x.d...  68.4 us
    pallas_call x1, Pallas kernels, exclusive_scan(): pl.pallas_call(functools.partial(scan_body, devices), out_shape=(jax.Shap...  26.4 us
    pallas_call x1, Pallas kernels, expert_mlp(): pl.pallas_call(functools.partial(expert_body, depth_steps), grid=(depth_s...  14.4 us
  transfers between devices with their start and end apart: 2, of which 2 were waited for; matrix products, arithmetic and copies ran while one was open for 0% of the time, Pallas kernels for 0%

profile of v12, /device:TPU:1, one launch (start us, length us, event | category | flops | bytes accessed | tf_op | source)
XLA Modules:
  0.0 342.8 jit_solution(17701363590657521991)
XLA Ops:
  6.5 0.7 neg.8
  7.2 0.8 multiply_bitcast_fusion
  8.5 1.3 reshape.145
  9.8 0.3 copy.28
  10.2 0.4 fusion.11
  10.6 0.4 while.17
  11.0 0.7 broadcast_in_dim.33.x_log
  11.7 26.4 %shard_map.145 = (f32[8,64,128]{2,1,0:T(8,128)}, f32[8,8,128]{2,1,0:T(8,128)}) custom-call(f32[8,64,128]{2,1,0:T(8,128)S(1)} %get-tuple-element.49.x_state, f32[8,8,128]{2,1,0:T(8,128)} %broadcast_in_dim.33.x_log), custom_call_target="tpu_custom_call" | custom-call | tf_op jit(solution)/shard_map/pallas_call | solution.py:198
  38.1 0.9 exponential_reduce_fusion
  39.3 1.0 multiply_add_fusion
  40.4 0.5 fusion.6
  40.8 1.3 fusion.5
  42.2 0.4 copy.32
  42.9 0.8 copy.34
  43.8 16.7 %shard_map.146 = bf16[16,16,512]{2,1,0:T(8,128)(2,1)} custom-call(bf16[16,16,512]{2,1,0:T(8,128)(2,1)} %bitcast.76), custom_call_target="tpu_custom_call" | custom-call | tf_op jit(solution)/shard_map/pallas_call | solution.py:49
  60.4 1.0 convert_bitcast_fusion
  61.9 0.4 broadcast_in_dim.34
  63.0 0.3 convolution_convert_fusion
  63.4 1.9 reshape.129.x_ref
  65.3 24.8 %shard_map.147 = bf16[16,16,1536]{2,1,0:T(8,128)(2,1)} custom-call(bf16[16,16,1536]{2,1,0:T(8,128)(2,1)} %reshape.129.x_ref), custom_call_target="tpu_custom_call" | custom-call | tf_op jit(solution)/shard_map/pallas_call | solution.py:49
  90.1 3.1 reshape.130
  93.4 92.7 %all-gather.2.cloned.1.call-done.seg_ref = bf16[768,8192]{1,0:T(8,128)(2,1)} async-done(((bf16[48,8192]{1,0:T(8,128)(2,1)}), bf16[768,8192]{1,0:T(8,128)(2,1)}) %all-gather.2.cloned.1.call-update) | async-done | bytes 12582928 | tf_op jit(solution)/shard_map/all_gather | solution.py:308
  186.2 14.4 %shard_map.148 = bf16[768,8192]{1,0:T(8,128)(2,1)} custom-call(bf16[768,8192]{1,0:T(8,128)(2,1)} %all-gather.2.cloned.1.call-done.seg_ref, bf16[8192,128]{1,0:T(8,128)(2,1)} %bitcast.73, bf16[8192,128]{1,0:T(8,128)(2,1)} %bitcast.74, bf16[128,8192]{1,0:T(8,128)(2,1)} %bitcast.75), custom_call_target="tpu_custom_call" | custom-call | flops 4831838208 | bytes 31457280 | tf_op jit(solution)/shard_map/pallas_call | solution.py:98
  200.8 0.5 copy-done.7
  201.4 98.7 %reduce-scatter.2.cloned.1.call-done = bf16[48,8192]{1,0:T(8,128)(2,1)} async-done(((bf16[768,8192]{1,0:T(8,128)(2,1)}), bf16[48,8192]{1,0:T(8,128)(2,1)}) %reduce-scatter.2.cloned.1.call-update) | async-done | bytes 786448 | tf_op jit(solution)/shard_map/reduce_scatter | solution.py:310
  300.0 3.0 reshape.131.x_ref
  303.1 26.9 %shard_map.149 = bf16[16,16,1536]{2,1,0:T(8,128)(2,1)} custom-call(bf16[16,16,1536]{2,1,0:T(8,128)(2,1)} %reshape.131.x_ref), custom_call_target="tpu_custom_call" | custom-call | tf_op jit(solution)/shard_map/pallas_call | solution.py:49
  330.0 2.2 reshape.132
  332.2 0.9 gather_fusion
  333.1 0.7 reshape.134
  333.8 1.4 multiply_reduce_fusion
  335.2 0.8 fusion.19
  (62 shorter events, 3.1 us)
Async XLA Ops:
  6.5 3.6 %copy-start = (bf16[256,128]{1,0:T(8,128)(2,1)S(1)}, bf16[256,128]{1,0:T(8,128)(2,1)}, u32[]{:S(2)}) copy-start(bf16[256,128]{1,0:T(8,128)(2,1)} %param.19) | copy-start | bytes 196612
  6.5 179.6 %all-gather.2.cloned.1.call-start = ((), (), s32[]{:S(2)}) async-start(), calls=%async_computation.1 | async-start | bytes 13369344 | tf_op jit(solution)/shard_map/all_gather | solution.py:308
  10.6 28.5 %copy-start.2 = (bf16[256,128]{1,0:T(8,128)(2,1)S(1)}, bf16[256,128]{1,0:T(8,128)(2,1)}, u32[]{:S(2)}) copy-start(bf16[256,128]{1,0:T(8,128)(2,1)} %param.20) | copy-start | bytes 196612
  10.6 28.7 %copy-start.3 = (f32[8,64,128]{2,1,0:T(8,128)S(1)}, f32[8,64,128]{2,1,0:T(8,128)}, u32[]{:S(2)}) copy-start(f32[8,64,128]{2,1,0:T(8,128)} %param.24) | copy-start | bytes 786436
  11.0 29.8 %copy-start.8 = (f32[8]{0:T(128)S(1)}, f32[8]{0:T(128)}, u32[]{:S(2)}) copy-start(f32[8]{0:T(128)} %param.23) | copy-start | bytes 100
  40.3 2.2 copy-start.1
  42.7 18.8 %copy-start.4 = (bf16[16,8192]{1,0:T(8,128)(2,1)S(1)}, bf16[16,8192]{1,0:T(8,128)(2,1)}, u32[]{:S(2)}) copy-start(bf16[16,8192]{1,0:T(8,128)(2,1)} %param.25) | copy-start | bytes 786436
  42.9 18.8 %copy-start.5 = (f32[8192]{0:T(1024)S(1)}, f32[8192]{0:T(1024)}, u32[]{:S(2)}) copy-start(f32[8192]{0:T(1024)} %param.26) | copy-start | bytes 98308
  61.4 1.1 copy-start.6
  93.2 206.8 %reduce-scatter.2.cloned.1.call-start = ((), (), s32[]{:S(2)}) async-start(), calls=%async_computation.2 | async-start | bytes 13369344 | tf_op jit(solution)/shard_map/reduce_scatter | solution.py:310
  200.6 0.7 copy-start.7
Sparse Core Ops, SparseCore 0:
  93.3 92.8 all-gather.1
  200.7 99.2 reduce-scatter.1

commit v13 on v12

--- a/solution.py
+++ b/solution.py
@@ -122,8 +122,8 @@
 def scan_rounds(devices):
     rounds, base = [], 1
     while base < devices:
-        rounds.append([j * base for j in range(1, 4) if j * base < devices])
-        base *= 4
+        rounds.append([base])
+        base *= 2
     return rounds
 
 
@@ -207,9 +207,9 @@
             pltpu.VMEM((levels + 1,) + state.shape, jnp.float32),
             pltpu.VMEM((levels + 1,) + log_rows.shape, jnp.float32),
             pltpu.VMEM((levels,) + wire_shape, jnp.bfloat16),
-            pltpu.VMEM((levels, 3) + wire_shape, jnp.bfloat16),
-            pltpu.SemaphoreType.DMA((levels, 3)),
-            pltpu.SemaphoreType.DMA((levels, 3)),
+            pltpu.VMEM((levels, 1) + wire_shape, jnp.bfloat16),
+            pltpu.SemaphoreType.DMA((levels, 1)),
+            pltpu.SemaphoreType.DMA((levels, 1)),
         ],
         compiler_params=pltpu.CompilerParams(collective_id=3, has_side_effects=True),
     )(state, log_rows)

time: 343 us -> 345 us (level)
  no operation moved by 1% of the time
where the time goes in v13:
time: 345 us; the launch traced here: 344 us
  waiting for transfers between devices  194 us (56%)
  Pallas kernels  108 us (31%)
  local copies, waits for them, and re-layouts  18.3 us (5%)
  between operations  13.7 us (4%)
  other arithmetic  7.08 us (2%)
    reduce_scatter x1, waiting for transfers between devices, on_device(): lax.psum_scatter(partial_value, 'seq', scatter_dimension=0, tiled=True)  98.4 us
    all_gather x1, waiting for transfers between devices, on_device(): segment = lax.all_gather(arrived, 'seq', axis=0, tiled=True)  96.1 us
    pallas_call x3, Pallas kernels, exchange(): pl.pallas_call(exchange_body, out_shape=jax.ShapeDtypeStruct(x.shape, x.d...  69 us
    pallas_call x1, Pallas kernels, exclusive_scan(): pl.pallas_call(functools.partial(scan_body, devices), out_shape=(jax.Shap...  24.2 us
    pallas_call x1, Pallas kernels, expert_mlp(): pl.pallas_call(functools.partial(expert_body, depth_steps), grid=(depth_s...  14.4 us
  transfers between devices with their start and end apart: 2, of which 2 were waited for; matrix products, arithmetic and copies ran while one was open for 0% of the time, Pallas kernels for 0%

profile of v13, /device:TPU:1, one launch (start us, length us, event | category | flops | bytes accessed | tf_op | source)
XLA Modules:
  0.0 344.1 jit_solution(17524675731369898622)
XLA Ops:
  6.5 0.7 neg.8
  7.2 0.8 multiply_bitcast_fusion
  8.5 1.3 reshape.145
  9.8 0.3 copy.28
  10.2 0.4 fusion.11
  10.6 0.4 while.17
  11.0 0.7 broadcast_in_dim.33.x_log
  11.7 24.2 %shard_map.145 = (f32[8,64,128]{2,1,0:T(8,128)}, f32[8,8,128]{2,1,0:T(8,128)}) custom-call(f32[8,64,128]{2,1,0:T(8,128)S(1)} %get-tuple-element.49.x_state, f32[8,8,128]{2,1,0:T(8,128)} %broadcast_in_dim.33.x_log), custom_call_target="tpu_custom_call" | custom-call | tf_op jit(solution)/shard_map/pallas_call | solution.py:198
  35.9 0.9 exponential_reduce_fusion
  37.0 1.0 multiply_add_fusion
  38.1 0.5 fusion.6
  38.6 1.3 fusion.5
  39.9 0.4 copy.32
  40.7 0.8 copy.34
  41.5 17.2 %shard_map.146 = bf16[16,16,512]{2,1,0:T(8,128)(2,1)} custom-call(bf16[16,16,512]{2,1,0:T(8,128)(2,1)} %bitcast.76), custom_call_target="tpu_custom_call" | custom-call | tf_op jit(solution)/shard_map/pallas_call | solution.py:49
  58.7 1.0 convert_bitcast_fusion
  60.2 0.4 broadcast_in_dim.34
  61.3 0.3 convolution_convert_fusion
  61.6 1.9 reshape.129.x_ref
  63.5 24.8 %shard_map.147 = bf16[16,16,1536]{2,1,0:T(8,128)(2,1)} custom-call(bf16[16,16,1536]{2,1,0:T(8,128)(2,1)} %reshape.129.x_ref), custom_call_target="tpu_custom_call" | custom-call | tf_op jit(solution)/shard_map/pallas_call | solution.py:49
  88.3 3.1 reshape.130
  91.7 96.1 %all-gather.2.cloned.1.call-done.seg_ref = bf16[768,8192]{1,0:T(8,128)(2,1)} async-done(((bf16[48,8192]{1,0:T(8,128)(2,1)}), bf16[768,8192]{1,0:T(8,128)(2,1)}) %all-gather.2.cloned.1.call-update) | async-done | bytes 12582928 | tf_op jit(solution)/shard_map/all_gather | solution.py:308
  187.8 14.4 %shard_map.148 = bf16[768,8192]{1,0:T(8,128)(2,1)} custom-call(bf16[768,8192]{1,0:T(8,128)(2,1)} %all-gather.2.cloned.1.call-done.seg_ref, bf16[8192,128]{1,0:T(8,128)(2,1)} %bitcast.73, bf16[8192,128]{1,0:T(8,128)(2,1)} %bitcast.74, bf16[128,8192]{1,0:T(8,128)(2,1)} %bitcast.75), custom_call_target="tpu_custom_call" | custom-call | flops 4831838208 | bytes 31457280 | tf_op jit(solution)/shard_map/pallas_call | solution.py:98
  202.4 0.5 copy-done.7
  203.0 98.4 %reduce-scatter.2.cloned.1.call-done = bf16[48,8192]{1,0:T(8,128)(2,1)} async-done(((bf16[768,8192]{1,0:T(8,128)(2,1)}), bf16[48,8192]{1,0:T(8,128)(2,1)}) %reduce-scatter.2.cloned.1.call-update) | async-done | bytes 786448 | tf_op jit(solution)/shard_map/reduce_scatter | solution.py:310
  301.3 3.0 reshape.131.x_ref
  304.4 26.9 %shard_map.149 = bf16[16,16,1536]{2,1,0:T(8,128)(2,1)} custom-call(bf16[16,16,1536]{2,1,0:T(8,128)(2,1)} %reshape.131.x_ref), custom_call_target="tpu_custom_call" | custom-call | tf_op jit(solution)/shard_map/pallas_call | solution.py:49
  331.3 2.2 reshape.132
  333.5 0.9 gather_fusion
  334.4 0.7 reshape.134
  335.1 1.4 multiply_reduce_fusion
  336.5 0.8 fusion.19
  (62 shorter events, 3.1 us)
Async XLA Ops:
  6.5 3.6 %copy-start = (bf16[256,128]{1,0:T(8,128)(2,1)S(1)}, bf16[256,128]{1,0:T(8,128)(2,1)}, u32[]{:S(2)}) copy-start(bf16[256,128]{1,0:T(8,128)(2,1)} %param.19) | copy-start | bytes 196612
  6.5 181.3 %all-gather.2.cloned.1.call-start = ((), (), s32[]{:S(2)}) async-start(), calls=%async_computation.1 | async-start | bytes 13369344 | tf_op jit(solution)/shard_map/all_gather | solution.py:308
  10.6 26.3 %copy-start.2 = (bf16[256,128]{1,0:T(8,128)(2,1)S(1)}, bf16[256,128]{1,0:T(8,128)(2,1)}, u32[]{:S(2)}) copy-start(bf16[256,128]{1,0:T(8,128)(2,1)} %param.20) | copy-start | bytes 196612
  10.6 26.4 %copy-start.3 = (f32[8,64,128]{2,1,0:T(8,128)S(1)}, f32[8,64,128]{2,1,0:T(8,128)}, u32[]{:S(2)}) copy-start(f32[8,64,128]{2,1,0:T(8,128)} %param.24) | copy-start | bytes 786436
  11.0 27.6 %copy-start.8 = (f32[8]{0:T(128)S(1)}, f32[8]{0:T(128)}, u32[]{:S(2)}) copy-start(f32[8]{0:T(128)} %param.23) | copy-start | bytes 100
  38.1 2.2 copy-start.1
  40.5 19.3 %copy-start.4 = (bf16[16,8192]{1,0:T(8,128)(2,1)S(1)}, bf16[16,8192]{1,0:T(8,128)(2,1)}, u32[]{:S(2)}) copy-start(bf16[16,8192]{1,0:T(8,128)(2,1)} %param.25) | copy-start | bytes 786436
  40.6 19.4 %copy-start.5 = (f32[8192]{0:T(1024)S(1)}, f32[8192]{0:T(1024)}, u32[]{:S(2)}) copy-start(f32[8192]{0:T(1024)} %param.26) | copy-start | bytes 98308
  59.7 1.1 copy-start.6
  91.5 209.9 %reduce-scatter.2.cloned.1.call-start = ((), (), s32[]{:S(2)}) async-start(), calls=%async_computation.2 | async-start | bytes 13369344 | tf_op jit(solution)/shard_map/reduce_scatter | solution.py:310
  202.2 0.7 copy-start.7
Sparse Core Ops, SparseCore 0:
  91.6 96.1 all-gather.1
  202.4 98.9 reduce-scatter.1

commit v14 on v12

--- a/solution.py
+++ b/solution.py
@@ -27,18 +27,21 @@
     pl.semaphore_wait(barrier, devices - 1)
     copies = []
     order = sorted(range(1, devices), key=lambda step: -min(step, devices - step))
+    half = x_ref.shape[2] // 2
     for step in order:
         peer = lax.rem(me + step, devices)
-        copy = pltpu.make_async_remote_copy(
-            src_ref=x_ref.at[peer],
-            dst_ref=o_ref.at[me],
-            send_sem=send_sem.at[step],
-            recv_sem=recv_sem.at[step],
-            device_id=(row, peer),
-            device_id_type=mesh_id,
-        )
-        copy.start()
-        copies.append(copy)
+        for part in range(2):
+            columns = pl.ds(part * half, half)
+            copy = pltpu.make_async_remote_copy(
+                src_ref=x_ref.at[peer, :, columns],
+                dst_ref=o_ref.at[me, :, columns],
+                send_sem=send_sem.at[part, step],
+                recv_sem=recv_sem.at[part, step],
+                device_id=(row, peer),
+                device_id_type=mesh_id,
+            )
+            copy.start()
+            copies.append(copy)
     local.wait()
     for copy in copies:
         copy.wait()
@@ -52,8 +55,8 @@
         in_specs=[pl.BlockSpec(memory_space=pltpu.VMEM)],
         out_specs=pl.BlockSpec(memory_space=pltpu.VMEM),
         scratch_shapes=[
-            pltpu.SemaphoreType.DMA((devices,)),
-            pltpu.SemaphoreType.DMA((devices,)),
+            pltpu.SemaphoreType.DMA((2, devices)),
+            pltpu.SemaphoreType.DMA((2, devices)),
             pltpu.SemaphoreType.DMA,
         ],
         compiler_params=pltpu.CompilerParams(collective_id=collective, has_side_effects=True),

time: 343 us -> 344 us (level)
  no operation moved by 1% of the time
where the time goes in v14:
time: 344 us
  waiting for transfers between devices  191 us (56%)
  Pallas kernels  110 us (32%)
  local copies, waits for them, and re-layouts  18.3 us (5%)
  between operations  13.7 us (4%)
  other arithmetic  7.08 us (2%)
    reduce_scatter x1, waiting for transfers between devices, on_device(): lax.psum_scatter(partial_value, 'seq', scatter_dimension=0, tiled=True)  98.7 us
    all_gather x1, waiting for transfers between devices, on_device(): segment = lax.all_gather(arrived, 'seq', axis=0, tiled=True)  92.7 us
    pallas_call x3, Pallas kernels, exchange(): pl.pallas_call(exchange_body, out_shape=jax.ShapeDtypeStruct(x.shape, x.d...  69.3 us
    pallas_call x1, Pallas kernels, exclusive_scan(): pl.pallas_call(functools.partial(scan_body, devices), out_shape=(jax.Shap...  26.4 us
    pallas_call x1, Pallas kernels, expert_mlp(): pl.pallas_call(functools.partial(expert_body, depth_steps), grid=(depth_s...  14.4 us
  transfers between devices with their start and end apart: 2, of which 2 were waited for; matrix products, arithmetic and copies ran while one was open for 0% of the time, Pallas kernels for 0%

profile of v14, /device:TPU:1, one launch (start us, length us, event | category | flops | bytes accessed | tf_op | source)
XLA Modules:
  0.0 343.7 jit_solution(13064770742453727072)
XLA Ops:
  6.5 0.7 neg.8
  7.2 0.8 multiply_bitcast_fusion
  8.5 1.3 reshape.145
  9.8 0.3 copy.28
  10.2 0.4 fusion.11
  10.6 0.4 while.17
  11.0 0.7 broadcast_in_dim.33.x_log
  11.7 26.4 %shard_map.145 = (f32[8,64,128]{2,1,0:T(8,128)}, f32[8,8,128]{2,1,0:T(8,128)}) custom-call(f32[8,64,128]{2,1,0:T(8,128)S(1)} %get-tuple-element.49.x_state, f32[8,8,128]{2,1,0:T(8,128)} %broadcast_in_dim.33.x_log), custom_call_target="tpu_custom_call" | custom-call | tf_op jit(solution)/shard_map/pallas_call | solution.py:201
  38.1 0.9 exponential_reduce_fusion
  39.3 1.0 multiply_add_fusion
  40.4 0.5 fusion.6
  40.8 1.3 fusion.5
  42.2 0.4 copy.32
  42.9 0.8 copy.34
  43.8 16.9 %shard_map.146 = bf16[16,16,512]{2,1,0:T(8,128)(2,1)} custom-call(bf16[16,16,512]{2,1,0:T(8,128)(2,1)} %bitcast.76), custom_call_target="tpu_custom_call" | custom-call | tf_op jit(solution)/shard_map/pallas_call | solution.py:52
  60.7 1.0 convert_bitcast_fusion
  62.2 0.4 broadcast_in_dim.34
  63.3 0.3 convolution_convert_fusion
  63.6 1.9 reshape.129.x_ref
  65.5 25.1 %shard_map.147 = bf16[16,16,1536]{2,1,0:T(8,128)(2,1)} custom-call(bf16[16,16,1536]{2,1,0:T(8,128)(2,1)} %reshape.129.x_ref), custom_call_target="tpu_custom_call" | custom-call | tf_op jit(solution)/shard_map/pallas_call | solution.py:52
  90.7 3.1 reshape.130
  94.0 92.7 %all-gather.2.cloned.1.call-done.seg_ref = bf16[768,8192]{1,0:T(8,128)(2,1)} async-done(((bf16[48,8192]{1,0:T(8,128)(2,1)}), bf16[768,8192]{1,0:T(8,128)(2,1)}) %all-gather.2.cloned.1.call-update) | async-done | bytes 12582928 | tf_op jit(solution)/shard_map/all_gather | solution.py:311
  186.8 14.4 %shard_map.148 = bf16[768,8192]{1,0:T(8,128)(2,1)} custom-call(bf16[768,8192]{1,0:T(8,128)(2,1)} %all-gather.2.cloned.1.call-done.seg_ref, bf16[8192,128]{1,0:T(8,128)(2,1)} %bitcast.73, bf16[8192,128]{1,0:T(8,128)(2,1)} %bitcast.74, bf16[128,8192]{1,0:T(8,128)(2,1)} %bitcast.75), custom_call_target="tpu_custom_call" | custom-call | flops 4831838208 | bytes 31457280 | tf_op jit(solution)/shard_map/pallas_call | solution.py:101
  201.4 0.5 copy-done.7
  201.9 98.7 %reduce-scatter.2.cloned.1.call-done = bf16[48,8192]{1,0:T(8,128)(2,1)} async-done(((bf16[768,8192]{1,0:T(8,128)(2,1)}), bf16[48,8192]{1,0:T(8,128)(2,1)}) %reduce-scatter.2.cloned.1.call-update) | async-done | bytes 786448 | tf_op jit(solution)/shard_map/reduce_scatter | solution.py:313
  300.6 3.0 reshape.131.x_ref
  303.7 27.2 %shard_map.149 = bf16[16,16,1536]{2,1,0:T(8,128)(2,1)} custom-call(bf16[16,16,1536]{2,1,0:T(8,128)(2,1)} %reshape.131.x_ref), custom_call_target="tpu_custom_call" | custom-call | tf_op jit(solution)/shard_map/pallas_call | solution.py:52
  330.9 2.2 reshape.132
  333.1 0.9 gather_fusion
  334.0 0.7 reshape.134
  334.6 1.4 multiply_reduce_fusion
  336.0 0.8 fusion.19
  (62 shorter events, 3.1 us)
Async XLA Ops:
  6.5 3.6 %copy-start = (bf16[256,128]{1,0:T(8,128)(2,1)S(1)}, bf16[256,128]{1,0:T(8,128)(2,1)}, u32[]{:S(2)}) copy-start(bf16[256,128]{1,0:T(8,128)(2,1)} %param.19) | copy-start | bytes 196612
  6.5 180.2 %all-gather.2.cloned.1.call-start = ((), (), s32[]{:S(2)}) async-start(), calls=%async_computation.1 | async-start | bytes 13369344 | tf_op jit(solution)/shard_map/all_gather | solution.py:311
  10.6 28.5 %copy-start.2 = (bf16[256,128]{1,0:T(8,128)(2,1)S(1)}, bf16[256,128]{1,0:T(8,128)(2,1)}, u32[]{:S(2)}) copy-start(bf16[256,128]{1,0:T(8,128)(2,1)} %param.20) | copy-start | bytes 196612
  10.6 28.7 %copy-start.3 = (f32[8,64,128]{2,1,0:T(8,128)S(1)}, f32[8,64,128]{2,1,0:T(8,128)}, u32[]{:S(2)}) copy-start(f32[8,64,128]{2,1,0:T(8,128)} %param.24) | copy-start | bytes 786436
  11.0 29.8 %copy-start.8 = (f32[8]{0:T(128)S(1)}, f32[8]{0:T(128)}, u32[]{:S(2)}) copy-start(f32[8]{0:T(128)} %param.23) | copy-start | bytes 100
  40.3 2.2 copy-start.1
  42.7 19.1 %copy-start.4 = (bf16[16,8192]{1,0:T(8,128)(2,1)S(1)}, bf16[16,8192]{1,0:T(8,128)(2,1)}, u32[]{:S(2)}) copy-start(bf16[16,8192]{1,0:T(8,128)(2,1)} %param.25) | copy-start | bytes 786436
  42.9 19.1 %copy-start.5 = (f32[8192]{0:T(1024)S(1)}, f32[8192]{0:T(1024)}, u32[]{:S(2)}) copy-start(f32[8192]{0:T(1024)} %param.26) | copy-start | bytes 98308
  61.7 1.1 copy-start.6
  93.8 206.8 %reduce-scatter.2.cloned.1.call-start = ((), (), s32[]{:S(2)}) async-start(), calls=%async_computation.2 | async-start | bytes 13369344 | tf_op jit(solution)/shard_map/reduce_scatter | solution.py:313
  201.2 0.7 copy-start.7
Sparse Core Ops, SparseCore 0:
  93.9 92.7 all-gather.1
  201.3 99.2 reduce-scatter.1

commit v15 on v12

--- a/solution.py
+++ b/solution.py
@@ -92,7 +92,7 @@
     rows, width = segment.shape
     hidden = gate_w.shape[1]
     block = 4096
-    columns = 2048
+    columns = 4096
     depth_steps = width // block
     column_steps = width // columns
     return pl.pallas_call(

time: 343 us -> 343 us (level)
  no operation moved by 1% of the time
where the time goes in v15:
time: 343 us
  waiting for transfers between devices  191 us (56%)
  Pallas kernels  109 us (32%)
  local copies, waits for them, and re-layouts  18.3 us (5%)
  between operations  13.7 us (4%)
  other arithmetic  7.08 us (2%)
    reduce_scatter x1, waiting for transfers between devices, on_device(): lax.psum_scatter(partial_value, 'seq', scatter_dimension=0, tiled=True)  98.4 us
    all_gather x1, waiting for transfers between devices, on_device(): segment = lax.all_gather(arrived, 'seq', axis=0, tiled=True)  92.7 us
    pallas_call x3, Pallas kernels, exchange(): pl.pallas_call(exchange_body, out_shape=jax.ShapeDtypeStruct(x.shape, x.d...  68.5 us
    pallas_call x1, Pallas kernels, exclusive_scan(): pl.pallas_call(functools.partial(scan_body, devices), out_shape=(jax.Shap...  26.4 us
    pallas_call x1, Pallas kernels, expert_mlp(): pl.pallas_call(functools.partial(expert_body, depth_steps), grid=(depth_s...  14.3 us
  transfers between devices with their start and end apart: 2, of which 2 were waited for; matrix products, arithmetic and copies ran while one was open for 0% of the time, Pallas kernels for 0%

profile of v15, /device:TPU:1, one launch (start us, length us, event | category | flops | bytes accessed | tf_op | source)
XLA Modules:
  0.0 342.5 jit_solution(15350310759939171815)
XLA Ops:
  6.5 0.7 neg.8
  7.2 0.8 multiply_bitcast_fusion
  8.5 1.3 reshape.145
  9.8 0.3 copy.28
  10.2 0.4 fusion.11
  10.6 0.4 while.17
  11.0 0.7 broadcast_in_dim.33.x_log
  11.7 26.4 %shard_map.145 = (f32[8,64,128]{2,1,0:T(8,128)}, f32[8,8,128]{2,1,0:T(8,128)}) custom-call(f32[8,64,128]{2,1,0:T(8,128)S(1)} %get-tuple-element.49.x_state, f32[8,8,128]{2,1,0:T(8,128)} %broadcast_in_dim.33.x_log), custom_call_target="tpu_custom_call" | custom-call | tf_op jit(solution)/shard_map/pallas_call | solution.py:198
  38.1 0.9 exponential_reduce_fusion
  39.3 1.0 multiply_add_fusion
  40.4 0.5 fusion.6
  40.8 1.3 fusion.5
  42.2 0.4 copy.32
  42.9 0.8 copy.34
  43.8 16.7 %shard_map.146 = bf16[16,16,512]{2,1,0:T(8,128)(2,1)} custom-call(bf16[16,16,512]{2,1,0:T(8,128)(2,1)} %bitcast.76), custom_call_target="tpu_custom_call" | custom-call | tf_op jit(solution)/shard_map/pallas_call | solution.py:49
  60.4 1.0 convert_bitcast_fusion
  61.9 0.4 broadcast_in_dim.34
  63.0 0.3 convolution_convert_fusion
  63.4 1.9 reshape.129.x_ref
  65.3 24.8 %shard_map.147 = bf16[16,16,1536]{2,1,0:T(8,128)(2,1)} custom-call(bf16[16,16,1536]{2,1,0:T(8,128)(2,1)} %reshape.129.x_ref), custom_call_target="tpu_custom_call" | custom-call | tf_op jit(solution)/shard_map/pallas_call | solution.py:49
  90.1 3.1 reshape.130
  93.4 92.7 %all-gather.2.cloned.1.call-done.seg_ref = bf16[768,8192]{1,0:T(8,128)(2,1)} async-done(((bf16[48,8192]{1,0:T(8,128)(2,1)}), bf16[768,8192]{1,0:T(8,128)(2,1)}) %all-gather.2.cloned.1.call-update) | async-done | bytes 12582928 | tf_op jit(solution)/shard_map/all_gather | solution.py:308
  186.2 14.3 %shard_map.148 = bf16[768,8192]{1,0:T(8,128)(2,1)} custom-call(bf16[768,8192]{1,0:T(8,128)(2,1)} %all-gather.2.cloned.1.call-done.seg_ref, bf16[8192,128]{1,0:T(8,128)(2,1)} %bitcast.73, bf16[8192,128]{1,0:T(8,128)(2,1)} %bitcast.74, bf16[128,8192]{1,0:T(8,128)(2,1)} %bitcast.75), custom_call_target="tpu_custom_call" | custom-call | flops 4831838208 | bytes 31457280 | tf_op jit(solution)/shard_map/pallas_call | solution.py:98
  200.7 0.5 copy-done.7
  201.3 98.4 %reduce-scatter.2.cloned.1.call-done = bf16[48,8192]{1,0:T(8,128)(2,1)} async-done(((bf16[768,8192]{1,0:T(8,128)(2,1)}), bf16[48,8192]{1,0:T(8,128)(2,1)}) %reduce-scatter.2.cloned.1.call-update) | async-done | bytes 786448 | tf_op jit(solution)/shard_map/reduce_scatter | solution.py:310
  299.7 3.0 reshape.131.x_ref
  302.7 27.0 %shard_map.149 = bf16[16,16,1536]{2,1,0:T(8,128)(2,1)} custom-call(bf16[16,16,1536]{2,1,0:T(8,128)(2,1)} %reshape.131.x_ref), custom_call_target="tpu_custom_call" | custom-call | tf_op jit(solution)/shard_map/pallas_call | solution.py:49
  329.8 2.2 reshape.132
  331.9 0.9 gather_fusion
  332.8 0.7 reshape.134
  333.5 1.4 multiply_reduce_fusion
  334.9 0.8 fusion.19
  (62 shorter events, 3.1 us)
Async XLA Ops:
  6.5 3.6 %copy-start = (bf16[256,128]{1,0:T(8,128)(2,1)S(1)}, bf16[256,128]{1,0:T(8,128)(2,1)}, u32[]{:S(2)}) copy-start(bf16[256,128]{1,0:T(8,128)(2,1)} %param.19) | copy-start | bytes 196612
  6.5 179.6 %all-gather.2.cloned.1.call-start = ((), (), s32[]{:S(2)}) async-start(), calls=%async_computation.1 | async-start | bytes 13369344 | tf_op jit(solution)/shard_map/all_gather | solution.py:308
  10.6 28.5 %copy-start.2 = (bf16[256,128]{1,0:T(8,128)(2,1)S(1)}, bf16[256,128]{1,0:T(8,128)(2,1)}, u32[]{:S(2)}) copy-start(bf16[256,128]{1,0:T(8,128)(2,1)} %param.20) | copy-start | bytes 196612
  10.6 28.7 %copy-start.3 = (f32[8,64,128]{2,1,0:T(8,128)S(1)}, f32[8,64,128]{2,1,0:T(8,128)}, u32[]{:S(2)}) copy-start(f32[8,64,128]{2,1,0:T(8,128)} %param.24) | copy-start | bytes 786436
  11.0 29.8 %copy-start.8 = (f32[8]{0:T(128)S(1)}, f32[8]{0:T(128)}, u32[]{:S(2)}) copy-start(f32[8]{0:T(128)} %param.23) | copy-start | bytes 100
  40.3 2.2 copy-start.1
  42.7 18.8 %copy-start.4 = (bf16[16,8192]{1,0:T(8,128)(2,1)S(1)}, bf16[16,8192]{1,0:T(8,128)(2,1)}, u32[]{:S(2)}) copy-start(bf16[16,8192]{1,0:T(8,128)(2,1)} %param.25) | copy-start | bytes 786436
  42.9 18.8 %copy-start.5 = (f32[8192]{0:T(1024)S(1)}, f32[8192]{0:T(1024)}, u32[]{:S(2)}) copy-start(f32[8192]{0:T(1024)} %param.26) | copy-start | bytes 98308
  61.4 1.1 copy-start.6
  93.2 206.5 %reduce-scatter.2.cloned.1.call-start = ((), (), s32[]{:S(2)}) async-start(), calls=%async_computation.2 | async-start | bytes 13369344 | tf_op jit(solution)/shard_map/reduce_scatter | solution.py:310
  200.5 0.7 copy-start.7
Sparse Core Ops, SparseCore 0:
  93.3 92.8 all-gather.1
  200.6 99.0 reduce-scatter.1

commit v16 on v13

--- a/solution.py
+++ b/solution.py
@@ -92,7 +92,7 @@
     rows, width = segment.shape
     hidden = gate_w.shape[1]
     block = 4096
-    columns = 2048
+    columns = 4096
     depth_steps = width // block
     column_steps = width // columns
     return pl.pallas_call(

time: 345 us -> 345 us (level)
  no operation moved by 1% of the time
where the time goes in v16:
time: 345 us; the launch traced here: 344 us
  waiting for transfers between devices  195 us (57%)
  Pallas kernels  107 us (31%)
  local copies, waits for them, and re-layouts  18.3 us (5%)
  between operations  13.7 us (4%)
  other arithmetic  7.08 us (2%)
    reduce_scatter x1, waiting for transfers between devices, on_device(): lax.psum_scatter(partial_value, 'seq', scatter_dimension=0, tiled=True)  98.4 us
    all_gather x1, waiting for transfers between devices, on_device(): segment = lax.all_gather(arrived, 'seq', axis=0, tiled=True)  96.1 us
    pallas_call x3, Pallas kernels, exchange(): pl.pallas_call(exchange_body, out_shape=jax.ShapeDtypeStruct(x.shape, x.d...  69 us
    pallas_call x1, Pallas kernels, exclusive_scan(): pl.pallas_call(functools.partial(scan_body, devices), out_shape=(jax.Shap...  24.2 us
    pallas_call x1, Pallas kernels, expert_mlp(): pl.pallas_call(functools.partial(expert_body, depth_steps), grid=(depth_s...  14.3 us
  transfers between devices with their start and end apart: 2, of which 2 were waited for; matrix products, arithmetic and copies ran while one was open for 0% of the time, Pallas kernels for 0%

profile of v16, /device:TPU:1, one launch (start us, length us, event | category | flops | bytes accessed | tf_op | source)
XLA Modules:
  0.0 344.1 jit_solution(559252162177180493)
XLA Ops:
  6.5 0.7 neg.8
  7.2 0.8 multiply_bitcast_fusion
  8.5 1.3 reshape.145
  9.8 0.3 copy.28
  10.2 0.4 fusion.11
  10.6 0.4 while.17
  11.0 0.7 broadcast_in_dim.33.x_log
  11.7 24.2 %shard_map.145 = (f32[8,64,128]{2,1,0:T(8,128)}, f32[8,8,128]{2,1,0:T(8,128)}) custom-call(f32[8,64,128]{2,1,0:T(8,128)S(1)} %get-tuple-element.49.x_state, f32[8,8,128]{2,1,0:T(8,128)} %broadcast_in_dim.33.x_log), custom_call_target="tpu_custom_call" | custom-call | tf_op jit(solution)/shard_map/pallas_call | solution.py:198
  35.9 0.9 exponential_reduce_fusion
  37.0 1.0 multiply_add_fusion
  38.1 0.5 fusion.6
  38.6 1.3 fusion.5
  39.9 0.4 copy.32
  40.7 0.8 copy.34
  41.5 17.2 %shard_map.146 = bf16[16,16,512]{2,1,0:T(8,128)(2,1)} custom-call(bf16[16,16,512]{2,1,0:T(8,128)(2,1)} %bitcast.76), custom_call_target="tpu_custom_call" | custom-call | tf_op jit(solution)/shard_map/pallas_call | solution.py:49
  58.7 1.0 convert_bitcast_fusion
  60.2 0.4 broadcast_in_dim.34
  61.3 0.3 convolution_convert_fusion
  61.6 1.9 reshape.129.x_ref
  63.5 24.8 %shard_map.147 = bf16[16,16,1536]{2,1,0:T(8,128)(2,1)} custom-call(bf16[16,16,1536]{2,1,0:T(8,128)(2,1)} %reshape.129.x_ref), custom_call_target="tpu_custom_call" | custom-call | tf_op jit(solution)/shard_map/pallas_call | solution.py:49
  88.3 3.1 reshape.130
  91.7 96.1 %all-gather.2.cloned.1.call-done.seg_ref = bf16[768,8192]{1,0:T(8,128)(2,1)} async-done(((bf16[48,8192]{1,0:T(8,128)(2,1)}), bf16[768,8192]{1,0:T(8,128)(2,1)}) %all-gather.2.cloned.1.call-update) | async-done | bytes 12582928 | tf_op jit(solution)/shard_map/all_gather | solution.py:308
  187.8 14.3 %shard_map.148 = bf16[768,8192]{1,0:T(8,128)(2,1)} custom-call(bf16[768,8192]{1,0:T(8,128)(2,1)} %all-gather.2.cloned.1.call-done.seg_ref, bf16[8192,128]{1,0:T(8,128)(2,1)} %bitcast.73, bf16[8192,128]{1,0:T(8,128)(2,1)} %bitcast.74, bf16[128,8192]{1,0:T(8,128)(2,1)} %bitcast.75), custom_call_target="tpu_custom_call" | custom-call | flops 4831838208 | bytes 31457280 | tf_op jit(solution)/shard_map/pallas_call | solution.py:98
  202.3 0.5 copy-done.7
  202.9 98.4 %reduce-scatter.2.cloned.1.call-done = bf16[48,8192]{1,0:T(8,128)(2,1)} async-done(((bf16[768,8192]{1,0:T(8,128)(2,1)}), bf16[48,8192]{1,0:T(8,128)(2,1)}) %reduce-scatter.2.cloned.1.call-update) | async-done | bytes 786448 | tf_op jit(solution)/shard_map/reduce_scatter | solution.py:310
  301.3 3.0 reshape.131.x_ref
  304.3 27.0 %shard_map.149 = bf16[16,16,1536]{2,1,0:T(8,128)(2,1)} custom-call(bf16[16,16,1536]{2,1,0:T(8,128)(2,1)} %reshape.131.x_ref), custom_call_target="tpu_custom_call" | custom-call | tf_op jit(solution)/shard_map/pallas_call | solution.py:49
  331.3 2.2 reshape.132
  333.5 0.9 gather_fusion
  334.4 0.7 reshape.134
  335.0 1.4 multiply_reduce_fusion
  336.5 0.8 fusion.19
  (62 shorter events, 3.1 us)
Async XLA Ops:
  6.5 3.6 %copy-start = (bf16[256,128]{1,0:T(8,128)(2,1)S(1)}, bf16[256,128]{1,0:T(8,128)(2,1)}, u32[]{:S(2)}) copy-start(bf16[256,128]{1,0:T(8,128)(2,1)} %param.19) | copy-start | bytes 196612
  6.5 181.3 %all-gather.2.cloned.1.call-start = ((), (), s32[]{:S(2)}) async-start(), calls=%async_computation.1 | async-start | bytes 13369344 | tf_op jit(solution)/shard_map/all_gather | solution.py:308
  10.6 26.3 %copy-start.2 = (bf16[256,128]{1,0:T(8,128)(2,1)S(1)}, bf16[256,128]{1,0:T(8,128)(2,1)}, u32[]{:S(2)}) copy-start(bf16[256,128]{1,0:T(8,128)(2,1)} %param.20) | copy-start | bytes 196612
  10.6 26.4 %copy-start.3 = (f32[8,64,128]{2,1,0:T(8,128)S(1)}, f32[8,64,128]{2,1,0:T(8,128)}, u32[]{:S(2)}) copy-start(f32[8,64,128]{2,1,0:T(8,128)} %param.24) | copy-start | bytes 786436
  11.0 27.6 %copy-start.8 = (f32[8]{0:T(128)S(1)}, f32[8]{0:T(128)}, u32[]{:S(2)}) copy-start(f32[8]{0:T(128)} %param.23) | copy-start | bytes 100
  38.1 2.2 copy-start.1
  40.5 19.3 %copy-start.4 = (bf16[16,8192]{1,0:T(8,128)(2,1)S(1)}, bf16[16,8192]{1,0:T(8,128)(2,1)}, u32[]{:S(2)}) copy-start(bf16[16,8192]{1,0:T(8,128)(2,1)} %param.25) | copy-start | bytes 786436
  40.6 19.4 %copy-start.5 = (f32[8192]{0:T(1024)S(1)}, f32[8192]{0:T(1024)}, u32[]{:S(2)}) copy-start(f32[8192]{0:T(1024)} %param.26) | copy-start | bytes 98308
  59.7 1.1 copy-start.6
  91.5 209.8 %reduce-scatter.2.cloned.1.call-start = ((), (), s32[]{:S(2)}) async-start(), calls=%async_computation.2 | async-start | bytes 13369344 | tf_op jit(solution)/shard_map/reduce_scatter | solution.py:310
  202.1 0.7 copy-start.7
Sparse Core Ops, SparseCore 0:
  91.6 96.1 all-gather.1
  202.3 99.0 reduce-scatter.1
